TPU v7x, 32 devices: a whole 2x2x4 slice. The times are simulated.
32 devices in a mesh: seg: 4 (over y, x), grid: 8 (over z, core).
Axes of the slice: x: 2, y: 2, z: 4, core: 2. Of those that a mesh axis runs over, the one named last changes fastest.
Arguments:
- tangent: float32 [4, 3, 96, 256, 256], P('seg', None, 'grid'), may hold values from -6 to 6
- base_flow: bfloat16 [4, 3, 96, 256, 256], P('seg', None, 'grid'), may hold values from -4 to 4
- base_shear: bfloat16 [4, 3, 96, 256, 256], P('seg', None, 'grid'), may hold values from -4 to 4
- wall_derivative: float32 [96, 96], replicated, may hold values from -0.625 to 0.625
- implicit_inverse: float32 [3, 96, 96], replicated, may hold values from -1 to 1
- successor: int32 [4], replicated, may hold values from 0 to 3, as said below
- spanwise_shift: int32 [4], P('seg'), may hold values from 0 to 255
Outputs:
- jvp: float32 [4, 3, 96, 256, 256], P('seg', None, 'grid')
Inputs may be any that keep to these rules, and one draw needn't show every extreme that they name: successor[s] = (s + k) mod 4 for one odd k shared by all segments, so the segments form one closed loop.
All inputs are finite; a program needn't handle non-finite values.
Results may differ from a plain program's by a relative error of at most 0.0003.
Values may be sent and summed in bfloat16 or wider, within the bound.
No kernel may reach another device: no remote copies, remote signals or barrier semaphores. Data moves between devices by JAX's collectives and lax.ppermute only.
A program may use at most 192 MiB of HBM per device.

v0:
```python
import math

import jax
import jax.numpy as jnp
from jax import lax
from jax.sharding import PartitionSpec as P

STEPS = 1


TIME_STEP = 0.05
GAMMAS = (8.0 / 15.0, 5.0 / 12.0, 3.0 / 4.0)
ZETAS = (0.0, -17.0 / 60.0, -5.0 / 12.0)
HIGHEST = lax.Precision.HIGHEST


def shifted(block, axis, distance):
    devices = range(lax.axis_size(axis))
    route = [((i - distance) % len(devices), i) for i in devices]
    return lax.ppermute(block, axis, route)


def spectral_table(points):
    row_index = jnp.arange(points, dtype=jnp.int32)[:, None]
    column_index = jnp.arange(points, dtype=jnp.int32)[None, :]
    offset = row_index - column_index
    parity = (1 - 2 * (offset % 2)).astype(jnp.float32)
    phase_angle = math.pi / points * offset.astype(jnp.float32)
    cotangent_base = jnp.where(offset == 0, jnp.float32(1.0), jnp.tan(phase_angle))
    return jnp.where(offset == 0, jnp.float32(0.0), 0.5 * parity / cotangent_base)


def derive_streamwise(matrix, velocity):
    return jnp.einsum("jk,cykz->cyjz", matrix, velocity, precision=HIGHEST)


def derive_spanwise(matrix, velocity):
    return jnp.einsum("cyxk,jk->cyxj", velocity, matrix, precision=HIGHEST)


def apply_wall(matrix, velocity):
    return jnp.einsum("jk,ckxz->cjxz", matrix, velocity, precision=HIGHEST)


def to_lines(velocity):
    return lax.all_to_all(velocity, "grid", split_axis=2, concat_axis=1, tiled=True)


def shards(
    tangent, base_flow, base_shear, wall_derivative, implicit_inverse, successor, spanwise_shift
):
    initial = tangent[0]
    segments = lax.axis_size("seg")
    position = lax.axis_index("seg")
    labels = jnp.arange(successor.shape[0], dtype=jnp.int32)
    ahead_label = jnp.sum(jnp.where(labels == position, successor, 0))
    offset = (ahead_label - position) % segments
    following = initial
    for bit_number in range((segments - 1).bit_length()):
        moved = shifted(following, "seg", -(1 << bit_number))
        following = jnp.where(offset // (1 << bit_number) % 2 == 1, moved, following)
    baseline = base_flow[0].astype(jnp.float32)
    stream_table = spectral_table(initial.shape[2])
    span_table = spectral_table(initial.shape[3])
    base_dx = derive_streamwise(stream_table, baseline)
    base_dz = derive_spanwise(span_table, baseline)
    total_sections = 3 * STEPS
    base_dy = base_shear[0].astype(jnp.float32)

    def slab_back(velocity):
        return lax.all_to_all(velocity, "grid", split_axis=1, concat_axis=2, tiled=True)

    velocity = initial
    velocity_lines = to_lines(velocity)
    velocity_dy = slab_back(apply_wall(wall_derivative, velocity_lines))
    previous = jnp.zeros_like(velocity)
    for number in range(total_sections):
        section = number % 3
        velocity_dx = derive_streamwise(stream_table, velocity)
        velocity_dz = derive_spanwise(span_table, velocity)
        carried = (
            baseline[0:1] * velocity_dx + baseline[1:2] * velocity_dy + baseline[2:3] * velocity_dz
        )
        sheared = velocity[0:1] * base_dx + velocity[1:2] * base_dy + velocity[2:3] * base_dz
        term = -(carried + sheared)
        right_side = velocity + TIME_STEP * (GAMMAS[section] * term + ZETAS[section] * previous)
        solved = apply_wall(implicit_inverse[section], to_lines(right_side))
        previous = term
        if number == total_sections - 1:
            velocity = slab_back(solved)
        else:
            velocity, velocity_dy = (
                lax.all_to_all(solved, "grid", split_axis=1, concat_axis=2, tiled=True),
                lax.all_to_all(
                    apply_wall(wall_derivative, solved),
                    "grid",
                    split_axis=1,
                    concat_axis=2,
                    tiled=True,
                ),
            )
    rolled = jnp.roll(velocity, spanwise_shift[0], axis=3)
    return (rolled - following)[None]


def solution(mesh):
    placed = (
        P("seg", None, "grid", None, None),
        P("seg", None, "grid", None, None),
        P("seg", None, "grid", None, None),
        P(),
        P(),
        P(),
        P("seg"),
    )
    return jax.shard_map(
        shards,
        mesh=mesh,
        in_specs=placed,
        out_specs=P("seg", None, "grid", None, None),
        check_vma=False,
    )
```

profile of v0, /device:TPU:9, one launch (start us, length us, event | category | flops | bytes accessed | tf_op | source)
XLA Modules:
  0.0 2831.0 jit_solution(1378554369701570919)
XLA Ops:
  0.0 13.9 copy.120
  13.9 277.1 %all_to_all.180 = f32[3,12,256,256]{3,1,0,2:T(8,128)S(1)} all-to-all(f32[3,12,256,256]{3,1,0,2:T(8,128)} %copy.120), channel_id=1, replica_groups=mesh['seg'=4,'grid'=8] {'grid'}, dimensions={2} | all-to-all | bytes 18874368 | tf_op jit(solution)/shard_map/all_to_all | solution.py:46
  290.9 11.8 copy.122
  302.8 18.6 fusion.37
  321.4 9.0 copy.124
  330.4 8.2 all-to-all-start.1
  338.6 2.2 collective-permute-start
  342.1 7.7 slice_bitcast_fusion.5
  349.8 3.7 bitcast_convert_fusion
  353.4 3.6 slice_bitcast_fusion.2
  357.1 9.0 fusion.35
  366.1 8.6 fusion.33
  374.7 13.4 fusion.70
  388.1 153.3 %all-to-all-done.1 = f32[3,96,32,256]{3,2,0,1:T(8,128)} async-done(((f32[3,96,32,256]{3,2,0,1:T(8,128)}), f32[3,96,32,256]{3,2,0,1:T(8,128)}, u32[]{:S(2)}, u32[]{:S(2)}) %all-to-all-start.1) | async-done | bytes 9437216 | tf_op jit(solution)/shard_map/all_to_all | solution.py:71
  541.4 9.4 copy.126
  550.8 42.2 %broadcast_select_fusion = (f32[3,12,256,256]{3,2,1,0:T(8,128)}, f32[3,12,256,256]{3,2,1,0:T(8,128)}, f32[3,12,256,256]{3,2,1,0:T(8,128)}) fusion(f32[3,12,256,256]{3,2,1,0:T(8,128)} %collective-permute-done, pred[]{:T(512)S(6)} %eq.46, f32[1,3,12,256,256]{4,3,2,1,0:T(8,128)} %param.7, f32[256,3,12,256]{0,3,2,1:T(8,128)} %fusion.33, ...), kind=kOutput, calls=%fused_computation.58 | convolution fusion | flops 7286947840 | bytes 108527616 | tf_op jit(solution)/shard_map/cyxk,jk->cyxj/dot_general | solution.py:38
  593.0 13.9 copy.129
  606.9 281.6 %all_to_all.181 = f32[3,12,256,256]{3,1,0,2:T(8,128)} all-to-all(f32[3,12,256,256]{3,1,0,2:T(8,128)} %copy.129), channel_id=1, replica_groups=mesh['seg'=4,'grid'=8] {'grid'}, dimensions={2} | all-to-all | bytes 18874368 | tf_op jit(solution)/shard_map/all_to_all | solution.py:46
  888.5 12.7 copy.131
  901.3 15.3 fusion.40
  916.6 3.6 copy-done.3
  920.2 10.1 convolution_bitcast_fusion.1
  930.3 9.2 copy.138
  939.5 8.0 all-to-all-start.4
  947.5 12.8 copy.133
  960.3 190.0 %all-to-all-done.4 = f32[3,96,32,256]{3,2,0,1:T(8,128)} async-done(((f32[3,96,32,256]{3,2,0,1:T(8,128)}), f32[3,96,32,256]{3,2,0,1:T(8,128)}, u32[]{:S(2)}, u32[]{:S(2)}) %all-to-all-start.4) | async-done | bytes 9437216 | tf_op jit(solution)/shard_map/all_to_all | solution.py:94
  1150.3 8.9 all-to-all-start.3
  1159.2 9.1 copy.140
  1168.4 193.6 %all-to-all-done.3 = f32[3,96,32,256]{3,2,0,1:T(8,128)} async-done(((f32[3,96,32,256]{3,2,0,1:T(8,128)}), f32[3,96,32,256]{3,2,0,1:T(8,128)}, u32[]{:S(2)}, u32[]{:S(2)}) %all-to-all-start.3) | async-done | bytes 9437216 | tf_op jit(solution)/shard_map/all_to_all | solution.py:93
  1361.9 4.9 copy.135
  1366.8 12.0 fusion.64
  1378.9 9.3 copy.134
  1388.1 4.9 fusion.197
  1393.1 2.1 copy.141
  1399.2 37.7 %multiply_add_fusion = (f32[3,12,256,256]{3,2,1,0:T(8,128)}, f32[3,12,256,256]{3,2,1,0:T(8,128)}) fusion(f32[3,12,256,256]{3,2,1,0:T(8,128)} %get-tuple-element.19, f32[3,12,8,32,256]{4,3,2,1,0:T(8,128)} %copy-done.2, f32[256,3,12,256]{0,3,2,1:T(8,128)} %fusion.33, f32[12,256,256]{2,1,0:T(8,128)} %bitcast.218, bf16[1,3,12,256,256]{4,3,2,1,0:T(8,128)(2,1)} %param.9, ...), kind=kOutput, calls=%fused_computation.51 | convolution fusion | flops 7291666432 | bytes 108527616 | tf_op jit(solution)/shard_map/jk,cykz->cyjz/dot_general | solution.py:34
  1436.9 13.8 copy.144
  1450.7 281.6 %all_to_all.182 = f32[3,12,256,256]{3,1,0,2:T(8,128)} all-to-all(f32[3,12,256,256]{3,1,0,2:T(8,128)} %copy.144), channel_id=1, replica_groups=mesh['seg'=4,'grid'=8] {'grid'}, dimensions={2} | all-to-all | bytes 18874368 | tf_op jit(solution)/shard_map/all_to_all | solution.py:46
  1732.3 12.7 copy.146
  1745.0 15.3 fusion.43
  1760.3 3.6 copy-done.4
  1763.9 10.1 convolution_bitcast_fusion
  1774.0 9.3 copy.153
  1783.3 8.0 all-to-all-start.7
  1791.3 12.7 copy.148
  1804.0 190.1 %all-to-all-done.7 = f32[3,96,32,256]{3,2,0,1:T(8,128)} async-done(((f32[3,96,32,256]{3,2,0,1:T(8,128)}), f32[3,96,32,256]{3,2,0,1:T(8,128)}, u32[]{:S(2)}, u32[]{:S(2)}) %all-to-all-start.7) | async-done | bytes 9437216 | tf_op jit(solution)/shard_map/all_to_all | solution.py:94
  1994.1 8.9 all-to-all-start.6
  2003.0 9.2 copy.155
  2012.2 193.6 %all-to-all-done.6 = f32[3,96,32,256]{3,2,0,1:T(8,128)} async-done(((f32[3,96,32,256]{3,2,0,1:T(8,128)}), f32[3,96,32,256]{3,2,0,1:T(8,128)}, u32[]{:S(2)}, u32[]{:S(2)}) %all-to-all-start.6) | async-done | bytes 9437216 | tf_op jit(solution)/shard_map/all_to_all | solution.py:93
  2205.8 4.9 copy.150
  2210.6 12.1 fusion.61
  2222.7 9.3 copy.149
  2232.0 4.9 fusion.196
  2237.0 2.1 copy.156
  2239.1 2.0 copy.157
  2243.1 35.5 %fusion.15 = f32[3,12,256,256]{3,2,1,0:T(8,128)} fusion(f32[3,12,256,256]{3,2,1,0:T(8,128)} %bitcast.215, f32[3,12,8,32,256]{4,3,2,1,0:T(8,128)} %copy.155, f32[256,3,12,256]{0,3,2,1:T(8,128)} %fusion.33, f32[256,3,12,256]{3,0,2,1:T(8,128)} %fusion.35, f32[3,12,256,256]{3,2,1,0:T(8,128)} %get-tuple-element.21, f32[3,12,256,256]{3,2,1,0:T(8,128)} %fusion.61, ...), kind=kOutput, calls=%fused_computation.20 | convolution fusion | flops 7291666432 | bytes 89653248 | tf_op jit(solution)/shard_map/jk,cykz->cyjz/dot_general | solution.py:34
  2278.6 9.3 copy.159
  2288.0 278.4 %all_to_all.183 = f32[3,12,256,256]{3,1,0,2:T(8,128)} all-to-all(f32[3,12,256,256]{3,1,0,2:T(8,128)S(1)} %copy.159), channel_id=1, replica_groups=mesh['seg'=4,'grid'=8] {'grid'}, dimensions={2} | all-to-all | bytes 18874368 | tf_op jit(solution)/shard_map/all_to_all | solution.py:46
  2566.4 12.7 copy.161
  2579.1 15.3 fusion.46
  2594.4 9.5 copy.163
  2603.8 8.1 all-to-all-start.9
  2613.9 200.8 %all-to-all-done.9 = f32[3,96,32,256]{3,2,0,1:T(8,128)} async-done(((f32[3,96,32,256]{3,2,0,1:T(8,128)}), f32[3,96,32,256]{3,2,0,1:T(8,128)}, u32[]{:S(2)}, u32[]{:S(2)}) %all-to-all-start.9) | async-done | bytes 9437216 | tf_op jit(solution)/shard_map/all_to_all | solution.py:71
  2814.7 4.9 copy.165
  2819.6 10.9 fusion.18
  (33 shorter events, 7.9 us)
Async XLA Ops:
  0.0 302.8 %copy-start = (f32[96,96]{1,0:T(8,128)S(1)}, f32[96,96]{1,0:T(8,128)}, u32[]{:S(2)}) copy-start(f32[96,96]{1,0:T(8,128)} %param.10) | copy-start | bytes 110596
  330.4 10.4 copy-start.7
  330.4 211.0 %all-to-all-start.1 = ((f32[3,96,32,256]{3,2,0,1:T(8,128)}), f32[3,96,32,256]{3,2,0,1:T(8,128)}, u32[]{:S(2)}, u32[]{:S(2)}) async-start(f32[3,96,32,256]{3,2,0,1:T(8,128)} %copy.124), calls=%async_computation.1 | async-start | bytes 18874368 | tf_op jit(solution)/shard_map/all_to_all | solution.py:71
  338.6 212.2 %collective-permute-start = (f32[3,12,256,256]{3,2,1,0:T(8,128)}, f32[3,12,256,256]{3,2,1,0:T(8,128)}, u32[]{:S(2)}, u32[]{:S(2)}) collective-permute-start(f32[3,12,256,256]{3,2,1,0:T(8,128)} %bitcast.211), channel_id=1, source_target_pairs={{8,0},{16,8},{24,16},{0,24},{9,1},{17,9},{25,17},{1,25},{10,2},{18... | collective-permute-start | bytes 28311560 | tf_op jit(solution)/shard_map/ppermute | solution.py:20
  349.8 7.3 slice-start.3
  353.4 3.6 slice-start.4
  357.0 17.6 slice-start
  357.0 17.6 slice-start.1
  366.1 8.6 slice-start.2
  541.4 9.4 copy-start.1
  888.5 12.7 copy-start.6
  916.6 3.6 copy-start.3
  939.5 210.8 %all-to-all-start.4 = ((f32[3,96,32,256]{3,2,0,1:T(8,128)}), f32[3,96,32,256]{3,2,0,1:T(8,128)}, u32[]{:S(2)}, u32[]{:S(2)}) async-start(f32[3,96,32,256]{3,2,0,1:T(8,128)} %copy.138), calls=%async_computation.4 | async-start | bytes 18874368 | tf_op jit(solution)/shard_map/all_to_all | solution.py:94
  1150.3 211.6 %all-to-all-start.3 = ((f32[3,96,32,256]{3,2,0,1:T(8,128)}), f32[3,96,32,256]{3,2,0,1:T(8,128)}, u32[]{:S(2)}, u32[]{:S(2)}) async-start(f32[3,96,32,256]{3,2,0,1:T(8,128)} %copy.133), calls=%async_computation.3 | async-start | bytes 18874368 | tf_op jit(solution)/shard_map/all_to_all | solution.py:93
  1366.8 12.0 copy-start.2
  1760.3 3.6 copy-start.4
  1783.3 210.8 %all-to-all-start.7 = ((f32[3,96,32,256]{3,2,0,1:T(8,128)}), f32[3,96,32,256]{3,2,0,1:T(8,128)}, u32[]{:S(2)}, u32[]{:S(2)}) async-start(f32[3,96,32,256]{3,2,0,1:T(8,128)} %copy.153), calls=%async_computation.7 | async-start | bytes 18874368 | tf_op jit(solution)/shard_map/all_to_all | solution.py:94
  1994.1 211.7 %all-to-all-start.6 = ((f32[3,96,32,256]{3,2,0,1:T(8,128)}), f32[3,96,32,256]{3,2,0,1:T(8,128)}, u32[]{:S(2)}, u32[]{:S(2)}) async-start(f32[3,96,32,256]{3,2,0,1:T(8,128)} %copy.148), calls=%async_computation.6 | async-start | bytes 18874368 | tf_op jit(solution)/shard_map/all_to_all | solution.py:93
  2210.6 12.1 copy-start.5
  2603.8 210.9 %all-to-all-start.9 = ((f32[3,96,32,256]{3,2,0,1:T(8,128)}), f32[3,96,32,256]{3,2,0,1:T(8,128)}, u32[]{:S(2)}, u32[]{:S(2)}) async-start(f32[3,96,32,256]{3,2,0,1:T(8,128)} %copy.163), calls=%async_computation.9 | async-start | bytes 18874368 | tf_op jit(solution)/shard_map/all_to_all | solution.py:71
  2611.9 207.7 %collective-permute-start.1 = (f32[3,12,256,256]{3,2,1,0:T(8,128)}, f32[3,12,256,256]{3,2,1,0:T(8,128)}, u32[]{:S(2)}, u32[]{:S(2)}) collective-permute-start(f32[3,12,256,256]{3,2,1,0:T(8,128)} %get-tuple-element.5), channel_id=1, source_target_pairs={{16,0},{24,8},{0,16},{8,24},{17,1},{25,9},{1,17},{9,25},{18,2},{26... | collective-permute-start | bytes 28311560 | tf_op jit(solution)/shard_map/ppermute | solution.py:20
where the time goes:
time: 2840 us; the launch traced here: 2830 us
  blocking collectives  1120 us (39%)
  waiting for transfers between devices  1120 us (39%)
  local copies, waits for them, and re-layouts  265 us (9%)
  matrix products  255 us (9%)
  starting transfers between devices  53.6 us (2%)
    all_to_all x4, blocking collectives, to_lines(): lax.all_to_all(velocity, 'grid', split_axis=2, concat_axis=1, tiled=True)  1120 us
    all_to_all x2, waiting for transfers between devices, shards(): lax.all_to_all(solved, 'grid', split_axis=1, concat_axis=2, tiled=True)  387 us
    all_to_all x2, waiting for transfers between devices, shards(): lax.all_to_all(apply_wall(wall_derivative, solved), 'grid', split_axis=1,...  380 us
    all_to_all x2, waiting for transfers between devices, slab_back(): lax.all_to_all(velocity, 'grid', split_axis=1, concat_axis=2, tiled=True)  354 us
    dot_general x4, matrix products, derive_streamwise(): return jnp.einsum('jk,cykz->cyjz', matrix, velocity, precision=HIGHEST)  95.7 us
    dot_general x6, matrix products, apply_wall(): return jnp.einsum('jk,ckxz->cjxz', matrix, velocity, precision=HIGHEST)  84.7 us
    dot_general x4, matrix products, derive_spanwise(): return jnp.einsum('cyxk,jk->cyxj', velocity, matrix, precision=HIGHEST)  74.9 us
    transpose x6, local copies, waits for them, and re-layouts, apply_wall(): return jnp.einsum('jk,ckxz->cjxz', matrix, velocity, precision=HIGHEST)  62.3 us
  transfers between devices with their start and end apart: 8, of which 6 were waited for; matrix products, arithmetic and copies ran while one was open for 4% of the time, Pallas kernels for 0%

commit v1 on v0

v1 whole, which is shorter than its diff:
```python
import functools

import numpy as np
import jax
import jax.numpy as jnp
from jax import lax
from jax.experimental import pallas as pl
from jax.experimental.pallas import tpu as pltpu
from jax.sharding import PartitionSpec as P

TIME_STEP = 0.05
GAMMAS = (8.0 / 15.0, 5.0 / 12.0, 3.0 / 4.0)
ZETAS = (0.0, -17.0 / 60.0, -5.0 / 12.0)
SECTIONS = 3
TOP = 32767.0
STEPS_PER_OCTAVE = 64.0
F32 = jnp.float32
BF16 = jnp.bfloat16
VMEM_LIMIT = 60 * 1024 * 1024


def spectral_table(points):
    offset = np.arange(points)[:, None] - np.arange(points)[None, :]
    away = np.where(offset == 0, 1, offset)
    table = 0.5 * (1 - 2 * (offset % 2)) / np.tan(np.pi * away / points)
    return np.where(offset == 0, 0.0, table).astype(np.float32)


def halves(table):
    high = table.astype(jnp.bfloat16)
    low = (table - high.astype(np.float32)).astype(jnp.bfloat16)
    return np.asarray(high), np.asarray(low)


def split(value):
    high = value.astype(BF16)
    return high, (value - high.astype(F32)).astype(BF16)


def dot(left, right):
    return jnp.dot(left, right, preferred_element_type=F32)


class Plan:
    def __init__(self, rows, nx, nz, parts):
        self.rows, self.nx, self.nz, self.parts = rows, nx, nz, parts
        self.cuts = 1 if nx // parts >= 16 else 2
        self.width = nx * self.cuts // parts
        self.depth = nz // self.cuts
        self.lines = rows * parts
        self.scale_rows = -(-rows // 16) * 16

    def rows_of(self, fields):
        return fields * self.rows * self.width

    def piece(self, number):
        along = pl.multiple_of(number // self.cuts * self.width, self.width)
        if self.cuts == 1:
            return pl.ds(along, self.width), pl.ds(0, self.depth)
        across = pl.multiple_of(number % self.cuts * self.depth, self.depth)
        return pl.ds(along, self.width), pl.ds(across, self.depth)


def scale_code(largest):
    return jnp.floor(jnp.log2(jnp.maximum(largest, 1e-35)) * STEPS_PER_OCTAVE) + 2.0


def encode(code):
    return TOP * jnp.exp2(code * (-1.0 / STEPS_PER_OCTAVE))


def decode(code):
    return (1.0 / TOP) * jnp.exp2(code * (1.0 / STEPS_PER_OCTAVE))


def to_short(value):
    return jnp.round(value).astype(jnp.int32).astype(jnp.int16)


def from_short(value):
    return value.astype(jnp.int32).astype(F32)


def column_max(values):
    return functools.reduce(
        jnp.maximum, [jnp.max(jnp.abs(v), axis=0, keepdims=True) for v in values]
    )


def pack_kernel(plan, me_ref, tangent_ref, flow_ref, *rest):
    outs, codes = rest[: plan.parts], rest[plan.parts]
    row = pl.program_id(0)
    me = me_ref[0]
    for d in range(plan.parts):
        along, across = plan.piece(me ^ d)
        values = [tangent_ref[c, 0, along, across] for c in range(3)]
        values.append(flow_ref[0, 0, along, across].astype(F32))
        for first, group in ((0, values[:3]), (3, values[3:])):
            code = scale_code(column_max(group))
            factor = encode(code)
            for k, value in enumerate(group):
                start = pl.multiple_of(((first + k) * plan.rows + row) * plan.width, plan.width)
                outs[d][pl.ds(start, plan.width), :] = to_short(value * factor)
            base = 0 if first == 0 else plan.scale_rows
            codes[d, pl.ds(base + row, 1), :] = code

    @pl.when(row == plan.rows - 1)
    def _():
        for d in range(plan.parts):
            outs[d][plan.rows_of(4) :, :] = codes[d].astype(jnp.int32).astype(jnp.int16)


def pack_start(plan, me, tangent, flow):
    height = plan.rows_of(4) + 2 * plan.scale_rows
    return pl.pallas_call(
        functools.partial(pack_kernel, plan),
        grid_spec=pltpu.PrefetchScalarGridSpec(
            num_scalar_prefetch=1,
            grid=(plan.rows,),
            in_specs=[
                pl.BlockSpec((3, 1, plan.nx, plan.nz), lambda j, *_: (0, j, 0, 0)),
                pl.BlockSpec((1, 1, plan.nx, plan.nz), lambda j, *_: (1, j, 0, 0)),
            ],
            out_specs=[pl.BlockSpec((height, plan.depth), lambda j, *_: (0, 0))] * plan.parts,
            scratch_shapes=[pltpu.VMEM((plan.parts, 2 * plan.scale_rows, plan.depth), F32)],
        ),
        out_shape=[jax.ShapeDtypeStruct((height, plan.depth), jnp.int16)] * plan.parts,
        compiler_params=pltpu.CompilerParams(vmem_limit_bytes=VMEM_LIMIT),
        cost_estimate=pl.CostEstimate(flops=0, transcendentals=0, bytes_accessed=20_000_000),
        name="pack_start",
    )(me, tangent, flow)


def explicit_kernel(plan, received, me_ref, *refs):
    parts = plan.parts
    if received:
        sources, refs = refs[:parts], refs[parts:]
    else:
        tangent_ref, refs = refs[0], refs[1:]
    flow_ref, shear_ref, dx_ref, dz_ref = refs[:4]
    outs = refs[4 : 4 + parts]
    speed, term, codes = refs[4 + parts : 7 + parts]
    row = pl.program_id(0)
    me = me_ref[0]
    nx = plan.nx
    if received:
        scales = refs[7 + parts]

        @pl.when(row == 0)
        def _():
            for d in range(parts):
                scales[d] = decode(from_short(sources[d][plan.rows_of(3) :, :]))

        for d in range(parts):
            along, across = plan.piece(me ^ d)
            for c in range(3):
                start = pl.multiple_of((c * plan.rows + row) * plan.width, plan.width)
                value = from_short(sources[d][pl.ds(start, plan.width), :])
                speed[c, along, across] = value * scales[d, c : c + 1, :]
    else:
        for c in range(3):
            speed[c] = tangent_ref[c, 0]
    for c in range(3):
        high, low = split(speed[c])
        flow = flow_ref[c, 0]
        both = dot(dx_ref[...], high)
        along_x = both[:nx] + both[nx:] + dot(dx_ref[:nx, :], low)
        along_z = dot(high, dz_ref[0]) + (dot(low, dz_ref[0]) + dot(high, dz_ref[1]))
        carried = flow_ref[0, 0].astype(F32) * along_x + flow_ref[2, 0].astype(F32) * along_z
        both = dot(dx_ref[...], flow)
        base_dx = both[:nx] + both[nx:]
        base_dz = dot(flow, dz_ref[0]) + dot(flow, dz_ref[1])
        sheared = (
            speed[0] * base_dx + speed[1] * shear_ref[c, 0].astype(F32) + speed[2] * base_dz
        )
        term[c] = -(carried + sheared)
    for d in range(parts):
        along, across = plan.piece(me ^ d)
        values = [term[c, along, across] for c in range(3)]
        code = scale_code(column_max(values))
        factor = encode(code)
        for c in range(3):
            start = pl.multiple_of((c * plan.rows + row) * plan.width, plan.width)
            outs[d][pl.ds(start, plan.width), :] = to_short(values[c] * factor)
        codes[d, pl.ds(row, 1), :] = code

    @pl.when(row == plan.rows - 1)
    def _():
        for d in range(parts):
            outs[d][plan.rows_of(3) :, :] = codes[d].astype(jnp.int32).astype(jnp.int16)


def explicit(plan, me, velocity, flow, shear, dx, dz):
    received = isinstance(velocity, list)
    parts = plan.parts
    height = plan.rows_of(3) + plan.scale_rows
    field = pl.BlockSpec((3, 1, plan.nx, plan.nz), lambda j, *_: (0, j, 0, 0))
    scratch = [
        pltpu.VMEM((3, plan.nx, plan.nz), F32),
        pltpu.VMEM((3, plan.nx, plan.nz), F32),
        pltpu.VMEM((parts, plan.scale_rows, plan.depth), F32),
    ]
    if received:
        first = [
            pl.BlockSpec(v.shape, lambda j, *_: (0, 0), pipeline_mode=pl.Buffered(1))
            for v in velocity
        ]
        scratch.append(pltpu.VMEM((parts, 16, plan.depth), F32))
    else:
        first, velocity = [field], [velocity]
    return pl.pallas_call(
        functools.partial(explicit_kernel, plan, received),
        grid_spec=pltpu.PrefetchScalarGridSpec(
            num_scalar_prefetch=1,
            grid=(plan.rows,),
            in_specs=first
            + [
                field,
                field,
                pl.BlockSpec(dx.shape, lambda j, *_: (0, 0)),
                pl.BlockSpec(dz.shape, lambda j, *_: (0, 0, 0)),
            ],
            out_specs=[pl.BlockSpec((height, plan.depth), lambda j, *_: (0, 0))] * parts,
            scratch_shapes=scratch,
        ),
        out_shape=[jax.ShapeDtypeStruct((height, plan.depth), jnp.int16)] * parts,
        compiler_params=pltpu.CompilerParams(vmem_limit_bytes=VMEM_LIMIT),
        cost_estimate=pl.CostEstimate(
            flops=12_000_000_000, transcendentals=0, bytes_accessed=40_000_000
        ),
        name="explicit",
    )(me, *velocity, flow, shear, dx, dz)


def stacked(matrices):
    rows = []
    for matrix in matrices:
        high, low = split(matrix)
        rows.append(jnp.concatenate([high, high], axis=1))
        rows.append(jnp.concatenate([low, jnp.zeros_like(low)], axis=1))
    return jnp.concatenate(rows, axis=0)


def precise_dot(left, right):
    high, low = split(left)
    right_high, right_low = split(right)
    return dot(high, right_high) + (dot(low, right_high) + dot(high, right_low))


def put(field, rows, value):
    for half in range(field.shape[0]):
        field[half, rows, :] = value[:, half * 128 : half * 128 + 128]


def get(field, rows):
    return jnp.concatenate([field[half, rows, :] for half in range(field.shape[0])], axis=1)


def unpack_lines(plan, me, sources, scales, field):
    for d, (source, scale) in enumerate(zip(sources, scales)):
        scale = decode(from_short(scale[...]))
        first = pl.multiple_of((me ^ d) * plan.rows_of(1), plan.width)
        for j in range(plan.rows):
            value = from_short(source[j * plan.width : (j + 1) * plan.width, :])
            put(field, pl.ds(first + j * plan.width, plan.width), value * scale[j : j + 1, :])


def first_lines_kernel(plan, me_ref, *refs):
    parts, lines = plan.parts, plan.lines
    values, scales = refs[:parts], refs[parts : 2 * parts]
    flows, flow_scales = refs[2 * parts : 3 * parts], refs[3 * parts : 4 * parts]
    wall_ref, right_ref, turned_ref, flow_ref, field, table = refs[4 * parts :]
    me = me_ref[0]

    @pl.when(pl.program_id(0) == 0)
    def _():
        table[...] = stacked([wall_ref[...]])
        unpack_lines(plan, me, flows, flow_scales, field)

        def turn(r, carry):
            flow_ref[r] = get(field, pl.ds(r, lines, stride=plan.width))
            return carry

        lax.fori_loop(0, plan.width, turn, 0)

    unpack_lines(plan, me, values, scales, field)

    def line(r, carry):
        value = get(field, pl.ds(r, lines, stride=plan.width))
        product = dot(table[...], jnp.concatenate(split(value), axis=0))
        turned = -(flow_ref[r] * (product[:lines] + product[lines:]))
        turned_ref[0, r] = turned
        right_ref[0, r] = value + (TIME_STEP * GAMMAS[0]) * turned
        return carry

    lax.fori_loop(0, plan.width, line, 0)


def first_lines(plan, me, blocks, wall):
    parts, lines, width, depth = plan.parts, plan.lines, plan.width, plan.depth
    at = plan.rows_of(4) // plan.scale_rows
    part = (plan.rows_of(1), depth)
    codes = (plan.scale_rows, depth)
    state = jax.ShapeDtypeStruct((3, width, lines, depth), F32)
    state_spec = pl.BlockSpec((1, width, lines, depth), lambda c, *_: (c, 0, 0, 0))
    return pl.pallas_call(
        functools.partial(first_lines_kernel, plan),
        grid_spec=pltpu.PrefetchScalarGridSpec(
            num_scalar_prefetch=1,
            grid=(3,),
            in_specs=[pl.BlockSpec(part, lambda c, *_: (c, 0))] * parts
            + [pl.BlockSpec(codes, lambda c, *_: (at, 0))] * parts
            + [pl.BlockSpec(part, lambda c, *_: (3, 0))] * parts
            + [pl.BlockSpec(codes, lambda c, *_: (at + 1, 0))] * parts
            + [pl.BlockSpec(wall.shape, lambda c, *_: (0, 0))],
            out_specs=[
                state_spec,
                state_spec,
                pl.BlockSpec((width, lines, depth), lambda c, *_: (0, 0, 0)),
            ],
            scratch_shapes=[
                pltpu.VMEM((depth // 128, lines * width, 128), F32),
                pltpu.VMEM((2 * lines, 2 * lines), BF16),
            ],
        ),
        out_shape=[state, state, jax.ShapeDtypeStruct((width, lines, depth), F32)],
        compiler_params=pltpu.CompilerParams(vmem_limit_bytes=VMEM_LIMIT),
        cost_estimate=pl.CostEstimate(
            flops=1_000_000_000, transcendentals=0, bytes_accessed=30_000_000
        ),
        name="first_lines",
    )(me, *(blocks * 4), wall)


def lines_kernel(plan, section, me_ref, *refs):
    parts, lines = plan.parts, plan.lines
    last = section == SECTIONS - 1
    values, scales, refs = refs[:parts], refs[parts : 2 * parts], refs[2 * parts :]
    if last:
        wall_ref, solve_ref, right_ref = refs[:3]
        outs, (field, table, codes) = refs[3 : 3 + parts], refs[3 + parts :]
    else:
        wall_ref, solve_ref, right_ref, turned_ref, flow_ref = refs[:5]
        outs, refs = refs[5 : 5 + parts], refs[5 + parts :]
        right_out, turned_out, field, table, codes = refs
    me = me_ref[0]
    component = pl.program_id(0)

    @pl.when(component == 0)
    def _():
        solve = solve_ref[0]
        tables = [solve] if last else [solve, precise_dot(wall_ref[...], solve)]
        table[...] = stacked(tables)
        codes[...] = jnp.zeros_like(codes)

    unpack_lines(plan, me, values, scales, field)

    def line(r, carry):
        here = pl.ds(r, lines, stride=plan.width)
        term = get(field, here)
        right = right_ref[0, r] + (TIME_STEP * GAMMAS[section]) * term
        product = dot(table[...], jnp.concatenate(split(right), axis=0))
        value = product[:lines] + product[lines : 2 * lines]
        put(field, here, value)
        if not last:
            slope = product[2 * lines : 3 * lines] + product[3 * lines :]
            turned = -(flow_ref[r] * slope)
            past = term + turned_ref[0, r]
            turned_out[0, r] = turned
            right_out[0, r] = (
                value
                + (TIME_STEP * ZETAS[section + 1]) * past
                + (TIME_STEP * GAMMAS[section + 1]) * turned
            )
        return carry

    lax.fori_loop(0, plan.width, line, 0)

    for d in range(parts):
        first = pl.multiple_of((me ^ d) * plan.rows_of(1), plan.width)
        chunk = [
            get(field, pl.ds(first + j * plan.width, plan.width)) for j in range(plan.rows)
        ]
        code = scale_code(column_max(chunk))
        factor = encode(code)
        for j in range(plan.rows):
            start = pl.multiple_of((component * plan.rows + j) * plan.width, plan.width)
            outs[d][pl.ds(start, plan.width), :] = to_short(chunk[j] * factor)
        codes[d, pl.ds(component, 1), :] = code

    @pl.when(component == 2)
    def _():
        for d in range(parts):
            outs[d][plan.rows_of(3) :, :] = codes[d].astype(jnp.int32).astype(jnp.int16)


def advance_lines(plan, section, me, blocks, wall, solves, right, turned, flow):
    parts, lines, width, depth = plan.parts, plan.lines, plan.width, plan.depth
    last = section == SECTIONS - 1
    at = plan.rows_of(3) // plan.scale_rows
    height = plan.rows_of(3) + 16
    state_spec = pl.BlockSpec((1, width, lines, depth), lambda c, *_: (c, 0, 0, 0))
    in_specs = (
        [pl.BlockSpec((plan.rows_of(1), depth), lambda c, *_: (c, 0))] * parts
        + [pl.BlockSpec((plan.scale_rows, depth), lambda c, *_: (at, 0))] * parts
        + [
            pl.BlockSpec(wall.shape, lambda c, *_: (0, 0)),
            pl.BlockSpec((1, lines, lines), lambda c, *_: (section, 0, 0)),
            state_spec,
        ]
    )
    args = [me, *blocks, *blocks, wall, solves, right]
    out_specs = [pl.BlockSpec((height, depth), lambda c, *_: (0, 0))] * parts
    out_shape = [jax.ShapeDtypeStruct((height, depth), jnp.int16)] * parts
    copies = 2
    if not last:
        in_specs += [
            state_spec,
            pl.BlockSpec(flow.shape, lambda c, *_: (0, 0, 0), pipeline_mode=pl.Buffered(1)),
        ]
        args += [turned, flow]
        out_specs = out_specs + [state_spec, state_spec]
        out_shape = out_shape + [jax.ShapeDtypeStruct(right.shape, F32)] * 2
        copies = 4
    results = pl.pallas_call(
        functools.partial(lines_kernel, plan, section),
        grid_spec=pltpu.PrefetchScalarGridSpec(
            num_scalar_prefetch=1,
            grid=(3,),
            in_specs=in_specs,
            out_specs=out_specs,
            scratch_shapes=[
                pltpu.VMEM((depth // 128, lines * width, 128), F32),
                pltpu.VMEM((copies * lines, 2 * lines), BF16),
                pltpu.VMEM((parts, 16, depth), F32),
            ],
        ),
        out_shape=out_shape,
        compiler_params=pltpu.CompilerParams(vmem_limit_bytes=VMEM_LIMIT),
        cost_estimate=pl.CostEstimate(
            flops=2_000_000_000, transcendentals=0, bytes_accessed=50_000_000
        ),
        name="advance_lines",
    )(*args)
    return results[:parts], results[parts:]


def result_kernel(plan, me_ref, shift_ref, pick_ref, *refs):
    parts = plan.parts
    sources = refs[:parts]
    near_ref, far_ref, out_ref, speed, scales = refs[parts:]
    row = pl.program_id(0)
    me = me_ref[0]

    @pl.when(row == 0)
    def _():
        for d in range(parts):
            scales[d] = decode(from_short(sources[d][plan.rows_of(3) :, :]))

    for d in range(parts):
        along, across = plan.piece(me ^ d)
        for c in range(3):
            start = pl.multiple_of((c * plan.rows + row) * plan.width, plan.width)
            value = from_short(sources[d][pl.ds(start, plan.width), :])
            speed[c, along, across] = value * scales[d, c : c + 1, :]
    far = pick_ref[0] != 0
    for c in range(3):
        rolled = pltpu.roll(speed[c], shift_ref[0], axis=1)

        @pl.when(far)
        def _():
            out_ref[c, 0] = rolled - far_ref[c, 0]

        @pl.when(jnp.logical_not(far))
        def _():
            out_ref[c, 0] = rolled - near_ref[c, 0]


def result(plan, me, shift, pick, blocks, near, far):
    parts = plan.parts
    block = (3, 1, plan.nx, plan.nz)
    return pl.pallas_call(
        functools.partial(result_kernel, plan),
        grid_spec=pltpu.PrefetchScalarGridSpec(
            num_scalar_prefetch=3,
            grid=(plan.rows,),
            in_specs=[
                pl.BlockSpec(b.shape, lambda j, *_: (0, 0), pipeline_mode=pl.Buffered(1))
                for b in blocks
            ]
            + [
                pl.BlockSpec(block, lambda j, me, shift, pick: (0, j * (1 - pick[0]), 0, 0)),
                pl.BlockSpec(block, lambda j, me, shift, pick: (0, j * pick[0], 0, 0)),
            ],
            out_specs=pl.BlockSpec(block, lambda j, *_: (0, j, 0, 0)),
            scratch_shapes=[
                pltpu.VMEM((3, plan.nx, plan.nz), F32),
                pltpu.VMEM((parts, 16, plan.depth), F32),
            ],
        ),
        out_shape=jax.ShapeDtypeStruct((3, plan.rows, plan.nx, plan.nz), F32),
        compiler_params=pltpu.CompilerParams(vmem_limit_bytes=VMEM_LIMIT),
        cost_estimate=pl.CostEstimate(flops=0, transcendentals=0, bytes_accessed=25_000_000),
        name="result",
    )(me, shift, pick, *blocks, near, far)


def exchange(blocks):
    parts = len(blocks)
    moved = [blocks[0]]
    for d in range(1, parts):
        moved.append(lax.ppermute(blocks[d], "grid", [(i, i ^ d) for i in range(parts)]))
    return moved


def behind(block, distance):
    devices = lax.axis_size("seg")
    route = [((i + distance) % devices, i) for i in range(devices)]
    return lax.ppermute(block, "seg", route)


def successors(tangent, successor):
    segments = lax.axis_size("seg")
    position = lax.axis_index("seg")
    labels = jnp.arange(successor.shape[0], dtype=jnp.int32)
    ahead = jnp.sum(jnp.where(labels == position, successor, 0))
    offset = (ahead - position) % segments
    near = behind(tangent, 1)
    bits = (segments - 1).bit_length()
    for bit in range(1, bits - 1):
        near = jnp.where(offset // (1 << bit) % 2 == 1, behind(near, 1 << bit), near)
    far = behind(near, 1 << (bits - 1))
    return near, far, (offset // (1 << (bits - 1)) % 2).reshape(1)


def shards(
    tangent, base_flow, base_shear, wall_derivative, implicit_inverse, successor, spanwise_shift
):
    tangent, flow, shear = tangent[0], base_flow[0], base_shear[0]
    _, rows, nx, nz = tangent.shape
    plan = Plan(rows, nx, nz, lax.axis_size("grid"))
    me = lax.axis_index("grid").astype(jnp.int32).reshape(1)
    dx = jnp.asarray(np.concatenate(halves(spectral_table(nx)), axis=0))
    dz = jnp.asarray(np.stack(halves(spectral_table(nz).T)))

    start = exchange(pack_start(plan, me, tangent, flow))
    term = exchange(explicit(plan, me, tangent, flow, shear, dx, dz))
    near, far, pick = successors(tangent, successor)
    right, turned, wall_flow = first_lines(plan, me, start, wall_derivative)
    for section in range(SECTIONS):
        value, state = advance_lines(
            plan, section, me, term, wall_derivative, implicit_inverse, right, turned, wall_flow
        )
        value = exchange(value)
        if section < SECTIONS - 1:
            right, turned = state
            term = exchange(explicit(plan, me, value, flow, shear, dx, dz))
    return result(plan, me, spanwise_shift, pick, value, near, far)[None]


def solution(mesh):
    placed = P("seg", None, "grid", None, None)
    return jax.shard_map(
        shards,
        mesh=mesh,
        in_specs=(placed, placed, placed, P(), P(), P(), P("seg")),
        out_specs=placed,
        check_vma=False,
    )
```

time: 2840 us -> 1050 us (0.37)
  blocking collectives: 1120 us -> 0 us
  waiting for transfers between devices: 1120 us -> 719 us
  Pallas kernels: 0 us -> 272 us
  local copies, waits for them, and re-layouts: 265 us -> 0.99 us
  matrix products: 255 us -> 0 us
    all_to_all x6 -> x0, waiting for transfers between devices: 1120 us -> none  [the longest x2 387 us: shards(): lax.all_to_all(solved, 'grid', split_axis=1, concat_axis=2, tiled=True)]
    all_to_all x4 -> x0, blocking collectives: 1120 us -> none  [to_lines(): lax.all_to_all(velocity, 'grid', split_axis=2, concat_axis=1, tiled=True)]
    ppermute x2 -> x51, waiting for transfers between devices: 0.01 us -> 719 us  [the longest x49 675 us: exchange(): lax.ppermute(blocks[d], 'grid', [(i, i ^ d) for i in range(parts)])]
    pallas_call x0 -> x9, Pallas kernels: none -> 272 us  [the longest x3 141 us: advance_lines(): pl.pallas_call(functools.partial(lines_kernel, plan, section), grid_spec=...]
    dot_general x14 -> x0, matrix products: 255 us -> none  [the longest x4 95.7 us: derive_streamwise(): return jnp.einsum('jk,cykz->cyjz', matrix, velocity, precision=HIGHEST)]
    all_to_all x12 -> x0, local copies, waits for them, and re-layouts: 111 us -> none  [the longest x4 49.9 us: to_lines(): lax.all_to_all(velocity, 'grid', split_axis=2, concat_axis=1, tiled=True)]
    transpose x6 -> x0, local copies, waits for them, and re-layouts: 62.3 us -> none  [apply_wall(): return jnp.einsum('jk,ckxz->cjxz', matrix, velocity, precision=HIGHEST)]
    ppermute x2 -> x51, starting transfers between devices: 3.42 us -> 55.5 us  [the longest x49 52.1 us: exchange(): lax.ppermute(blocks[d], 'grid', [(i, i ^ d) for i in range(parts)])]
  transfers between devices with their start and end apart: 8 -> 51, of which waited for: 6 -> 34; matrix products, arithmetic and copies ran while one was open for 4% -> 0% of each run, Pallas kernels for 0% -> 24%
where the time goes in v1:
time: 1050 us
  waiting for transfers between devices  719 us (68%)
  Pallas kernels  272 us (26%)
  starting transfers between devices  55.5 us (5%)
    ppermute x49, waiting for transfers between devices, exchange(): lax.ppermute(blocks[d], 'grid', [(i, i ^ d) for i in range(parts)])  675 us
    pallas_call x3, Pallas kernels, advance_lines(): pl.pallas_call(functools.partial(lines_kernel, plan, section), grid_spec=...  141 us
    pallas_call x3, Pallas kernels, explicit(): pl.pallas_call(functools.partial(explicit_kernel, plan, received), grid_s...  67.1 us
    ppermute x49, starting transfers between devices, exchange(): lax.ppermute(blocks[d], 'grid', [(i, i ^ d) for i in range(parts)])  52.1 us
    ppermute x2, waiting for transfers between devices, behind(): return lax.ppermute(block, 'seg', route)  44.3 us
    pallas_call x1, Pallas kernels, first_lines(): pl.pallas_call(functools.partial(first_lines_kernel, plan), grid_spec=plt...  36.9 us
  transfers between devices with their start and end apart: 51, of which 34 were waited for; matrix products, arithmetic and copies ran while one was open for 0% of the time, Pallas kernels for 24%

profile of v1, /device:TPU:9, one launch (start us, length us, event | category | flops | bytes accessed | tf_op | source)
XLA Modules:
  0.0 1049.9 jit_solution(17446906827104858907)
XLA Ops:
  0.0 2.2 collective-permute-start.49
  2.2 20.8 %explicit.3 = (s16[1168,256]{1,0:T(8,128)(2,1)}, s16[1168,256]{1,0:T(8,128)(2,1)}, s16[1168,256]{1,0:T(8,128)(2,1)}, s16[1168,256]{1,0:T(8,128)(2,1)}, s16[1168,...) custom-call(s32[1]{0:T(128)} %bitcast.me_ref, ...), custom_call_target="tpu_custom_call" | custom-call | flops 12000000000 | bytes 40000000 | tf_op jit(solution)/shard_map/explicit/pallas_call | solution.py:211
  24.0 11.8 %pack_start.1 = (s16[1568,256]{1,0:T(8,128)(2,1)}, s16[1568,256]{1,0:T(8,128)(2,1)}, s16[1568,256]{1,0:T(8,128)(2,1)}, s16[1568,256]{1,0:T(8,128)(2,1)}, s16[156...) custom-call(s32[1]{0:T(128)} %bitcast.me_ref, ...), custom_call_target="tpu_custom_call" | custom-call | bytes 20000000 | tf_op jit(solution)/shard_map/pack_start/pallas_call | solution.py:115
  35.9 2.3 collective-permute-start.10
  39.6 2.4 collective-permute-start.12
  43.2 62.3 %collective-permute-done.2.refs_3_.refs_11_ = s16[1168,256]{1,0:T(8,128)(2,1)S(1)} collective-permute-done((s16[1168,256]{1,0:T(8,128)(2,1)S(1)}, s16[1168,256]{1,0:T(8,128)(2,1)S(1)}, u32[]{:S(2)}, u32[]{:S(2)}) %collective-permute-start.2) | collective-permute-done | bytes 598048 | tf_op jit(solution)/shard_map/ppermute | solution.py:512
  105.5 18.6 %collective-permute-done.10.refs_4_.refs_12_.refs_20_.refs_28_ = s16[1568,256]{1,0:T(8,128)(2,1)S(1)} collective-permute-done((s16[1568,256]{1,0:T(8,128)(2,1)}, s16[1568,256]{1,0:T(8,128)(2,1)S(1)}, u32[]{:S(2)}, u32[]{:S(2)}) %collective-permute-start.10) | collective-permute-done | bytes 802848 | tf_op jit(solution)/shard_map/ppermute | solution.py:512
  124.1 2.1 collective-permute-start.7
  126.2 15.3 %collective-permute-done.11.refs_5_.refs_13_.refs_21_.refs_29_ = s16[1568,256]{1,0:T(8,128)(2,1)S(1)} collective-permute-done((s16[1568,256]{1,0:T(8,128)(2,1)}, s16[1568,256]{1,0:T(8,128)(2,1)S(1)}, u32[]{:S(2)}, u32[]{:S(2)}) %collective-permute-start.11) | collective-permute-done | bytes 802848 | tf_op jit(solution)/shard_map/ppermute | solution.py:512
  141.5 3.0 collective-permute-start.8
  144.5 15.3 %collective-permute-done.12.refs_6_.refs_14_.refs_22_.refs_30_ = s16[1568,256]{1,0:T(8,128)(2,1)S(1)} collective-permute-done((s16[1568,256]{1,0:T(8,128)(2,1)}, s16[1568,256]{1,0:T(8,128)(2,1)S(1)}, u32[]{:S(2)}, u32[]{:S(2)}) %collective-permute-start.12) | collective-permute-done | bytes 802848 | tf_op jit(solution)/shard_map/ppermute | solution.py:512
  159.8 44.3 %collective-permute-done.49.refs_8_ = f32[3,12,256,256]{3,2,1,0:T(8,128)} collective-permute-done((f32[3,12,256,256]{3,2,1,0:T(8,128)}, f32[3,12,256,256]{3,2,1,0:T(8,128)}, u32[]{:S(2)}, u32[]{:S(2)}) %collective-permute-start.49) | collective-permute-done | bytes 9437216 | tf_op jit(solution)/shard_map/ppermute | solution.py:519
  205.4 2.3 collective-permute-start.3
  207.7 2.1 collective-permute-start.4
  209.8 1.3 collective-permute-start.5
  211.6 36.9 %first_lines.1 = (f32[3,32,96,256]{3,2,1,0:T(8,128)}, f32[3,32,96,256]{3,2,1,0:T(8,128)}, f32[32,96,256]{2,1,0:T(8,128)}) custom-call(s32[1]{0:T(128)} %bitcast.me_ref, s16[1568,256]{1,0:T(8,128)(2,1)} %get-tuple-element.75.refs_0_.refs_8_.refs_16_.refs_24_, s16[1568,256]{1,0:T(8,128)(2,1)} %copy-done.4, ...), custom_call_target="tpu_custom_call" | custom-call | flops 1000000000 | bytes 30000000 | tf_op jit(solution)/shard_map/first_lines/pallas_call | solution.py:306
  248.5 23.9 %collective-permute-done.3.refs_4_.refs_12_ = s16[1168,256]{1,0:T(8,128)(2,1)} collective-permute-done((s16[1168,256]{1,0:T(8,128)(2,1)}, s16[1168,256]{1,0:T(8,128)(2,1)}, u32[]{:S(2)}, u32[]{:S(2)}) %collective-permute-start.3) | collective-permute-done | bytes 598048 | tf_op jit(solution)/shard_map/ppermute | solution.py:512
  272.4 12.8 %collective-permute-done.4.refs_5_.refs_13_ = s16[1168,256]{1,0:T(8,128)(2,1)} collective-permute-done((s16[1168,256]{1,0:T(8,128)(2,1)}, s16[1168,256]{1,0:T(8,128)(2,1)}, u32[]{:S(2)}, u32[]{:S(2)}) %collective-permute-start.4) | collective-permute-done | bytes 598048 | tf_op jit(solution)/shard_map/ppermute | solution.py:512
  285.2 12.8 %collective-permute-done.5.refs_6_.refs_14_ = s16[1168,256]{1,0:T(8,128)(2,1)} collective-permute-done((s16[1168,256]{1,0:T(8,128)(2,1)}, s16[1168,256]{1,0:T(8,128)(2,1)}, u32[]{:S(2)}, u32[]{:S(2)}) %collective-permute-start.5) | collective-permute-done | bytes 598048 | tf_op jit(solution)/shard_map/ppermute | solution.py:512
  298.0 12.8 %collective-permute-done.6.refs_7_.refs_15_ = s16[1168,256]{1,0:T(8,128)(2,1)} collective-permute-done((s16[1168,256]{1,0:T(8,128)(2,1)}, s16[1168,256]{1,0:T(8,128)(2,1)}, u32[]{:S(2)}, u32[]{:S(2)}) %collective-permute-start.6) | collective-permute-done | bytes 598048 | tf_op jit(solution)/shard_map/ppermute | solution.py:512
  310.8 49.7 %advance_lines.3 = (s16[1168,256]{1,0:T(8,128)(2,1)}, s16[1168,256]{1,0:T(8,128)(2,1)}, s16[1168,256]{1,0:T(8,128)(2,1)}, s16[1168,256]{1,0:T(8,128)(2,1)}, s16[...) custom-call(s32[1]{0:T(128)} %bitcast.me_ref, ...), custom_call_target="tpu_custom_call" | custom-call | flops 2000000000 | bytes 50000000 | tf_op jit(solution)/shard_map/advance_lines/pallas_call | solution.py:425
  361.1 1.7 collective-permute-start.16
  362.8 1.7 collective-permute-start.17
  365.5 34.0 %collective-permute-done.15.refs_2_ = s16[1168,256]{1,0:T(8,128)(2,1)S(1)} collective-permute-done((s16[1168,256]{1,0:T(8,128)(2,1)}, s16[1168,256]{1,0:T(8,128)(2,1)S(1)}, u32[]{:S(2)}, u32[]{:S(2)}) %collective-permute-start.15) | collective-permute-done | bytes 598048 | tf_op jit(solution)/shard_map/ppermute | solution.py:512
  400.0 12.3 %collective-permute-done.16.refs_3_ = s16[1168,256]{1,0:T(8,128)(2,1)S(1)} collective-permute-done((s16[1168,256]{1,0:T(8,128)(2,1)}, s16[1168,256]{1,0:T(8,128)(2,1)S(1)}, u32[]{:S(2)}, u32[]{:S(2)}) %collective-permute-start.16) | collective-permute-done | bytes 598048 | tf_op jit(solution)/shard_map/ppermute | solution.py:512
  413.4 28.0 %collective-permute-done.18.refs_5_ = s16[1168,256]{1,0:T(8,128)(2,1)S(1)} collective-permute-done((s16[1168,256]{1,0:T(8,128)(2,1)}, s16[1168,256]{1,0:T(8,128)(2,1)S(1)}, u32[]{:S(2)}, u32[]{:S(2)}) %collective-permute-start.18) | collective-permute-done | bytes 598048 | tf_op jit(solution)/shard_map/ppermute | solution.py:512
  441.4 14.6 %collective-permute-done.19.refs_6_ = s16[1168,256]{1,0:T(8,128)(2,1)S(1)} collective-permute-done((s16[1168,256]{1,0:T(8,128)(2,1)}, s16[1168,256]{1,0:T(8,128)(2,1)S(1)}, u32[]{:S(2)}, u32[]{:S(2)}) %collective-permute-start.19) | collective-permute-done | bytes 598048 | tf_op jit(solution)/shard_map/ppermute | solution.py:512
  456.0 12.9 %collective-permute-done.20.refs_7_ = s16[1168,256]{1,0:T(8,128)(2,1)} collective-permute-done((s16[1168,256]{1,0:T(8,128)(2,1)}, s16[1168,256]{1,0:T(8,128)(2,1)}, u32[]{:S(2)}, u32[]{:S(2)}) %collective-permute-start.20) | collective-permute-done | bytes 598048 | tf_op jit(solution)/shard_map/ppermute | solution.py:512
  469.0 23.1 %explicit.4 = (s16[1168,256]{1,0:T(8,128)(2,1)}, s16[1168,256]{1,0:T(8,128)(2,1)}, s16[1168,256]{1,0:T(8,128)(2,1)}, s16[1168,256]{1,0:T(8,128)(2,1)}, s16[1168,...) custom-call(s32[1]{0:T(128)} %bitcast.me_ref, ...), custom_call_target="tpu_custom_call" | custom-call | flops 12000000000 | bytes 40000000 | tf_op jit(solution)/shard_map/explicit/pallas_call | solution.py:211
  492.6 1.7 collective-permute-start.23
  494.6 2.4 collective-permute-start.25
  497.0 33.6 %collective-permute-done.22.refs_2_.refs_10_ = s16[1168,256]{1,0:T(8,128)(2,1)S(1)} collective-permute-done((s16[1168,256]{1,0:T(8,128)(2,1)}, s16[1168,256]{1,0:T(8,128)(2,1)S(1)}, u32[]{:S(2)}, u32[]{:S(2)}) %collective-permute-start.22) | collective-permute-done | bytes 598048 | tf_op jit(solution)/shard_map/ppermute | solution.py:512
  531.0 12.4 %collective-permute-done.23.refs_3_.refs_11_ = s16[1168,256]{1,0:T(8,128)(2,1)S(1)} collective-permute-done((s16[1168,256]{1,0:T(8,128)(2,1)}, s16[1168,256]{1,0:T(8,128)(2,1)S(1)}, u32[]{:S(2)}, u32[]{:S(2)}) %collective-permute-start.23) | collective-permute-done | bytes 598048 | tf_op jit(solution)/shard_map/ppermute | solution.py:512
  544.7 3.0 collective-permute-done.25.refs_5_.refs_13_
  547.7 38.0 %collective-permute-done.26.refs_6_.refs_14_ = s16[1168,256]{1,0:T(8,128)(2,1)S(1)} collective-permute-done((s16[1168,256]{1,0:T(8,128)(2,1)}, s16[1168,256]{1,0:T(8,128)(2,1)S(1)}, u32[]{:S(2)}, u32[]{:S(2)}) %collective-permute-start.26) | collective-permute-done | bytes 598048 | tf_op jit(solution)/shard_map/ppermute | solution.py:512
  585.7 13.4 %collective-permute-done.27.refs_7_.refs_15_ = s16[1168,256]{1,0:T(8,128)(2,1)} collective-permute-done((s16[1168,256]{1,0:T(8,128)(2,1)}, s16[1168,256]{1,0:T(8,128)(2,1)}, u32[]{:S(2)}, u32[]{:S(2)}) %collective-permute-start.27) | collective-permute-done | bytes 598048 | tf_op jit(solution)/shard_map/ppermute | solution.py:512
  599.1 49.9 %advance_lines.4 = (s16[1168,256]{1,0:T(8,128)(2,1)}, s16[1168,256]{1,0:T(8,128)(2,1)}, s16[1168,256]{1,0:T(8,128)(2,1)}, s16[1168,256]{1,0:T(8,128)(2,1)}, s16[...) custom-call(s32[1]{0:T(128)} %bitcast.me_ref, ...), custom_call_target="tpu_custom_call" | custom-call | flops 2000000000 | bytes 50000000 | tf_op jit(solution)/shard_map/advance_lines/pallas_call | solution.py:425
  649.2 2.1 collective-permute-start.30
  651.6 2.0 collective-permute-start.32
  653.6 33.4 %collective-permute-done.29.refs_2_ = s16[1168,256]{1,0:T(8,128)(2,1)S(1)} collective-permute-done((s16[1168,256]{1,0:T(8,128)(2,1)}, s16[1168,256]{1,0:T(8,128)(2,1)S(1)}, u32[]{:S(2)}, u32[]{:S(2)}) %collective-permute-start.29) | collective-permute-done | bytes 598048 | tf_op jit(solution)/shard_map/ppermute | solution.py:512
  687.6 12.2 %collective-permute-done.30.refs_3_ = s16[1168,256]{1,0:T(8,128)(2,1)S(1)} collective-permute-done((s16[1168,256]{1,0:T(8,128)(2,1)}, s16[1168,256]{1,0:T(8,128)(2,1)S(1)}, u32[]{:S(2)}, u32[]{:S(2)}) %collective-permute-start.30) | collective-permute-done | bytes 598048 | tf_op jit(solution)/shard_map/ppermute | solution.py:512
  699.8 1.5 collective-permute-start.34
  701.3 3.3 collective-permute-done.32.refs_5_
  704.6 38.0 %collective-permute-done.33.refs_6_ = s16[1168,256]{1,0:T(8,128)(2,1)S(1)} collective-permute-done((s16[1168,256]{1,0:T(8,128)(2,1)}, s16[1168,256]{1,0:T(8,128)(2,1)S(1)}, u32[]{:S(2)}, u32[]{:S(2)}) %collective-permute-start.33) | collective-permute-done | bytes 598048 | tf_op jit(solution)/shard_map/ppermute | solution.py:512
  742.6 13.4 %collective-permute-done.34.refs_7_ = s16[1168,256]{1,0:T(8,128)(2,1)} collective-permute-done((s16[1168,256]{1,0:T(8,128)(2,1)}, s16[1168,256]{1,0:T(8,128)(2,1)}, u32[]{:S(2)}, u32[]{:S(2)}) %collective-permute-start.34) | collective-permute-done | bytes 598048 | tf_op jit(solution)/shard_map/ppermute | solution.py:512
  756.1 23.2 %explicit.5 = (s16[1168,256]{1,0:T(8,128)(2,1)}, s16[1168,256]{1,0:T(8,128)(2,1)}, s16[1168,256]{1,0:T(8,128)(2,1)}, s16[1168,256]{1,0:T(8,128)(2,1)}, s16[1168,...) custom-call(s32[1]{0:T(128)} %bitcast.me_ref, ...), custom_call_target="tpu_custom_call" | custom-call | flops 12000000000 | bytes 40000000 | tf_op jit(solution)/shard_map/explicit/pallas_call | solution.py:211
  779.5 2.1 collective-permute-start.37
  781.8 2.0 collective-permute-start.39
  783.9 33.4 %collective-permute-done.36.refs_2_.refs_10_ = s16[1168,256]{1,0:T(8,128)(2,1)S(1)} collective-permute-done((s16[1168,256]{1,0:T(8,128)(2,1)}, s16[1168,256]{1,0:T(8,128)(2,1)S(1)}, u32[]{:S(2)}, u32[]{:S(2)}) %collective-permute-start.36) | collective-permute-done | bytes 598048 | tf_op jit(solution)/shard_map/ppermute | solution.py:512
  817.9 12.2 %collective-permute-done.37.refs_3_.refs_11_ = s16[1168,256]{1,0:T(8,128)(2,1)S(1)} collective-permute-done((s16[1168,256]{1,0:T(8,128)(2,1)}, s16[1168,256]{1,0:T(8,128)(2,1)S(1)}, u32[]{:S(2)}, u32[]{:S(2)}) %collective-permute-start.37) | collective-permute-done | bytes 598048 | tf_op jit(solution)/shard_map/ppermute | solution.py:512
  830.0 1.5 collective-permute-start.41
  831.5 3.3 collective-permute-done.39.refs_5_.refs_13_
  834.9 38.0 %collective-permute-done.40.refs_6_.refs_14_ = s16[1168,256]{1,0:T(8,128)(2,1)S(1)} collective-permute-done((s16[1168,256]{1,0:T(8,128)(2,1)}, s16[1168,256]{1,0:T(8,128)(2,1)S(1)}, u32[]{:S(2)}, u32[]{:S(2)}) %collective-permute-start.40) | collective-permute-done | bytes 598048 | tf_op jit(solution)/shard_map/ppermute | solution.py:512
  872.9 13.4 %collective-permute-done.41.refs_7_.refs_15_ = s16[1168,256]{1,0:T(8,128)(2,1)} collective-permute-done((s16[1168,256]{1,0:T(8,128)(2,1)}, s16[1168,256]{1,0:T(8,128)(2,1)}, u32[]{:S(2)}, u32[]{:S(2)}) %collective-permute-start.41) | collective-permute-done | bytes 598048 | tf_op jit(solution)/shard_map/ppermute | solution.py:512
  886.4 41.4 %advance_lines.5 = (s16[1168,256]{1,0:T(8,128)(2,1)}, s16[1168,256]{1,0:T(8,128)(2,1)}, s16[1168,256]{1,0:T(8,128)(2,1)}, s16[1168,256]{1,0:T(8,128)(2,1)}, s16[...) custom-call(s32[1]{0:T(128)} %bitcast.me_ref, ...), custom_call_target="tpu_custom_call" | custom-call | flops 2000000000 | bytes 50000000 | tf_op jit(solution)/shard_map/advance_lines/pallas_call | solution.py:425
  927.9 2.1 collective-permute-start.44
  930.2 2.0 collective-permute-start.46
  932.3 33.4 %collective-permute-done.43.refs_2_ = s16[1168,256]{1,0:T(8,128)(2,1)S(1)} collective-permute-done((s16[1168,256]{1,0:T(8,128)(2,1)}, s16[1168,256]{1,0:T(8,128)(2,1)S(1)}, u32[]{:S(2)}, u32[]{:S(2)}) %collective-permute-start.43) | collective-permute-done | bytes 598048 | tf_op jit(solution)/shard_map/ppermute | solution.py:512
  966.3 12.2 %collective-permute-done.44.refs_3_ = s16[1168,256]{1,0:T(8,128)(2,1)S(1)} collective-permute-done((s16[1168,256]{1,0:T(8,128)(2,1)}, s16[1168,256]{1,0:T(8,128)(2,1)S(1)}, u32[]{:S(2)}, u32[]{:S(2)}) %collective-permute-start.44) | collective-permute-done | bytes 598048 | tf_op jit(solution)/shard_map/ppermute | solution.py:512
  978.5 1.5 collective-permute-start.48
  982.0 1.3 collective-permute-done.46.refs_5_
  983.3 38.1 %collective-permute-done.47.refs_6_ = s16[1168,256]{1,0:T(8,128)(2,1)} collective-permute-done((s16[1168,256]{1,0:T(8,128)(2,1)}, s16[1168,256]{1,0:T(8,128)(2,1)}, u32[]{:S(2)}, u32[]{:S(2)}) %collective-permute-start.47) | collective-permute-done | bytes 598048 | tf_op jit(solution)/shard_map/ppermute | solution.py:512
  1021.4 13.3 %collective-permute-done.48.refs_7_ = s16[1168,256]{1,0:T(8,128)(2,1)} collective-permute-done((s16[1168,256]{1,0:T(8,128)(2,1)}, s16[1168,256]{1,0:T(8,128)(2,1)}, u32[]{:S(2)}, u32[]{:S(2)}) %collective-permute-start.48) | collective-permute-done | bytes 598048 | tf_op jit(solution)/shard_map/ppermute | solution.py:512
  1034.8 15.1 %result.1 = f32[3,12,256,256]{3,2,1,0:T(8,128)} custom-call(s32[1]{0:T(128)} %bitcast.me_ref, s32[1]{0:T(128)S(6)} %copy.10.shift_ref, s32[1]{0:T(128)} %bitcast.1.pick_ref, s16[1168,256]{1,0:T(8,128)(2,1)} %get-tuple-element.121.refs_0_, s16[1168,256]{1,0:T(8,128)(2,1)} %copy-done.20, s16[1168,256]{1,0:T(8,128)(2,1)} %copy-done.21, ...), custom_call_target="tpu_custom_call" | custom-call | bytes 25000000 | tf_op jit(solution)/shard_map/result/pallas_call | solution.py:482
  (126 shorter events, 15.1 us)
Async XLA Ops:
  0.0 204.1 %collective-permute-start.49 = (f32[3,12,256,256]{3,2,1,0:T(8,128)}, f32[3,12,256,256]{3,2,1,0:T(8,128)}, u32[]{:S(2)}, u32[]{:S(2)}) collective-permute-start(f32[3,12,256,256]{3,2,1,0:T(8,128)} %bitcast.6), channel_id=1, source_target_pairs={{8,0},{16,8},{24,16},{0,24},{9,1},{17,9},{25,17},{1,25},{10,2},{18... | collective-permute-start | bytes 28311560 | tf_op jit(solution)/shard_map/ppermute | solution.py:519
  22.9 15.8 %collective-permute-start = (s16[1168,256]{1,0:T(8,128)(2,1)}, s16[1168,256]{1,0:T(8,128)(2,1)S(1)}, u32[]{:S(2)}, u32[]{:S(2)}) collective-permute-start(s16[1168,256]{1,0:T(8,128)(2,1)} %get-tuple-element.68), channel_id=1, source_target_pairs={{0,1},{1,0},{2,3},{3,2},{4,5},{5,4},{6,7},{7,6},{8,9},{9,8},{10,11... | collective-permute-start | bytes 1794056 | tf_op jit(solution)/shard_map/ppermute | solution.py:512
  23.9 18.2 %collective-permute-start.1 = (s16[1168,256]{1,0:T(8,128)(2,1)}, s16[1168,256]{1,0:T(8,128)(2,1)S(1)}, u32[]{:S(2)}, u32[]{:S(2)}) collective-permute-start(s16[1168,256]{1,0:T(8,128)(2,1)} %get-tuple-element.69), channel_id=1, source_target_pairs={{0,2},{1,3},{2,0},{3,1},{4,6},{5,7},{6,4},{7,5},{8,10},{9,11},{10,... | collective-permute-start | bytes 1794056 | tf_op jit(solution)/shard_map/ppermute | solution.py:512
  35.9 88.2 %collective-permute-start.10 = (s16[1568,256]{1,0:T(8,128)(2,1)}, s16[1568,256]{1,0:T(8,128)(2,1)S(1)}, u32[]{:S(2)}, u32[]{:S(2)}) collective-permute-start(s16[1568,256]{1,0:T(8,128)(2,1)} %get-tuple-element.79), channel_id=1, source_target_pairs={{0,4},{1,5},{2,6},{3,7},{4,0},{5,1},{6,2},{7,3},{8,12},{9,13},{10,... | collective-permute-start | bytes 2408456 | tf_op jit(solution)/shard_map/ppermute | solution.py:512
  38.2 103.3 %collective-permute-start.11 = (s16[1568,256]{1,0:T(8,128)(2,1)}, s16[1568,256]{1,0:T(8,128)(2,1)S(1)}, u32[]{:S(2)}, u32[]{:S(2)}) collective-permute-start(s16[1568,256]{1,0:T(8,128)(2,1)} %get-tuple-element.80), channel_id=1, source_target_pairs={{0,5},{1,4},{2,7},{3,6},{4,1},{5,0},{6,3},{7,2},{8,13},{9,12},{10,... | collective-permute-start | bytes 2408456 | tf_op jit(solution)/shard_map/ppermute | solution.py:512
  39.6 120.2 %collective-permute-start.12 = (s16[1568,256]{1,0:T(8,128)(2,1)}, s16[1568,256]{1,0:T(8,128)(2,1)S(1)}, u32[]{:S(2)}, u32[]{:S(2)}) collective-permute-start(s16[1568,256]{1,0:T(8,128)(2,1)} %get-tuple-element.81), channel_id=1, source_target_pairs={{0,6},{1,7},{2,4},{3,5},{4,2},{5,3},{6,0},{7,1},{8,14},{9,15},{10,... | collective-permute-start | bytes 2408456 | tf_op jit(solution)/shard_map/ppermute | solution.py:512
  42.0 63.5 %collective-permute-start.2 = (s16[1168,256]{1,0:T(8,128)(2,1)S(1)}, s16[1168,256]{1,0:T(8,128)(2,1)S(1)}, u32[]{:S(2)}, u32[]{:S(2)}) collective-permute-start(s16[1168,256]{1,0:T(8,128)(2,1)S(1)} %copy-done.34), channel_id=1, source_target_pairs={{0,3},{1,2},{2,1},{3,0},{4,7},{5,6},{6,5},{7,4},{8,11},{9,10},{10,... | collective-permute-start | bytes 1794056 | tf_op jit(solution)/shard_map/ppermute | solution.py:512
  105.5 102.2 %copy-start.13 = (s16[1168,256]{1,0:T(8,128)(2,1)}, s16[1168,256]{1,0:T(8,128)(2,1)S(1)}, u32[]{:S(2)}) copy-start(s16[1168,256]{1,0:T(8,128)(2,1)S(1)} %collective-permute-done.2.refs_3_.refs_11_) | copy-start | bytes 1794052
  105.5 99.8 %collective-permute-start.13 = (s16[1568,256]{1,0:T(8,128)(2,1)}, s16[1568,256]{1,0:T(8,128)(2,1)S(1)}, u32[]{:S(2)}, u32[]{:S(2)}) collective-permute-start(s16[1568,256]{1,0:T(8,128)(2,1)} %get-tuple-element.82), channel_id=1, source_target_pairs={{0,7},{1,6},{2,5},{3,4},{4,3},{5,2},{6,1},{7,0},{8,15},{9,14},{10,... | collective-permute-start | bytes 2408456 | tf_op jit(solution)/shard_map/ppermute | solution.py:512
  124.1 87.5 %copy-start = (s16[1568,256]{1,0:T(8,128)(2,1)}, s16[1568,256]{1,0:T(8,128)(2,1)S(1)}, u32[]{:S(2)}) copy-start(s16[1568,256]{1,0:T(8,128)(2,1)S(1)} %collective-permute-done.10.refs_4_.refs_12_.refs_20_.refs_28_) | copy-start | bytes 2408452
  124.1 83.6 %collective-permute-start.7 = (s16[1568,256]{1,0:T(8,128)(2,1)}, s16[1568,256]{1,0:T(8,128)(2,1)S(1)}, u32[]{:S(2)}, u32[]{:S(2)}) collective-permute-start(s16[1568,256]{1,0:T(8,128)(2,1)} %get-tuple-element.76), channel_id=1, source_target_pairs={{0,1},{1,0},{2,3},{3,2},{4,5},{5,4},{6,7},{7,6},{8,9},{9,8},{10,11... | collective-permute-start | bytes 2408456 | tf_op jit(solution)/shard_map/ppermute | solution.py:512
  141.5 70.1 %copy-start.1 = (s16[1568,256]{1,0:T(8,128)(2,1)}, s16[1568,256]{1,0:T(8,128)(2,1)S(1)}, u32[]{:S(2)}) copy-start(s16[1568,256]{1,0:T(8,128)(2,1)S(1)} %collective-permute-done.11.refs_5_.refs_13_.refs_21_.refs_29_) | copy-start | bytes 2408452
  141.5 68.3 %collective-permute-start.8 = (s16[1568,256]{1,0:T(8,128)(2,1)}, s16[1568,256]{1,0:T(8,128)(2,1)}, u32[]{:S(2)}, u32[]{:S(2)}) collective-permute-start(s16[1568,256]{1,0:T(8,128)(2,1)} %get-tuple-element.77), channel_id=1, source_target_pairs={{0,2},{1,3},{2,0},{3,1},{4,6},{5,7},{6,4},{7,5},{8,10},{9,11},{10,... | collective-permute-start | bytes 2408456 | tf_op jit(solution)/shard_map/ppermute | solution.py:512
  159.8 51.3 %collective-permute-start.9 = (s16[1568,256]{1,0:T(8,128)(2,1)}, s16[1568,256]{1,0:T(8,128)(2,1)}, u32[]{:S(2)}, u32[]{:S(2)}) collective-permute-start(s16[1568,256]{1,0:T(8,128)(2,1)} %get-tuple-element.78), channel_id=1, source_target_pairs={{0,3},{1,2},{2,1},{3,0},{4,7},{5,6},{6,5},{7,4},{8,11},{9,10},{10,... | collective-permute-start | bytes 2408456 | tf_op jit(solution)/shard_map/ppermute | solution.py:512
  204.1 830.6 %collective-permute-start.50 = (f32[3,12,256,256]{3,2,1,0:T(8,128)}, f32[3,12,256,256]{3,2,1,0:T(8,128)}, u32[]{:S(2)}, u32[]{:S(2)}) collective-permute-start(f32[3,12,256,256]{3,2,1,0:T(8,128)} %collective-permute-done.49.refs_8_), channel_id=1, source_target_pairs={{16,0},{24,8},{0,16},{8,24},{17,1},{25,9},{1,17},{9,25},{18,2},{26... | collective-permute-start | bytes 28311560 | tf_op jit(solution)/shard_map/ppermute | solution.py:519
  205.4 67.0 %collective-permute-start.3 = (s16[1168,256]{1,0:T(8,128)(2,1)}, s16[1168,256]{1,0:T(8,128)(2,1)}, u32[]{:S(2)}, u32[]{:S(2)}) collective-permute-start(s16[1168,256]{1,0:T(8,128)(2,1)} %get-tuple-element.71), channel_id=1, source_target_pairs={{0,4},{1,5},{2,6},{3,7},{4,0},{5,1},{6,2},{7,3},{8,12},{9,13},{10,... | collective-permute-start | bytes 1794056 | tf_op jit(solution)/shard_map/ppermute | solution.py:512
  207.7 77.5 %collective-permute-start.4 = (s16[1168,256]{1,0:T(8,128)(2,1)}, s16[1168,256]{1,0:T(8,128)(2,1)}, u32[]{:S(2)}, u32[]{:S(2)}) collective-permute-start(s16[1168,256]{1,0:T(8,128)(2,1)} %get-tuple-element.72), channel_id=1, source_target_pairs={{0,5},{1,4},{2,7},{3,6},{4,1},{5,0},{6,3},{7,2},{8,13},{9,12},{10,... | collective-permute-start | bytes 1794056 | tf_op jit(solution)/shard_map/ppermute | solution.py:512
  209.8 88.2 %collective-permute-start.5 = (s16[1168,256]{1,0:T(8,128)(2,1)}, s16[1168,256]{1,0:T(8,128)(2,1)}, u32[]{:S(2)}, u32[]{:S(2)}) collective-permute-start(s16[1168,256]{1,0:T(8,128)(2,1)} %get-tuple-element.73), channel_id=1, source_target_pairs={{0,6},{1,7},{2,4},{3,5},{4,2},{5,3},{6,0},{7,1},{8,14},{9,15},{10,... | collective-permute-start | bytes 1794056 | tf_op jit(solution)/shard_map/ppermute | solution.py:512
  211.1 99.7 %collective-permute-start.6 = (s16[1168,256]{1,0:T(8,128)(2,1)}, s16[1168,256]{1,0:T(8,128)(2,1)}, u32[]{:S(2)}, u32[]{:S(2)}) collective-permute-start(s16[1168,256]{1,0:T(8,128)(2,1)} %get-tuple-element.74), channel_id=1, source_target_pairs={{0,7},{1,6},{2,5},{3,4},{4,3},{5,2},{6,1},{7,0},{8,15},{9,14},{10,... | collective-permute-start | bytes 1794056 | tf_op jit(solution)/shard_map/ppermute | solution.py:512
  360.5 4.0 collective-permute-start.14
  361.1 38.4 %collective-permute-start.15 = (s16[1168,256]{1,0:T(8,128)(2,1)}, s16[1168,256]{1,0:T(8,128)(2,1)S(1)}, u32[]{:S(2)}, u32[]{:S(2)}) collective-permute-start(s16[1168,256]{1,0:T(8,128)(2,1)} %get-tuple-element.88), channel_id=1, source_target_pairs={{0,2},{1,3},{2,0},{3,1},{4,6},{5,7},{6,4},{7,5},{8,10},{9,11},{10,... | collective-permute-start | bytes 1794056 | tf_op jit(solution)/shard_map/ppermute | solution.py:512
  361.1 51.2 %collective-permute-start.16 = (s16[1168,256]{1,0:T(8,128)(2,1)}, s16[1168,256]{1,0:T(8,128)(2,1)S(1)}, u32[]{:S(2)}, u32[]{:S(2)}) collective-permute-start(s16[1168,256]{1,0:T(8,128)(2,1)} %get-tuple-element.89), channel_id=1, source_target_pairs={{0,3},{1,2},{2,1},{3,0},{4,7},{5,6},{6,5},{7,4},{8,11},{9,10},{10,... | collective-permute-start | bytes 1794056 | tf_op jit(solution)/shard_map/ppermute | solution.py:512
  362.8 50.6 %collective-permute-start.17 = (s16[1168,256]{1,0:T(8,128)(2,1)}, s16[1168,256]{1,0:T(8,128)(2,1)S(1)}, u32[]{:S(2)}, u32[]{:S(2)}) collective-permute-start(s16[1168,256]{1,0:T(8,128)(2,1)} %get-tuple-element.90), channel_id=1, source_target_pairs={{0,4},{1,5},{2,6},{3,7},{4,0},{5,1},{6,2},{7,3},{8,12},{9,13},{10,... | collective-permute-start | bytes 1794056 | tf_op jit(solution)/shard_map/ppermute | solution.py:512
  364.5 104.5 %copy-start.26 = (s16[1168,256]{1,0:T(8,128)(2,1)}, s16[1168,256]{1,0:T(8,128)(2,1)S(1)}, u32[]{:S(2)}) copy-start(s16[1168,256]{1,0:T(8,128)(2,1)S(1)} %collective-permute-done.14.refs_1_) | copy-start | bytes 1794052
  364.5 77.0 %collective-permute-start.18 = (s16[1168,256]{1,0:T(8,128)(2,1)}, s16[1168,256]{1,0:T(8,128)(2,1)S(1)}, u32[]{:S(2)}, u32[]{:S(2)}) collective-permute-start(s16[1168,256]{1,0:T(8,128)(2,1)} %get-tuple-element.91), channel_id=1, source_target_pairs={{0,5},{1,4},{2,7},{3,6},{4,1},{5,0},{6,3},{7,2},{8,13},{9,12},{10,... | collective-permute-start | bytes 1794056 | tf_op jit(solution)/shard_map/ppermute | solution.py:512
  399.5 69.5 %copy-start.28 = (s16[1168,256]{1,0:T(8,128)(2,1)}, s16[1168,256]{1,0:T(8,128)(2,1)S(1)}, u32[]{:S(2)}) copy-start(s16[1168,256]{1,0:T(8,128)(2,1)S(1)} %collective-permute-done.15.refs_2_) | copy-start | bytes 1794052
  399.5 56.5 %collective-permute-start.19 = (s16[1168,256]{1,0:T(8,128)(2,1)}, s16[1168,256]{1,0:T(8,128)(2,1)S(1)}, u32[]{:S(2)}, u32[]{:S(2)}) collective-permute-start(s16[1168,256]{1,0:T(8,128)(2,1)} %get-tuple-element.92), channel_id=1, source_target_pairs={{0,6},{1,7},{2,4},{3,5},{4,2},{5,3},{6,0},{7,1},{8,14},{9,15},{10,... | collective-permute-start | bytes 1794056 | tf_op jit(solution)/shard_map/ppermute | solution.py:512
  412.3 56.6 %collective-permute-start.20 = (s16[1168,256]{1,0:T(8,128)(2,1)}, s16[1168,256]{1,0:T(8,128)(2,1)}, u32[]{:S(2)}, u32[]{:S(2)}) collective-permute-start(s16[1168,256]{1,0:T(8,128)(2,1)} %get-tuple-element.93), channel_id=1, source_target_pairs={{0,7},{1,6},{2,5},{3,4},{4,3},{5,2},{6,1},{7,0},{8,15},{9,14},{10,... | collective-permute-start | bytes 1794056 | tf_op jit(solution)/shard_map/ppermute | solution.py:512
  492.1 2.5 collective-permute-start.21
  492.5 38.0 %collective-permute-start.22 = (s16[1168,256]{1,0:T(8,128)(2,1)}, s16[1168,256]{1,0:T(8,128)(2,1)S(1)}, u32[]{:S(2)}, u32[]{:S(2)}) collective-permute-start(s16[1168,256]{1,0:T(8,128)(2,1)} %get-tuple-element.96), channel_id=1, source_target_pairs={{0,2},{1,3},{2,0},{3,1},{4,6},{5,7},{6,4},{7,5},{8,10},{9,11},{10,... | collective-permute-start | bytes 1794056 | tf_op jit(solution)/shard_map/ppermute | solution.py:512
  492.6 50.8 %collective-permute-start.23 = (s16[1168,256]{1,0:T(8,128)(2,1)}, s16[1168,256]{1,0:T(8,128)(2,1)S(1)}, u32[]{:S(2)}, u32[]{:S(2)}) collective-permute-start(s16[1168,256]{1,0:T(8,128)(2,1)} %get-tuple-element.97), channel_id=1, source_target_pairs={{0,3},{1,2},{2,1},{3,0},{4,7},{5,6},{6,5},{7,4},{8,11},{9,10},{10,... | collective-permute-start | bytes 1794056 | tf_op jit(solution)/shard_map/ppermute | solution.py:512
  494.3 50.4 %collective-permute-start.24 = (s16[1168,256]{1,0:T(8,128)(2,1)}, s16[1168,256]{1,0:T(8,128)(2,1)S(1)}, u32[]{:S(2)}, u32[]{:S(2)}) collective-permute-start(s16[1168,256]{1,0:T(8,128)(2,1)} %get-tuple-element.98), channel_id=1, source_target_pairs={{0,4},{1,5},{2,6},{3,7},{4,0},{5,1},{6,2},{7,3},{8,12},{9,13},{10,... | collective-permute-start | bytes 1794056 | tf_op jit(solution)/shard_map/ppermute | solution.py:512
  494.6 104.5 %copy-start.14 = (s16[1168,256]{1,0:T(8,128)(2,1)}, s16[1168,256]{1,0:T(8,128)(2,1)S(1)}, u32[]{:S(2)}) copy-start(s16[1168,256]{1,0:T(8,128)(2,1)S(1)} %collective-permute-done.21.refs_1_.refs_9_) | copy-start | bytes 1794052
  494.6 53.0 %collective-permute-start.25 = (s16[1168,256]{1,0:T(8,128)(2,1)}, s16[1168,256]{1,0:T(8,128)(2,1)S(1)}, u32[]{:S(2)}, u32[]{:S(2)}) collective-permute-start(s16[1168,256]{1,0:T(8,128)(2,1)} %get-tuple-element.99), channel_id=1, source_target_pairs={{0,5},{1,4},{2,7},{3,6},{4,1},{5,0},{6,3},{7,2},{8,13},{9,12},{10,... | collective-permute-start | bytes 1794056 | tf_op jit(solution)/shard_map/ppermute | solution.py:512
  530.6 55.1 %collective-permute-start.26 = (s16[1168,256]{1,0:T(8,128)(2,1)}, s16[1168,256]{1,0:T(8,128)(2,1)S(1)}, u32[]{:S(2)}, u32[]{:S(2)}) collective-permute-start(s16[1168,256]{1,0:T(8,128)(2,1)} %get-tuple-element.100), channel_id=1, source_target_pairs={{0,6},{1,7},{2,4},{3,5},{4,2},{5,3},{6,0},{7,1},{8,14},{9,15},{10,... | collective-permute-start | bytes 1794056 | tf_op jit(solution)/shard_map/ppermute | solution.py:512
  543.4 55.7 %collective-permute-start.27 = (s16[1168,256]{1,0:T(8,128)(2,1)}, s16[1168,256]{1,0:T(8,128)(2,1)}, u32[]{:S(2)}, u32[]{:S(2)}) collective-permute-start(s16[1168,256]{1,0:T(8,128)(2,1)} %get-tuple-element.101), channel_id=1, source_target_pairs={{0,7},{1,6},{2,5},{3,4},{4,3},{5,2},{6,1},{7,0},{8,15},{9,14},{10,... | collective-permute-start | bytes 1794056 | tf_op jit(solution)/shard_map/ppermute | solution.py:512
  649.1 2.5 collective-permute-start.28
  649.1 37.8 %collective-permute-start.29 = (s16[1168,256]{1,0:T(8,128)(2,1)}, s16[1168,256]{1,0:T(8,128)(2,1)S(1)}, u32[]{:S(2)}, u32[]{:S(2)}) collective-permute-start(s16[1168,256]{1,0:T(8,128)(2,1)} %get-tuple-element.106), channel_id=1, source_target_pairs={{0,2},{1,3},{2,0},{3,1},{4,6},{5,7},{6,4},{7,5},{8,10},{9,11},{10,... | collective-permute-start | bytes 1794056 | tf_op jit(solution)/shard_map/ppermute | solution.py:512
  649.2 50.6 %collective-permute-start.30 = (s16[1168,256]{1,0:T(8,128)(2,1)}, s16[1168,256]{1,0:T(8,128)(2,1)S(1)}, u32[]{:S(2)}, u32[]{:S(2)}) collective-permute-start(s16[1168,256]{1,0:T(8,128)(2,1)} %get-tuple-element.107), channel_id=1, source_target_pairs={{0,3},{1,2},{2,1},{3,0},{4,7},{5,6},{6,5},{7,4},{8,11},{9,10},{10,... | collective-permute-start | bytes 1794056 | tf_op jit(solution)/shard_map/ppermute | solution.py:512
  651.3 50.0 %collective-permute-start.31 = (s16[1168,256]{1,0:T(8,128)(2,1)}, s16[1168,256]{1,0:T(8,128)(2,1)S(1)}, u32[]{:S(2)}, u32[]{:S(2)}) collective-permute-start(s16[1168,256]{1,0:T(8,128)(2,1)} %get-tuple-element.108), channel_id=1, source_target_pairs={{0,4},{1,5},{2,6},{3,7},{4,0},{5,1},{6,2},{7,3},{8,12},{9,13},{10,... | collective-permute-start | bytes 1794056 | tf_op jit(solution)/shard_map/ppermute | solution.py:512
  651.6 104.5 %copy-start.25 = (s16[1168,256]{1,0:T(8,128)(2,1)}, s16[1168,256]{1,0:T(8,128)(2,1)S(1)}, u32[]{:S(2)}) copy-start(s16[1168,256]{1,0:T(8,128)(2,1)S(1)} %collective-permute-done.28.refs_1_) | copy-start | bytes 1794052
  651.6 53.0 %collective-permute-start.32 = (s16[1168,256]{1,0:T(8,128)(2,1)}, s16[1168,256]{1,0:T(8,128)(2,1)S(1)}, u32[]{:S(2)}, u32[]{:S(2)}) collective-permute-start(s16[1168,256]{1,0:T(8,128)(2,1)} %get-tuple-element.109), channel_id=1, source_target_pairs={{0,5},{1,4},{2,7},{3,6},{4,1},{5,0},{6,3},{7,2},{8,13},{9,12},{10,... | collective-permute-start | bytes 1794056 | tf_op jit(solution)/shard_map/ppermute | solution.py:512
  687.0 69.1 %copy-start.27 = (s16[1168,256]{1,0:T(8,128)(2,1)}, s16[1168,256]{1,0:T(8,128)(2,1)S(1)}, u32[]{:S(2)}) copy-start(s16[1168,256]{1,0:T(8,128)(2,1)S(1)} %collective-permute-done.29.refs_2_) | copy-start | bytes 1794052
  687.0 55.6 %collective-permute-start.33 = (s16[1168,256]{1,0:T(8,128)(2,1)}, s16[1168,256]{1,0:T(8,128)(2,1)S(1)}, u32[]{:S(2)}, u32[]{:S(2)}) collective-permute-start(s16[1168,256]{1,0:T(8,128)(2,1)} %get-tuple-element.110), channel_id=1, source_target_pairs={{0,6},{1,7},{2,4},{3,5},{4,2},{5,3},{6,0},{7,1},{8,14},{9,15},{10,... | collective-permute-start | bytes 1794056 | tf_op jit(solution)/shard_map/ppermute | solution.py:512
  699.8 56.3 %collective-permute-start.34 = (s16[1168,256]{1,0:T(8,128)(2,1)}, s16[1168,256]{1,0:T(8,128)(2,1)}, u32[]{:S(2)}, u32[]{:S(2)}) collective-permute-start(s16[1168,256]{1,0:T(8,128)(2,1)} %get-tuple-element.111), channel_id=1, source_target_pairs={{0,7},{1,6},{2,5},{3,4},{4,3},{5,2},{6,1},{7,0},{8,15},{9,14},{10,... | collective-permute-start | bytes 1794056 | tf_op jit(solution)/shard_map/ppermute | solution.py:512
  779.3 2.5 collective-permute-start.35
  779.4 37.8 %collective-permute-start.36 = (s16[1168,256]{1,0:T(8,128)(2,1)}, s16[1168,256]{1,0:T(8,128)(2,1)S(1)}, u32[]{:S(2)}, u32[]{:S(2)}) collective-permute-start(s16[1168,256]{1,0:T(8,128)(2,1)} %get-tuple-element.114), channel_id=1, source_target_pairs={{0,2},{1,3},{2,0},{3,1},{4,6},{5,7},{6,4},{7,5},{8,10},{9,11},{10,... | collective-permute-start | bytes 1794056 | tf_op jit(solution)/shard_map/ppermute | solution.py:512
  779.5 50.6 %collective-permute-start.37 = (s16[1168,256]{1,0:T(8,128)(2,1)}, s16[1168,256]{1,0:T(8,128)(2,1)S(1)}, u32[]{:S(2)}, u32[]{:S(2)}) collective-permute-start(s16[1168,256]{1,0:T(8,128)(2,1)} %get-tuple-element.115), channel_id=1, source_target_pairs={{0,3},{1,2},{2,1},{3,0},{4,7},{5,6},{6,5},{7,4},{8,11},{9,10},{10,... | collective-permute-start | bytes 1794056 | tf_op jit(solution)/shard_map/ppermute | solution.py:512
  781.5 50.0 %collective-permute-start.38 = (s16[1168,256]{1,0:T(8,128)(2,1)}, s16[1168,256]{1,0:T(8,128)(2,1)S(1)}, u32[]{:S(2)}, u32[]{:S(2)}) collective-permute-start(s16[1168,256]{1,0:T(8,128)(2,1)} %get-tuple-element.116), channel_id=1, source_target_pairs={{0,4},{1,5},{2,6},{3,7},{4,0},{5,1},{6,2},{7,3},{8,12},{9,13},{10,... | collective-permute-start | bytes 1794056 | tf_op jit(solution)/shard_map/ppermute | solution.py:512
  781.8 104.5 %copy-start.5 = (s16[1168,256]{1,0:T(8,128)(2,1)}, s16[1168,256]{1,0:T(8,128)(2,1)S(1)}, u32[]{:S(2)}) copy-start(s16[1168,256]{1,0:T(8,128)(2,1)S(1)} %collective-permute-done.35.refs_1_.refs_9_) | copy-start | bytes 1794052
  781.8 53.0 %collective-permute-start.39 = (s16[1168,256]{1,0:T(8,128)(2,1)}, s16[1168,256]{1,0:T(8,128)(2,1)S(1)}, u32[]{:S(2)}, u32[]{:S(2)}) collective-permute-start(s16[1168,256]{1,0:T(8,128)(2,1)} %get-tuple-element.117), channel_id=1, source_target_pairs={{0,5},{1,4},{2,7},{3,6},{4,1},{5,0},{6,3},{7,2},{8,13},{9,12},{10,... | collective-permute-start | bytes 1794056 | tf_op jit(solution)/shard_map/ppermute | solution.py:512
  817.2 69.1 %copy-start.6 = (s16[1168,256]{1,0:T(8,128)(2,1)}, s16[1168,256]{1,0:T(8,128)(2,1)S(1)}, u32[]{:S(2)}) copy-start(s16[1168,256]{1,0:T(8,128)(2,1)S(1)} %collective-permute-done.36.refs_2_.refs_10_) | copy-start | bytes 1794052
  817.2 55.6 %collective-permute-start.40 = (s16[1168,256]{1,0:T(8,128)(2,1)}, s16[1168,256]{1,0:T(8,128)(2,1)S(1)}, u32[]{:S(2)}, u32[]{:S(2)}) collective-permute-start(s16[1168,256]{1,0:T(8,128)(2,1)} %get-tuple-element.118), channel_id=1, source_target_pairs={{0,6},{1,7},{2,4},{3,5},{4,2},{5,3},{6,0},{7,1},{8,14},{9,15},{10,... | collective-permute-start | bytes 1794056 | tf_op jit(solution)/shard_map/ppermute | solution.py:512
  830.0 56.3 %collective-permute-start.41 = (s16[1168,256]{1,0:T(8,128)(2,1)}, s16[1168,256]{1,0:T(8,128)(2,1)}, u32[]{:S(2)}, u32[]{:S(2)}) collective-permute-start(s16[1168,256]{1,0:T(8,128)(2,1)} %get-tuple-element.119), channel_id=1, source_target_pairs={{0,7},{1,6},{2,5},{3,4},{4,3},{5,2},{6,1},{7,0},{8,15},{9,14},{10,... | collective-permute-start | bytes 1794056 | tf_op jit(solution)/shard_map/ppermute | solution.py:512
  886.3 93.6 %copy-start.38 = (s32[4]{0:T(128)S(1)}, s32[4]{0:T(128)}, u32[]{:S(2)}) copy-start(s32[4]{0:T(128)} %param.14) | copy-start | bytes 52
  927.7 2.5 collective-permute-start.42
  927.8 37.8 %collective-permute-start.43 = (s16[1168,256]{1,0:T(8,128)(2,1)}, s16[1168,256]{1,0:T(8,128)(2,1)S(1)}, u32[]{:S(2)}, u32[]{:S(2)}) collective-permute-start(s16[1168,256]{1,0:T(8,128)(2,1)} %get-tuple-element.123), channel_id=1, source_target_pairs={{0,2},{1,3},{2,0},{3,1},{4,6},{5,7},{6,4},{7,5},{8,10},{9,11},{10,... | collective-permute-start | bytes 1794056 | tf_op jit(solution)/shard_map/ppermute | solution.py:512
  927.9 50.6 %collective-permute-start.44 = (s16[1168,256]{1,0:T(8,128)(2,1)}, s16[1168,256]{1,0:T(8,128)(2,1)S(1)}, u32[]{:S(2)}, u32[]{:S(2)}) collective-permute-start(s16[1168,256]{1,0:T(8,128)(2,1)} %get-tuple-element.124), channel_id=1, source_target_pairs={{0,3},{1,2},{2,1},{3,0},{4,7},{5,6},{6,5},{7,4},{8,11},{9,10},{10,... | collective-permute-start | bytes 1794056 | tf_op jit(solution)/shard_map/ppermute | solution.py:512
  930.0 52.0 %collective-permute-start.45 = (s16[1168,256]{1,0:T(8,128)(2,1)}, s16[1168,256]{1,0:T(8,128)(2,1)S(1)}, u32[]{:S(2)}, u32[]{:S(2)}) collective-permute-start(s16[1168,256]{1,0:T(8,128)(2,1)} %get-tuple-element.125), channel_id=1, source_target_pairs={{0,4},{1,5},{2,6},{3,7},{4,0},{5,1},{6,2},{7,3},{8,12},{9,13},{10,... | collective-permute-start | bytes 1794056 | tf_op jit(solution)/shard_map/ppermute | solution.py:512
  930.2 104.5 %copy-start.20 = (s16[1168,256]{1,0:T(8,128)(2,1)}, s16[1168,256]{1,0:T(8,128)(2,1)S(1)}, u32[]{:S(2)}) copy-start(s16[1168,256]{1,0:T(8,128)(2,1)S(1)} %collective-permute-done.42.refs_1_) | copy-start | bytes 1794052
  930.2 53.0 %collective-permute-start.46 = (s16[1168,256]{1,0:T(8,128)(2,1)}, s16[1168,256]{1,0:T(8,128)(2,1)S(1)}, u32[]{:S(2)}, u32[]{:S(2)}) collective-permute-start(s16[1168,256]{1,0:T(8,128)(2,1)} %get-tuple-element.126), channel_id=1, source_target_pairs={{0,5},{1,4},{2,7},{3,6},{4,1},{5,0},{6,3},{7,2},{8,13},{9,12},{10,... | collective-permute-start | bytes 1794056 | tf_op jit(solution)/shard_map/ppermute | solution.py:512
  965.7 69.1 %copy-start.21 = (s16[1168,256]{1,0:T(8,128)(2,1)}, s16[1168,256]{1,0:T(8,128)(2,1)S(1)}, u32[]{:S(2)}) copy-start(s16[1168,256]{1,0:T(8,128)(2,1)S(1)} %collective-permute-done.43.refs_2_) | copy-start | bytes 1794052
  965.7 55.7 %collective-permute-start.47 = (s16[1168,256]{1,0:T(8,128)(2,1)}, s16[1168,256]{1,0:T(8,128)(2,1)}, u32[]{:S(2)}, u32[]{:S(2)}) collective-permute-start(s16[1168,256]{1,0:T(8,128)(2,1)} %get-tuple-element.127), channel_id=1, source_target_pairs={{0,6},{1,7},{2,4},{3,5},{4,2},{5,3},{6,0},{7,1},{8,14},{9,15},{10,... | collective-permute-start | bytes 1794056 | tf_op jit(solution)/shard_map/ppermute | solution.py:512
  978.5 56.3 %collective-permute-start.48 = (s16[1168,256]{1,0:T(8,128)(2,1)}, s16[1168,256]{1,0:T(8,128)(2,1)}, u32[]{:S(2)}, u32[]{:S(2)}) collective-permute-start(s16[1168,256]{1,0:T(8,128)(2,1)} %get-tuple-element.128), channel_id=1, source_target_pairs={{0,7},{1,6},{2,5},{3,4},{4,3},{5,2},{6,1},{7,0},{8,15},{9,14},{10,... | collective-permute-start | bytes 1794056 | tf_op jit(solution)/shard_map/ppermute | solution.py:512
  (26 other events, 1054.2 us)

commit v2 on v1

v2 whole, which is shorter than its diff:
```python
import functools

import numpy as np
import jax
import jax.numpy as jnp
from jax import lax
from jax.experimental import pallas as pl
from jax.experimental.pallas import tpu as pltpu
from jax.sharding import PartitionSpec as P

TIME_STEP = 0.05
GAMMAS = (8.0 / 15.0, 5.0 / 12.0, 3.0 / 4.0)
ZETAS = (0.0, -17.0 / 60.0, -5.0 / 12.0)
SECTIONS = 3
WHOLE = (True, False)
GROUPS = ((0,), (1, 2))
TOP = 32767.0
STEPS_PER_OCTAVE = 64.0
F32 = jnp.float32
BF16 = jnp.bfloat16
VMEM_LIMIT = 60 * 1024 * 1024


def spectral_table(points):
    offset = np.arange(points)[:, None] - np.arange(points)[None, :]
    away = np.where(offset == 0, 1, offset)
    table = 0.5 * (1 - 2 * (offset % 2)) / np.tan(np.pi * away / points)
    return np.where(offset == 0, 0.0, table).astype(np.float32)


def halves(table):
    high = table.astype(jnp.bfloat16)
    low = (table - high.astype(np.float32)).astype(jnp.bfloat16)
    return np.asarray(high), np.asarray(low)


def split(value):
    high = value.astype(BF16)
    return high, (value - high.astype(F32)).astype(BF16)


def dot(left, right):
    return jnp.dot(left, right, preferred_element_type=F32)


def aligned(value, multiple):
    return value if isinstance(value, int) else pl.multiple_of(value, multiple)


def partner(whole, me, d):
    return d if whole else me ^ d


class Plan:
    def __init__(self, rows, nx, nz, parts):
        self.rows, self.nx, self.nz, self.parts = rows, nx, nz, parts
        self.cuts = 1 if nx // parts >= 16 else 2
        self.width = nx * self.cuts // parts
        self.depth = nz // self.cuts
        self.lines = rows * parts
        self.scale_rows = -(-rows // 16) * 16
        early = max(rows // 3, 1)
        self.spans = ((0, early), (early, rows - early))

    def rows_of(self, fields, rows=None):
        return fields * (rows or self.rows) * self.width

    def piece(self, number):
        along = aligned(number // self.cuts * self.width, self.width)
        if self.cuts == 1:
            return pl.ds(along, self.width), pl.ds(0, self.depth)
        across = aligned(number % self.cuts * self.depth, self.depth)
        return pl.ds(along, self.width), pl.ds(across, self.depth)


def scale_code(largest):
    return jnp.floor(jnp.log2(jnp.maximum(largest, 1e-35)) * STEPS_PER_OCTAVE) + 2.0


def encode(code):
    return TOP * jnp.exp2(code * (-1.0 / STEPS_PER_OCTAVE))


def decode(code):
    return (1.0 / TOP) * jnp.exp2(code * (1.0 / STEPS_PER_OCTAVE))


def to_short(value):
    return jnp.round(value).astype(jnp.int32).astype(jnp.int16)


def from_short(value):
    return value.astype(jnp.int32).astype(F32)


def column_max(values):
    return functools.reduce(
        jnp.maximum, [jnp.max(jnp.abs(v), axis=0, keepdims=True) for v in values]
    )


def pack_kernel(plan, tangent_ref, flow_ref, out_ref, codes):
    row = pl.program_id(0)
    for d in range(plan.parts):
        along, across = plan.piece(d)
        values = [tangent_ref[c, 0, along, across] for c in range(3)]
        values.append(flow_ref[0, 0, along, across].astype(F32))
        for first, group in ((0, values[:3]), (3, values[3:])):
            code = scale_code(column_max(group))
            factor = encode(code)
            for k, value in enumerate(group):
                start = pl.multiple_of(((first + k) * plan.rows + row) * plan.width, plan.width)
                out_ref[d, pl.ds(start, plan.width), :] = to_short(value * factor)
            base = 0 if first == 0 else plan.scale_rows
            codes[d, pl.ds(base + row, 1), :] = code

    @pl.when(row == plan.rows - 1)
    def _():
        for d in range(plan.parts):
            out_ref[d, plan.rows_of(4) :, :] = codes[d].astype(jnp.int32).astype(jnp.int16)


def pack_start(plan, tangent, flow):
    shape = (plan.parts, plan.rows_of(4) + 2 * plan.scale_rows, plan.depth)
    return pl.pallas_call(
        functools.partial(pack_kernel, plan),
        grid=(plan.rows,),
        in_specs=[
            pl.BlockSpec((3, 1, plan.nx, plan.nz), lambda j: (0, j, 0, 0)),
            pl.BlockSpec((1, 1, plan.nx, plan.nz), lambda j: (1, j, 0, 0)),
        ],
        out_specs=pl.BlockSpec(shape, lambda j: (0, 0, 0)),
        scratch_shapes=[pltpu.VMEM((plan.parts, 2 * plan.scale_rows, plan.depth), F32)],
        out_shape=jax.ShapeDtypeStruct(shape, jnp.int16),
        compiler_params=pltpu.CompilerParams(vmem_limit_bytes=VMEM_LIMIT),
        cost_estimate=pl.CostEstimate(flops=0, transcendentals=0, bytes_accessed=20_000_000),
        name="pack_start",
    )(tangent, flow)


def pieces(plan, whole):
    return 1 if whole else plan.parts


def each(plan, whole, refs):
    return [refs[0].at[d] for d in range(plan.parts)] if whole else list(refs)


def block_specs(plan, whole, rows, depth, index, **more):
    if whole:
        return [pl.BlockSpec((plan.parts, rows, depth), lambda i, *_: (0, index(i), 0), **more)]
    return [pl.BlockSpec((rows, depth), lambda i, *_: (index(i), 0), **more)] * plan.parts


def block_shapes(plan, whole, rows):
    shape = (plan.parts, rows, plan.depth) if whole else (rows, plan.depth)
    return [jax.ShapeDtypeStruct(shape, jnp.int16)] * pieces(plan, whole)


def flat(groups):
    return [block for blocks in groups for block in blocks]


def grouped(plan, refs):
    lists = []
    for whole in WHOLE:
        count = pieces(plan, whole)
        lists.append(refs[:count])
        refs = refs[count:]
    return lists, refs


def receive(plan, me, row, sources, scales, speed):
    for whole, group, blocks, factors in zip(WHOLE, GROUPS, sources, scales):
        for d in range(plan.parts):
            along, across = plan.piece(partner(whole, me, d))
            for k, c in enumerate(group):
                start = pl.multiple_of((k * plan.rows + row) * plan.width, plan.width)
                value = from_short(blocks[d][pl.ds(start, plan.width), :])
                speed[c, along, across] = value * factors[d, k : k + 1, :]


def prepare(plan, sources, scales):
    for group, blocks, factors in zip(GROUPS, sources, scales):
        for d in range(plan.parts):
            factors[d] = decode(from_short(blocks[d][plan.rows_of(len(group)) :, :]))


def blockwise(plan, refs):
    lists, rest = grouped(plan, refs)
    return [each(plan, whole, blocks) for whole, blocks in zip(WHOLE, lists)], rest


def explicit_kernel(plan, which, received, me_ref, *refs):
    parts, nx = plan.parts, plan.nx
    if received:
        sources, refs = blockwise(plan, refs)
    else:
        tangent_ref, refs = refs[0], refs[1:]
    flow_ref, shear_ref, dx_ref, dz_ref = refs[:4]
    refs = refs[4:]
    if received:
        base_dx_ref, base_dz_ref, refs = refs[0], refs[1], refs[2:]
    whole, (above, rows) = WHOLE[which], plan.spans[which]
    count = pieces(plan, whole)
    outs, refs = each(plan, whole, refs[:count]), refs[count:]
    if not received:
        base_dx_ref, base_dz_ref, refs = refs[0], refs[1], refs[2:]
    speed, term, codes = refs[:3]
    scales = refs[3:]
    row = pl.program_id(0)
    me = me_ref[0]
    if received:

        @pl.when(row == 0)
        def _():
            prepare(plan, sources, scales)

        receive(plan, me, above + row, sources, scales, speed)
    else:
        for c in range(3):
            speed[c] = tangent_ref[c, 0]
    for c in range(3):
        if not received:
            flow = flow_ref[c, 0]
            both = dot(dx_ref[...], flow)
            base_dx_ref[c, 0] = both[:nx] + both[nx:]
            base_dz_ref[c, 0] = dot(flow, dz_ref[0]) + dot(flow, dz_ref[1])
        high, low = split(speed[c])
        both = dot(dx_ref[...], high)
        along_x = both[:nx] + both[nx:] + dot(dx_ref[:nx, :], low)
        along_z = dot(high, dz_ref[0]) + (dot(low, dz_ref[0]) + dot(high, dz_ref[1]))
        carried = flow_ref[0, 0].astype(F32) * along_x + flow_ref[2, 0].astype(F32) * along_z
        sheared = (
            speed[0] * base_dx_ref[c, 0]
            + speed[1] * shear_ref[c, 0].astype(F32)
            + speed[2] * base_dz_ref[c, 0]
        )
        term[c] = -(carried + sheared)
    for d in range(parts):
        along, across = plan.piece(partner(whole, me, d))
        values = [term[c, along, across] for c in range(3)]
        code = scale_code(column_max(values))
        factor = encode(code)
        for c, value in enumerate(values):
            start = pl.multiple_of((c * rows + row) * plan.width, plan.width)
            outs[d][pl.ds(start, plan.width), :] = to_short(value * factor)
        codes[d, pl.ds(row, 1), :] = code

    @pl.when(row == rows - 1)
    def _():
        for d in range(parts):
            outs[d][plan.rows_of(3, rows) :, :] = codes[d].astype(jnp.int32).astype(jnp.int16)


def whole_blocks(plan):
    specs = []
    for whole, group in zip(WHOLE, GROUPS):
        height = plan.rows_of(len(group)) + 16
        once = dict(pipeline_mode=pl.Buffered(1))
        specs += block_specs(plan, whole, height, plan.depth, lambda j: 0, **once)
    return specs


def explicit(plan, which, me, velocity, flow, shear, dx, dz, bases=None):
    received = bases is not None
    parts = plan.parts
    whole, (above, rows) = WHOLE[which], plan.spans[which]
    height = plan.rows_of(3, rows) + plan.scale_rows
    block = (3, 1, plan.nx, plan.nz)
    field = pl.BlockSpec(block, lambda j, *_: (0, above + j, 0, 0))
    own = pl.BlockSpec(block, lambda j, *_: (0, j, 0, 0))
    scratch = [
        pltpu.VMEM((3, plan.nx, plan.nz), F32),
        pltpu.VMEM((3, plan.nx, plan.nz), F32),
        pltpu.VMEM((parts, plan.scale_rows, plan.depth), F32),
    ]
    out_specs = block_specs(plan, whole, height, plan.depth, lambda j: 0)
    out_shape = block_shapes(plan, whole, height)
    if received:
        first, more = whole_blocks(plan), [own, own]
        velocity = flat(velocity)
        scratch += [pltpu.VMEM((parts, 16, plan.depth), F32)] * len(GROUPS)
    else:
        first, velocity, bases, more = [field], [velocity], [], []
        out_specs += [own, own]
        out_shape += [jax.ShapeDtypeStruct((3, rows, plan.nx, plan.nz), F32)] * 2
    results = pl.pallas_call(
        functools.partial(explicit_kernel, plan, which, received),
        grid_spec=pltpu.PrefetchScalarGridSpec(
            num_scalar_prefetch=1,
            grid=(rows,),
            in_specs=first
            + [
                field,
                field,
                pl.BlockSpec(dx.shape, lambda j, *_: (0, 0)),
                pl.BlockSpec(dz.shape, lambda j, *_: (0, 0, 0)),
            ]
            + more,
            out_specs=out_specs,
            scratch_shapes=scratch,
        ),
        out_shape=out_shape,
        compiler_params=pltpu.CompilerParams(vmem_limit_bytes=VMEM_LIMIT),
        cost_estimate=pl.CostEstimate(
            flops=1_000_000_000 * rows, transcendentals=0, bytes_accessed=4_000_000 * rows
        ),
        name="explicit",
    )(me, *velocity, flow, shear, dx, dz, *bases)
    count = pieces(plan, whole)
    return exchange(plan, whole, results[:count]), results[count:]


def stacked(matrices):
    rows = []
    for matrix in matrices:
        high, low = split(matrix)
        rows.append(jnp.concatenate([high, high], axis=1))
        rows.append(jnp.concatenate([low, jnp.zeros_like(low)], axis=1))
    return jnp.concatenate(rows, axis=0)


def precise_dot(left, right):
    high, low = split(left)
    right_high, right_low = split(right)
    return dot(high, right_high) + (dot(low, right_high) + dot(high, right_low))


def put(field, rows, value):
    for half in range(field.shape[0]):
        field[half, rows, :] = value[:, half * 128 : half * 128 + 128]


def get(field, rows):
    return jnp.concatenate([field[half, rows, :] for half in range(field.shape[0])], axis=1)


def unpack_lines(plan, whole, me, span, sources, scales, field):
    above, rows = span
    for d, (source, scale) in enumerate(zip(sources, scales)):
        scale = decode(from_short(scale[...]))
        first = aligned(partner(whole, me, d) * plan.rows_of(1), plan.width)
        for j in range(rows):
            value = from_short(source[j * plan.width : (j + 1) * plan.width, :])
            here = pl.ds(first + (above + j) * plan.width, plan.width)
            put(field, here, value * scale[j : j + 1, :])


def first_lines_kernel(plan, *refs):
    lines = plan.lines
    values, scales, flows, flow_scales = (each(plan, True, refs[i : i + 1]) for i in range(4))
    wall_ref, right_ref, turned_ref, flow_ref, field, table = refs[4:]

    @pl.when(pl.program_id(0) == 0)
    def _():
        table[...] = stacked([wall_ref[...]])
        unpack_lines(plan, True, None, (0, plan.rows), flows, flow_scales, field)

        def turn(r, carry):
            flow_ref[r] = get(field, pl.ds(r, lines, stride=plan.width))
            return carry

        lax.fori_loop(0, plan.width, turn, 0)

    unpack_lines(plan, True, None, (0, plan.rows), values, scales, field)

    def line(r, carry):
        value = get(field, pl.ds(r, lines, stride=plan.width))
        product = dot(table[...], jnp.concatenate(split(value), axis=0))
        turned = -(flow_ref[r] * (product[:lines] + product[lines:]))
        turned_ref[0, r] = turned
        right_ref[0, r] = value + (TIME_STEP * GAMMAS[0]) * turned
        return carry

    lax.fori_loop(0, plan.width, line, 0, unroll=4)


def first_lines(plan, blocks, wall):
    lines, width, depth = plan.lines, plan.width, plan.depth
    at = plan.rows_of(4) // plan.scale_rows
    rows, codes = plan.rows_of(1), plan.scale_rows
    state = jax.ShapeDtypeStruct((3, width, lines, depth), F32)
    state_spec = pl.BlockSpec((1, width, lines, depth), lambda c: (c, 0, 0, 0))
    return pl.pallas_call(
        functools.partial(first_lines_kernel, plan),
        grid=(3,),
        in_specs=block_specs(plan, True, rows, depth, lambda c: c)
        + block_specs(plan, True, codes, depth, lambda c: at)
        + block_specs(plan, True, rows, depth, lambda c: 3)
        + block_specs(plan, True, codes, depth, lambda c: at + 1)
        + [pl.BlockSpec(wall.shape, lambda c: (0, 0))],
        out_specs=[
            state_spec,
            state_spec,
            pl.BlockSpec((width, lines, depth), lambda c: (0, 0, 0)),
        ],
        scratch_shapes=[
            pltpu.VMEM((depth // 128, lines * width, 128), F32),
            pltpu.VMEM((2 * lines, 2 * lines), BF16),
        ],
        out_shape=[state, state, jax.ShapeDtypeStruct((width, lines, depth), F32)],
        compiler_params=pltpu.CompilerParams(vmem_limit_bytes=VMEM_LIMIT),
        cost_estimate=pl.CostEstimate(
            flops=1_000_000_000, transcendentals=0, bytes_accessed=30_000_000
        ),
        name="first_lines",
    )(blocks, blocks, blocks, blocks, wall)


def lines_kernel(plan, section, group, whole, me_ref, *refs):
    parts, lines = plan.parts, plan.lines
    last = section == SECTIONS - 1
    count = pieces(plan, whole)
    values, refs = blockwise(plan, refs)
    scales, refs = blockwise(plan, refs)
    if last:
        wall_ref, solve_ref, right_ref = refs[:3]
        outs, (field, table, codes) = refs[3 : 3 + count], refs[3 + count :]
    else:
        wall_ref, solve_ref, right_ref, turned_ref, flow_ref = refs[:5]
        outs, refs = refs[5 : 5 + count], refs[5 + count :]
        right_out, turned_out, field, table, codes = refs
    outs = each(plan, whole, outs)
    me = me_ref[0]
    component = pl.program_id(0)

    @pl.when(component == 0)
    def _():
        solve = solve_ref[0]
        tables = [solve] if last else [solve, precise_dot(wall_ref[...], solve)]
        table[...] = stacked(tables)
        codes[...] = jnp.zeros_like(codes)

    for g in range(len(WHOLE)):
        unpack_lines(plan, WHOLE[g], me, plan.spans[g], values[g], scales[g], field)

    def line(r, carry):
        here = pl.ds(r, lines, stride=plan.width)
        term = get(field, here)
        right = right_ref[0, r] + (TIME_STEP * GAMMAS[section]) * term
        product = dot(table[...], jnp.concatenate(split(right), axis=0))
        value = product[:lines] + product[lines : 2 * lines]
        put(field, here, value)
        if not last:
            slope = product[2 * lines : 3 * lines] + product[3 * lines :]
            turned = -(flow_ref[r] * slope)
            past = term + turned_ref[0, r]
            turned_out[0, r] = turned
            right_out[0, r] = (
                value
                + (TIME_STEP * ZETAS[section + 1]) * past
                + (TIME_STEP * GAMMAS[section + 1]) * turned
            )
        return carry

    lax.fori_loop(0, plan.width, line, 0, unroll=4)

    for d in range(parts):
        first = aligned(partner(whole, me, d) * plan.rows_of(1), plan.width)
        chunk = [
            get(field, pl.ds(first + j * plan.width, plan.width)) for j in range(plan.rows)
        ]
        code = scale_code(column_max(chunk))
        factor = encode(code)
        for j in range(plan.rows):
            start = pl.multiple_of((component * plan.rows + j) * plan.width, plan.width)
            outs[d][pl.ds(start, plan.width), :] = to_short(chunk[j] * factor)
        codes[d, pl.ds(component, 1), :] = code

    @pl.when(component == len(group) - 1)
    def _():
        for d in range(parts):
            outs[d][plan.rows_of(len(group)) :, :] = codes[d].astype(jnp.int32).astype(jnp.int16)


def advance_lines(plan, section, group, whole, me, blocks, wall, solves, right, turned, flow):
    lines, width, depth = plan.lines, plan.width, plan.depth
    last = section == SECTIONS - 1
    height = plan.rows_of(len(group)) + 16
    skip = group[0] if right.shape[0] == 3 else 0
    value_specs, scale_specs = [], []
    for kind, (_, rows) in zip(WHOLE, plan.spans):
        at = plan.rows_of(3, rows) // plan.scale_rows
        value_specs += block_specs(plan, kind, plan.rows_of(1, rows), depth, lambda c: c + group[0])
        scale_specs += block_specs(plan, kind, plan.scale_rows, depth, lambda c, at=at: at)
    state_spec = pl.BlockSpec((1, width, lines, depth), lambda c, *_: (c, 0, 0, 0))
    read_spec = pl.BlockSpec((1, width, lines, depth), lambda c, *_: (c + skip, 0, 0, 0))
    in_specs = (
        value_specs
        + scale_specs
        + [
            pl.BlockSpec(wall.shape, lambda c, *_: (0, 0)),
            pl.BlockSpec((1, lines, lines), lambda c, *_: (section, 0, 0)),
            read_spec,
        ]
    )
    args = [me, *flat(blocks), *flat(blocks), wall, solves, right]
    out_specs = block_specs(plan, whole, height, depth, lambda c: 0)
    out_shape = block_shapes(plan, whole, height)
    copies = 2
    if not last:
        in_specs += [
            read_spec,
            pl.BlockSpec(flow.shape, lambda c, *_: (0, 0, 0), pipeline_mode=pl.Buffered(1)),
        ]
        args += [turned, flow]
        out_specs = out_specs + [state_spec, state_spec]
        state = jax.ShapeDtypeStruct((len(group), width, lines, depth), F32)
        out_shape = out_shape + [state, state]
        copies = 4
    results = pl.pallas_call(
        functools.partial(lines_kernel, plan, section, group, whole),
        grid_spec=pltpu.PrefetchScalarGridSpec(
            num_scalar_prefetch=1,
            grid=(len(group),),
            in_specs=in_specs,
            out_specs=out_specs,
            scratch_shapes=[
                pltpu.VMEM((depth // 128, lines * width, 128), F32),
                pltpu.VMEM((copies * lines, 2 * lines), BF16),
                pltpu.VMEM((plan.parts, 16, depth), F32),
            ],
        ),
        out_shape=out_shape,
        compiler_params=pltpu.CompilerParams(vmem_limit_bytes=VMEM_LIMIT),
        cost_estimate=pl.CostEstimate(
            flops=700_000_000 * len(group),
            transcendentals=0,
            bytes_accessed=17_000_000 * len(group),
        ),
        name="advance_lines",
    )(*args)
    count = pieces(plan, whole)
    return results[:count], results[count:]


def result_kernel(plan, me_ref, shift_ref, successor_ref, *refs):
    sources, refs = blockwise(plan, refs)
    follower_ref, out_ref, speed = refs[:3]
    scales = refs[3:]
    row = pl.program_id(0)

    @pl.when(row == 0)
    def _():
        prepare(plan, sources, scales)

    receive(plan, me_ref[0], row, sources, scales, speed)
    for c in range(3):
        out_ref[c, 0] = pltpu.roll(speed[c], shift_ref[0], axis=1) - follower_ref[0, c, 0]


def result(plan, me, shift, successor, blocks, tangents):
    parts = plan.parts
    block = (3, 1, plan.nx, plan.nz)
    return pl.pallas_call(
        functools.partial(result_kernel, plan),
        grid_spec=pltpu.PrefetchScalarGridSpec(
            num_scalar_prefetch=3,
            grid=(plan.rows,),
            in_specs=whole_blocks(plan)
            + [
                pl.BlockSpec(
                    (1, *block), lambda j, me, shift, successor: (successor[0], 0, j, 0, 0)
                )
            ],
            out_specs=pl.BlockSpec(block, lambda j, *_: (0, j, 0, 0)),
            scratch_shapes=[pltpu.VMEM((3, plan.nx, plan.nz), F32)]
            + [pltpu.VMEM((parts, 16, plan.depth), F32)] * len(GROUPS),
        ),
        out_shape=jax.ShapeDtypeStruct((3, plan.rows, plan.nx, plan.nz), F32),
        compiler_params=pltpu.CompilerParams(vmem_limit_bytes=VMEM_LIMIT),
        cost_estimate=pl.CostEstimate(flops=0, transcendentals=0, bytes_accessed=25_000_000),
        name="result",
    )(me, shift, successor, *flat(blocks), tangents)


def exchange(plan, whole, blocks):
    if whole:
        return [lax.all_to_all(blocks[0], "grid", split_axis=0, concat_axis=0, tiled=True)]
    parts = plan.parts
    moved = list(blocks)
    half = parts // 2
    order = [half // 2, *range(half, parts)] + [d for d in range(1, half) if d != half // 2][::-1]
    for d in order:
        moved[d] = lax.ppermute(blocks[d], "grid", [(i, i ^ d) for i in range(parts)])
    return moved


def shards(
    tangent, base_flow, base_shear, wall_derivative, implicit_inverse, successor, spanwise_shift
):
    tangent, flow, shear = tangent[0], base_flow[0], base_shear[0]
    _, rows, nx, nz = tangent.shape
    plan = Plan(rows, nx, nz, lax.axis_size("grid"))
    me = lax.axis_index("grid").astype(jnp.int32).reshape(1)
    ahead = lax.dynamic_slice_in_dim(successor, lax.axis_index("seg"), 1)
    dx = jnp.asarray(np.concatenate(halves(spectral_table(nx)), axis=0))
    dz = jnp.asarray(np.stack(halves(spectral_table(nz).T)))

    start = pack_start(plan, tangent, flow)
    later, start, following = lax.optimization_barrier((me, start, tangent))
    tangents = lax.all_gather(following, "seg")
    (start,) = exchange(plan, True, [start])
    term, bases = zip(
        *(explicit(plan, i, later, tangent, flow, shear, dx, dz) for i in range(len(WHOLE)))
    )
    right, turned, wall_flow = first_lines(plan, start, wall_derivative)
    states = [(right, turned) for _ in GROUPS]
    for section in range(SECTIONS):
        value = []
        for g, (whole, group) in enumerate(zip(WHOLE, GROUPS)):
            blocks, states[g] = advance_lines(
                plan,
                section,
                group,
                whole,
                me,
                term,
                wall_derivative,
                implicit_inverse,
                *(states[g] if section < SECTIONS - 1 else (states[g][0], None)),
                wall_flow,
            )
            value.append(exchange(plan, whole, blocks))
        if section < SECTIONS - 1:
            term = [
                explicit(plan, i, me, value, flow, shear, dx, dz, bases[i])[0]
                for i in range(len(WHOLE))
            ]
    return result(plan, me, spanwise_shift, ahead, value, tangents)[None]


def solution(mesh):
    placed = P("seg", None, "grid", None, None)
    return jax.shard_map(
        shards,
        mesh=mesh,
        in_specs=(placed, placed, placed, P(), P(), P(), P("seg")),
        out_specs=placed,
        check_vma=False,
    )
```

time: 1050 us -> 915 us (0.87)
  waiting for transfers between devices: 719 us -> 574 us
  Pallas kernels: 272 us -> 227 us
  starting transfers between devices: 55.5 us -> 85.9 us
  between operations: 1.67 us -> 14.4 us
  local copies, waits for them, and re-layouts: 0.99 us -> 11.6 us
    ppermute x49 -> x42, waiting for transfers between devices: 675 us -> 447 us  [exchange(): lax.ppermute(blocks[d], 'grid', [(i, i ^ d) for i in range(parts)])]
    all_to_all x0 -> x7, waiting for transfers between devices: none -> 128 us  [exchange(): lax.all_to_all(blocks[0], 'grid', split_axis=0, concat_axis=0, tiled=True)]
    pallas_call x8 -> x14, Pallas kernels: 257 us -> 212 us  [the longest x6 100 us: advance_lines(): pl.pallas_call(functools.partial(lines_kernel, plan, section, group, whol...]
    ppermute x2 -> x0, waiting for transfers between devices: 44.3 us -> none  [behind(): return lax.ppermute(block, 'seg', route)]
    all_to_all x0 -> x7, starting transfers between devices: none -> 30.9 us  [exchange(): lax.all_to_all(blocks[0], 'grid', split_axis=0, concat_axis=0, tiled=True)]
    ppermute x49 -> x42, starting transfers between devices: 52.1 us -> 55 us  [exchange(): lax.ppermute(blocks[d], 'grid', [(i, i ^ d) for i in range(parts)])]
  transfers between devices with their start and end apart: 51 -> 50, of which waited for: 34 -> 32; matrix products, arithmetic and copies ran while one was open for 0% -> 0% of each run, Pallas kernels for 24% -> 22%
where the time goes in v2:
time: 915 us; the launch traced here: 913 us
  waiting for transfers between devices  574 us (63%)
  Pallas kernels  227 us (25%)
  starting transfers between devices  85.9 us (9%)
  between operations  14.4 us (2%)
  local copies, waits for them, and re-layouts  11.6 us (1%)
    ppermute x42, waiting for transfers between devices, exchange(): lax.ppermute(blocks[d], 'grid', [(i, i ^ d) for i in range(parts)])  447 us
    all_to_all x7, waiting for transfers between devices, exchange(): lax.all_to_all(blocks[0], 'grid', split_axis=0, concat_axis=0, tiled=True)  128 us
    pallas_call x6, Pallas kernels, advance_lines(): pl.pallas_call(functools.partial(lines_kernel, plan, section, group, whol...  100 us
    pallas_call x6, Pallas kernels, explicit(): pl.pallas_call(functools.partial(explicit_kernel, plan, which, received),...  78.3 us
    ppermute x42, starting transfers between devices, exchange(): lax.ppermute(blocks[d], 'grid', [(i, i ^ d) for i in range(parts)])  55 us
    all_to_all x7, starting transfers between devices, exchange(): lax.all_to_all(blocks[0], 'grid', split_axis=0, concat_axis=0, tiled=True)  30.9 us
    pallas_call x1, Pallas kernels, first_lines(): pl.pallas_call(functools.partial(first_lines_kernel, plan), grid=(3,), in...  21.4 us
  transfers between devices with their start and end apart: 50, of which 32 were waited for; matrix products, arithmetic and copies ran while one was open for 0% of the time, Pallas kernels for 22%

profile of v2, /device:TPU:9, one launch (start us, length us, event | category | flops | bytes accessed | tf_op | source)
XLA Modules:
  0.0 913.2 jit_solution(16620202614513417536)
XLA Ops:
  6.5 11.7 %pack_start.1 = s16[8,1568,256]{2,1,0:T(8,128)(2,1)} custom-call(f32[3,12,256,256]{3,2,1,0:T(8,128)} %bitcast.6, bf16[3,12,256,256]{3,2,1,0:T(8,128)(2,1)} %bitcast.10), custom_call_target="tpu_custom_call" | custom-call | bytes 20000000 | tf_op jit(solution)/shard_map/pack_start/pallas_call | solution.py:125
  18.3 5.7 all-to-all-start.1
  24.0 10.6 %explicit.6 = (s16[8,400,256]{2,1,0:T(8,128)(2,1)}, f32[3,4,256,256]{3,2,1,0:T(8,128)}, f32[3,4,256,256]{3,2,1,0:T(8,128)}) custom-call(s32[1]{0:T(128)} %bitcast.me_ref, f32[3,12,256,256]{3,2,1,0:T(8,128)} %bitcast.8, bf16[3,12,256,256]{3,2,1,0:T(8,128)(2,1)} %bitcast.11, bf16[3,12,256,256]{3,2,1,0:T(8,128)(2,1)} %bitcast.17, ...), custom_call_target="tpu_custom_call" | custom-call | flops 4000000000 | bytes 16000000 | tf_op jit(solution)/shard_map/explicit/pallas_call | solution.py:288
  34.5 127.7 %all-to-all-done.1.refs_0_.refs_1_.refs_2_.refs_3_ = s16[8,1568,256]{2,1,0:T(8,128)(2,1)} async-done(((s16[8,1568,256]{2,1,0:T(8,128)(2,1)}), s16[8,1568,256]{2,1,0:T(8,128)(2,1)}, u32[]{:S(2)}, u32[]{:S(2)}) %all-to-all-start.1) | async-done | bytes 6422560 | tf_op jit(solution)/shard_map/all_to_all | solution.py:580
  162.2 7.2 all-to-all-start
  169.3 17.1 %explicit.7 = (s16[784,256]{1,0:T(8,128)(2,1)}, s16[784,256]{1,0:T(8,128)(2,1)}, s16[784,256]{1,0:T(8,128)(2,1)}, s16[784,256]{1,0:T(8,128)(2,1)}, s16[784,256]{...) custom-call(s32[1]{0:T(128)} %bitcast.me_ref, ...), custom_call_target="tpu_custom_call" | custom-call | flops 8000000000 | bytes 32000000 | tf_op jit(solution)/shard_map/explicit/pallas_call | solution.py:288
  188.6 2.1 collective-permute-start.3
  192.3 13.4 %collective-permute-done.1.refs_3_.refs_12_ = s16[784,256]{1,0:T(8,128)(2,1)S(1)} collective-permute-done((s16[784,256]{1,0:T(8,128)(2,1)}, s16[784,256]{1,0:T(8,128)(2,1)S(1)}, u32[]{:S(2)}, u32[]{:S(2)}) %collective-permute-start.1) | collective-permute-done | bytes 401440 | tf_op jit(solution)/shard_map/ppermute | solution.py:586
  205.7 3.2 collective-permute-start.6
  208.9 21.4 %first_lines.1 = (f32[3,32,96,256]{3,2,1,0:T(8,128)}, f32[3,32,96,256]{3,2,1,0:T(8,128)}, f32[32,96,256]{2,1,0:T(8,128)}) custom-call(s16[8,1568,256]{2,1,0:T(8,128)(2,1)} %all-to-all-done.1.refs_0_.refs_1_.refs_2_.refs_3_, s16[8,1568,256]{2,1,0:T(8,128)(2,1)} %all-to-all-done.1.refs_0_.refs_1_.refs_2_.refs_3_, ...), custom_call_target="tpu_custom_call" | custom-call | flops 1000000000 | bytes 30000000 | tf_op jit(solution)/shard_map/first_lines/pallas_call | solution.py:385
  230.4 26.3 %collective-permute-done.4.refs_6_.refs_15_ = s16[784,256]{1,0:T(8,128)(2,1)S(1)} collective-permute-done((s16[784,256]{1,0:T(8,128)(2,1)}, s16[784,256]{1,0:T(8,128)(2,1)S(1)}, u32[]{:S(2)}, u32[]{:S(2)}) %collective-permute-start.4) | collective-permute-done | bytes 401440 | tf_op jit(solution)/shard_map/ppermute | solution.py:586
  256.7 10.3 %collective-permute-done.5.refs_7_.refs_16_ = s16[784,256]{1,0:T(8,128)(2,1)} collective-permute-done((s16[784,256]{1,0:T(8,128)(2,1)}, s16[784,256]{1,0:T(8,128)(2,1)}, u32[]{:S(2)}, u32[]{:S(2)}) %collective-permute-start.5) | collective-permute-done | bytes 401440 | tf_op jit(solution)/shard_map/ppermute | solution.py:586
  267.0 9.1 collective-permute-done.6.refs_8_.refs_17_
  277.3 14.1 %advance_lines.6 = (s16[8,400,256]{2,1,0:T(8,128)(2,1)}, f32[1,32,96,256]{3,2,1,0:T(8,128)}, f32[1,32,96,256]{3,2,1,0:T(8,128)}) custom-call(s32[1]{0:T(128)} %bitcast.me_ref, s16[8,400,256]{2,1,0:T(8,128)(2,1)} %copy-done.2, s16[784,256]{1,0:T(8,128)(2,1)} %get-tuple-element.74.refs_1_.refs_10_, s16[784,256]{1,0:T(8,128)(2,1)} %copy-done.6, ...), custom_call_target="tpu_custom_call" | custom-call | flops 700000000 | bytes 17000000 | tf_op jit(solution)/shard_map/advance_lines/pallas_call | solution.py:512
  291.4 3.5 all-to-all-start.2
  295.0 22.6 %advance_lines.7 = (s16[784,256]{1,0:T(8,128)(2,1)}, s16[784,256]{1,0:T(8,128)(2,1)}, s16[784,256]{1,0:T(8,128)(2,1)}, s16[784,256]{1,0:T(8,128)(2,1)}, s16[784,...) custom-call(s32[1]{0:T(128)} %bitcast.me_ref, ...), custom_call_target="tpu_custom_call" | custom-call | flops 1400000000 | bytes 34000000 | tf_op jit(solution)/shard_map/advance_lines/pallas_call | solution.py:512
  322.0 51.2 %collective-permute-done.10.refs_5_ = s16[784,256]{1,0:T(8,128)(2,1)S(1)} collective-permute-done((s16[784,256]{1,0:T(8,128)(2,1)}, s16[784,256]{1,0:T(8,128)(2,1)S(1)}, u32[]{:S(2)}, u32[]{:S(2)}) %collective-permute-start.10) | collective-permute-done | bytes 401440 | tf_op jit(solution)/shard_map/ppermute | solution.py:586
  373.2 2.7 collective-permute-start.8
  376.0 5.9 collective-permute-done.11.refs_6_
  381.9 3.1 collective-permute-start.9
  384.9 7.2 collective-permute-done.12.refs_7_
  392.1 8.7 collective-permute-done.13.refs_8_
  403.5 9.5 %explicit.8 = s16[8,400,256]{2,1,0:T(8,128)(2,1)} custom-call(s32[1]{0:T(128)} %bitcast.me_ref, s16[8,400,256]{2,1,0:T(8,128)(2,1)} %copy-done.4, s16[784,256]{1,0:T(8,128)(2,1)} %get-tuple-element.87.refs_1_, s16[784,256]{1,0:T(8,128)(2,1)} %copy-done.36, s16[784,256]{1,0:T(8,128)(2,1)} %copy-done.38, s16[784,256]{1,0:T(8,128)(2,1)} %collective-permute-done.9.refs_4_, ...), custom_call_target="tpu_custom_call" | custom-call | flops 4000000000 | bytes 16000000 | tf_op jit(solution)/shard_map/explicit/pallas_call | solution.py:288
  413.0 3.7 all-to-all-start.3
  416.8 15.9 %explicit.9 = (s16[784,256]{1,0:T(8,128)(2,1)}, s16[784,256]{1,0:T(8,128)(2,1)}, s16[784,256]{1,0:T(8,128)(2,1)}, s16[784,256]{1,0:T(8,128)(2,1)}, s16[784,256]{...) custom-call(s32[1]{0:T(128)} %bitcast.me_ref, ...), custom_call_target="tpu_custom_call" | custom-call | flops 8000000000 | bytes 32000000 | tf_op jit(solution)/shard_map/explicit/pallas_call | solution.py:288
  434.9 2.1 collective-permute-start.17
  438.6 14.3 %collective-permute-done.15.refs_3_.refs_12_ = s16[784,256]{1,0:T(8,128)(2,1)S(1)} collective-permute-done((s16[784,256]{1,0:T(8,128)(2,1)}, s16[784,256]{1,0:T(8,128)(2,1)S(1)}, u32[]{:S(2)}, u32[]{:S(2)}) %collective-permute-start.15) | collective-permute-done | bytes 401440 | tf_op jit(solution)/shard_map/ppermute | solution.py:586
  452.9 3.4 collective-permute-start.20
  456.3 14.4 %collective-permute-done.16.refs_4_.refs_13_ = s16[784,256]{1,0:T(8,128)(2,1)S(1)} collective-permute-done((s16[784,256]{1,0:T(8,128)(2,1)}, s16[784,256]{1,0:T(8,128)(2,1)S(1)}, u32[]{:S(2)}, u32[]{:S(2)}) %collective-permute-start.16) | collective-permute-done | bytes 401440 | tf_op jit(solution)/shard_map/ppermute | solution.py:586
  472.1 32.0 %collective-permute-done.18.refs_6_.refs_15_ = s16[784,256]{1,0:T(8,128)(2,1)S(1)} collective-permute-done((s16[784,256]{1,0:T(8,128)(2,1)}, s16[784,256]{1,0:T(8,128)(2,1)S(1)}, u32[]{:S(2)}, u32[]{:S(2)}) %collective-permute-start.18) | collective-permute-done | bytes 401440 | tf_op jit(solution)/shard_map/ppermute | solution.py:586
  504.1 10.2 %collective-permute-done.19.refs_7_.refs_16_ = s16[784,256]{1,0:T(8,128)(2,1)S(1)} collective-permute-done((s16[784,256]{1,0:T(8,128)(2,1)}, s16[784,256]{1,0:T(8,128)(2,1)S(1)}, u32[]{:S(2)}, u32[]{:S(2)}) %collective-permute-start.19) | collective-permute-done | bytes 401440 | tf_op jit(solution)/shard_map/ppermute | solution.py:586
  515.0 8.1 collective-permute-done.20.refs_8_.refs_17_
  524.4 14.2 %advance_lines.8 = (s16[8,400,256]{2,1,0:T(8,128)(2,1)}, f32[1,32,96,256]{3,2,1,0:T(8,128)}, f32[1,32,96,256]{3,2,1,0:T(8,128)}) custom-call(s32[1]{0:T(128)} %bitcast.me_ref, s16[8,400,256]{2,1,0:T(8,128)(2,1)} %copy-done.1, s16[784,256]{1,0:T(8,128)(2,1)} %get-tuple-element.99.refs_1_.refs_10_, s16[784,256]{1,0:T(8,128)(2,1)} %copy-done.11, ...), custom_call_target="tpu_custom_call" | custom-call | flops 700000000 | bytes 17000000 | tf_op jit(solution)/shard_map/advance_lines/pallas_call | solution.py:512
  538.6 3.5 all-to-all-start.4
  542.2 22.6 %advance_lines.9 = (s16[784,256]{1,0:T(8,128)(2,1)}, s16[784,256]{1,0:T(8,128)(2,1)}, s16[784,256]{1,0:T(8,128)(2,1)}, s16[784,256]{1,0:T(8,128)(2,1)}, s16[784,...) custom-call(s32[1]{0:T(128)} %bitcast.me_ref, ...), custom_call_target="tpu_custom_call" | custom-call | flops 1400000000 | bytes 34000000 | tf_op jit(solution)/shard_map/advance_lines/pallas_call | solution.py:512
  565.0 1.9 collective-permute-start.23
  570.5 19.5 %collective-permute-done.22.refs_3_ = s16[784,256]{1,0:T(8,128)(2,1)S(1)} collective-permute-done((s16[784,256]{1,0:T(8,128)(2,1)}, s16[784,256]{1,0:T(8,128)(2,1)S(1)}, u32[]{:S(2)}, u32[]{:S(2)}) %collective-permute-start.22) | collective-permute-done | bytes 401440 | tf_op jit(solution)/shard_map/ppermute | solution.py:586
  590.1 2.6 collective-permute-start.27
  592.7 6.0 collective-permute-done.23.refs_4_
  598.7 30.7 %collective-permute-done.25.refs_6_ = s16[784,256]{1,0:T(8,128)(2,1)S(1)} collective-permute-done((s16[784,256]{1,0:T(8,128)(2,1)}, s16[784,256]{1,0:T(8,128)(2,1)S(1)}, u32[]{:S(2)}, u32[]{:S(2)}) %collective-permute-start.25) | collective-permute-done | bytes 401440 | tf_op jit(solution)/shard_map/ppermute | solution.py:586
  629.3 10.2 %collective-permute-done.26.refs_7_ = s16[784,256]{1,0:T(8,128)(2,1)S(1)} collective-permute-done((s16[784,256]{1,0:T(8,128)(2,1)}, s16[784,256]{1,0:T(8,128)(2,1)S(1)}, u32[]{:S(2)}, u32[]{:S(2)}) %collective-permute-start.26) | collective-permute-done | bytes 401440 | tf_op jit(solution)/shard_map/ppermute | solution.py:586
  640.3 8.1 collective-permute-done.27.refs_8_
  649.7 9.5 %explicit.10 = s16[8,400,256]{2,1,0:T(8,128)(2,1)} custom-call(s32[1]{0:T(128)} %bitcast.me_ref, s16[8,400,256]{2,1,0:T(8,128)(2,1)} %copy-done.3, s16[784,256]{1,0:T(8,128)(2,1)} %get-tuple-element.112.refs_1_, s16[784,256]{1,0:T(8,128)(2,1)} %copy-done.27, s16[784,256]{1,0:T(8,128)(2,1)} %copy-done.28, s16[784,256]{1,0:T(8,128)(2,1)} %copy-done.30, ...), custom_call_target="tpu_custom_call" | custom-call | flops 4000000000 | bytes 16000000 | tf_op jit(solution)/shard_map/explicit/pallas_call | solution.py:288
  659.2 3.5 all-to-all-start.5
  662.7 15.8 %explicit.11 = (s16[784,256]{1,0:T(8,128)(2,1)}, s16[784,256]{1,0:T(8,128)(2,1)}, s16[784,256]{1,0:T(8,128)(2,1)}, s16[784,256]{1,0:T(8,128)(2,1)}, s16[784,256]...) custom-call(s32[1]{0:T(128)} %bitcast.me_ref, ...), custom_call_target="tpu_custom_call" | custom-call | flops 8000000000 | bytes 32000000 | tf_op jit(solution)/shard_map/explicit/pallas_call | solution.py:288
  678.8 1.9 collective-permute-start.30
  680.7 1.9 collective-permute-start.31
  684.3 14.6 %collective-permute-done.29.refs_3_.refs_12_ = s16[784,256]{1,0:T(8,128)(2,1)S(1)} collective-permute-done((s16[784,256]{1,0:T(8,128)(2,1)}, s16[784,256]{1,0:T(8,128)(2,1)S(1)}, u32[]{:S(2)}, u32[]{:S(2)}) %collective-permute-start.29) | collective-permute-done | bytes 401440 | tf_op jit(solution)/shard_map/ppermute | solution.py:586
  698.9 3.3 collective-permute-start.34
  702.2 14.4 %collective-permute-done.30.refs_4_.refs_13_ = s16[784,256]{1,0:T(8,128)(2,1)S(1)} collective-permute-done((s16[784,256]{1,0:T(8,128)(2,1)}, s16[784,256]{1,0:T(8,128)(2,1)S(1)}, u32[]{:S(2)}, u32[]{:S(2)}) %collective-permute-start.30) | collective-permute-done | bytes 401440 | tf_op jit(solution)/shard_map/ppermute | solution.py:586
  717.9 32.0 %collective-permute-done.32.refs_6_.refs_15_ = s16[784,256]{1,0:T(8,128)(2,1)S(1)} collective-permute-done((s16[784,256]{1,0:T(8,128)(2,1)}, s16[784,256]{1,0:T(8,128)(2,1)S(1)}, u32[]{:S(2)}, u32[]{:S(2)}) %collective-permute-start.32) | collective-permute-done | bytes 401440 | tf_op jit(solution)/shard_map/ppermute | solution.py:586
  749.9 10.2 %collective-permute-done.33.refs_7_.refs_16_ = s16[784,256]{1,0:T(8,128)(2,1)S(1)} collective-permute-done((s16[784,256]{1,0:T(8,128)(2,1)}, s16[784,256]{1,0:T(8,128)(2,1)S(1)}, u32[]{:S(2)}, u32[]{:S(2)}) %collective-permute-start.33) | collective-permute-done | bytes 401440 | tf_op jit(solution)/shard_map/ppermute | solution.py:586
  760.9 8.1 collective-permute-done.34.refs_8_.refs_17_
  770.2 9.9 %advance_lines.10 = s16[8,400,256]{2,1,0:T(8,128)(2,1)} custom-call(s32[1]{0:T(128)} %bitcast.me_ref, s16[8,400,256]{2,1,0:T(8,128)(2,1)} %copy-done, s16[784,256]{1,0:T(8,128)(2,1)} %get-tuple-element.120.refs_1_.refs_10_, s16[784,256]{1,0:T(8,128)(2,1)} %copy-done.15, s16[784,256]{1,0:T(8,128)(2,1)} %copy-done.17, s16[784,256]{1,0:T(8,128)(2,1)} %copy-done.18, ...), custom_call_target="tpu_custom_call" | custom-call | flops 700000000 | bytes 17000000 | tf_op jit(solution)/shard_map/advance_lines/pallas_call | solution.py:512
  780.1 3.8 all-to-all-start.6
  783.9 16.8 %advance_lines.11 = (s16[784,256]{1,0:T(8,128)(2,1)}, s16[784,256]{1,0:T(8,128)(2,1)}, s16[784,256]{1,0:T(8,128)(2,1)}, s16[784,256]{1,0:T(8,128)(2,1)}, s16[784...) custom-call(s32[1]{0:T(128)} %bitcast.me_ref, ...), custom_call_target="tpu_custom_call" | custom-call | flops 1400000000 | bytes 34000000 | tf_op jit(solution)/shard_map/advance_lines/pallas_call | solution.py:512
  800.9 1.9 collective-permute-start.37
  806.2 13.6 %collective-permute-done.36.refs_3_ = s16[784,256]{1,0:T(8,128)(2,1)S(1)} collective-permute-done((s16[784,256]{1,0:T(8,128)(2,1)}, s16[784,256]{1,0:T(8,128)(2,1)S(1)}, u32[]{:S(2)}, u32[]{:S(2)}) %collective-permute-start.36) | collective-permute-done | bytes 401440 | tf_op jit(solution)/shard_map/ppermute | solution.py:586
  819.8 3.3 collective-permute-start.41
  824.3 13.8 %collective-permute-done.37.refs_4_ = s16[784,256]{1,0:T(8,128)(2,1)S(1)} collective-permute-done((s16[784,256]{1,0:T(8,128)(2,1)}, s16[784,256]{1,0:T(8,128)(2,1)S(1)}, u32[]{:S(2)}, u32[]{:S(2)}) %collective-permute-start.37) | collective-permute-done | bytes 401440 | tf_op jit(solution)/shard_map/ppermute | solution.py:586
  838.8 32.0 %collective-permute-done.39.refs_6_ = s16[784,256]{1,0:T(8,128)(2,1)} collective-permute-done((s16[784,256]{1,0:T(8,128)(2,1)}, s16[784,256]{1,0:T(8,128)(2,1)}, u32[]{:S(2)}, u32[]{:S(2)}) %collective-permute-start.39) | collective-permute-done | bytes 401440 | tf_op jit(solution)/shard_map/ppermute | solution.py:586
  870.8 10.3 %collective-permute-done.40.refs_7_ = s16[784,256]{1,0:T(8,128)(2,1)} collective-permute-done((s16[784,256]{1,0:T(8,128)(2,1)}, s16[784,256]{1,0:T(8,128)(2,1)}, u32[]{:S(2)}, u32[]{:S(2)}) %collective-permute-start.40) | collective-permute-done | bytes 401440 | tf_op jit(solution)/shard_map/ppermute | solution.py:586
  881.1 8.8 collective-permute-done.41.refs_8_
  891.1 15.3 %result.1 = f32[3,12,256,256]{3,2,1,0:T(8,128)} custom-call(s32[1]{0:T(128)} %bitcast.me_ref, s32[1]{0:T(128)S(6)} %copy.10.shift_ref, s32[1]{0:T(128)} %dynamic_slice.3.successor_ref, s16[8,400,256]{2,1,0:T(8,128)(2,1)} %copy-done.5, s16[784,256]{1,0:T(8,128)(2,1)} %get-tuple-element.130.refs_1_, s16[784,256]{1,0:T(8,128)(2,1)} %copy-done.23, ...), custom_call_target="tpu_custom_call" | custom-call | bytes 25000000 | tf_op jit(solution)/shard_map/result/pallas_call | solution.py:556
  (133 shorter events, 36.6 us)
Async XLA Ops:
  6.5 883.4 %all-gather.3.cloned.1.call-start = ((), (), s32[]{:S(2)}) async-start(), calls=%async_computation.7 | async-start | bytes 47185920 | tf_op jit(solution)/shard_map/all_gather | solution.py:603
  18.3 143.9 %all-to-all-start.1 = ((s16[8,1568,256]{2,1,0:T(8,128)(2,1)}), s16[8,1568,256]{2,1,0:T(8,128)(2,1)}, u32[]{:S(2)}, u32[]{:S(2)}) async-start(s16[8,1568,256]{2,1,0:T(8,128)(2,1)} %pack_start.1), calls=%async_computation.1 | async-start | bytes 12845056 | tf_op jit(solution)/shard_map/all_to_all | solution.py:580
  162.2 113.9 %all-to-all-start = ((s16[8,400,256]{2,1,0:T(8,128)(2,1)}), s16[8,400,256]{2,1,0:T(8,128)(2,1)S(1)}, u32[]{:S(2)}, u32[]{:S(2)}) async-start(s16[8,400,256]{2,1,0:T(8,128)(2,1)} %get-tuple-element.73), calls=%async_computation | async-start | bytes 3276800 | tf_op jit(solution)/shard_map/all_to_all | solution.py:580
  186.4 4.8 collective-permute-start
  186.8 19.0 %collective-permute-start.1 = (s16[784,256]{1,0:T(8,128)(2,1)}, s16[784,256]{1,0:T(8,128)(2,1)S(1)}, u32[]{:S(2)}, u32[]{:S(2)}) collective-permute-start(s16[784,256]{1,0:T(8,128)(2,1)} %get-tuple-element.76), channel_id=1, source_target_pairs={{0,2},{1,3},{2,0},{3,1},{4,6},{5,7},{6,4},{7,5},{8,10},{9,11},{10,... | collective-permute-start | bytes 1204232 | tf_op jit(solution)/shard_map/ppermute | solution.py:586
  186.8 43.6 %collective-permute-start.2 = (s16[784,256]{1,0:T(8,128)(2,1)}, s16[784,256]{1,0:T(8,128)(2,1)S(1)}, u32[]{:S(2)}, u32[]{:S(2)}) collective-permute-start(s16[784,256]{1,0:T(8,128)(2,1)} %get-tuple-element.77), channel_id=1, source_target_pairs={{0,3},{1,2},{2,1},{3,0},{4,7},{5,6},{6,5},{7,4},{8,11},{9,10},{10,... | collective-permute-start | bytes 1204232 | tf_op jit(solution)/shard_map/ppermute | solution.py:586
  188.6 41.8 %collective-permute-start.3 = (s16[784,256]{1,0:T(8,128)(2,1)}, s16[784,256]{1,0:T(8,128)(2,1)S(1)}, u32[]{:S(2)}, u32[]{:S(2)}) collective-permute-start(s16[784,256]{1,0:T(8,128)(2,1)} %get-tuple-element.78), channel_id=1, source_target_pairs={{0,4},{1,5},{2,6},{3,7},{4,0},{5,1},{6,2},{7,3},{8,12},{9,13},{10,... | collective-permute-start | bytes 1204232 | tf_op jit(solution)/shard_map/ppermute | solution.py:586
  190.7 66.0 %collective-permute-start.4 = (s16[784,256]{1,0:T(8,128)(2,1)}, s16[784,256]{1,0:T(8,128)(2,1)S(1)}, u32[]{:S(2)}, u32[]{:S(2)}) collective-permute-start(s16[784,256]{1,0:T(8,128)(2,1)} %get-tuple-element.79), channel_id=1, source_target_pairs={{0,5},{1,4},{2,7},{3,6},{4,1},{5,0},{6,3},{7,2},{8,13},{9,12},{10,... | collective-permute-start | bytes 1204232 | tf_op jit(solution)/shard_map/ppermute | solution.py:586
  191.2 75.8 %collective-permute-start.5 = (s16[784,256]{1,0:T(8,128)(2,1)}, s16[784,256]{1,0:T(8,128)(2,1)}, u32[]{:S(2)}, u32[]{:S(2)}) collective-permute-start(s16[784,256]{1,0:T(8,128)(2,1)} %get-tuple-element.80), channel_id=1, source_target_pairs={{0,6},{1,7},{2,4},{3,5},{4,2},{5,3},{6,0},{7,1},{8,14},{9,15},{10,... | collective-permute-start | bytes 1204232 | tf_op jit(solution)/shard_map/ppermute | solution.py:586
  205.7 70.3 %collective-permute-start.6 = (s16[784,256]{1,0:T(8,128)(2,1)}, s16[784,256]{1,0:T(8,128)(2,1)}, u32[]{:S(2)}, u32[]{:S(2)}) collective-permute-start(s16[784,256]{1,0:T(8,128)(2,1)} %get-tuple-element.81), channel_id=1, source_target_pairs={{0,7},{1,6},{2,5},{3,4},{4,3},{5,2},{6,1},{7,0},{8,15},{9,14},{10,... | collective-permute-start | bytes 1204232 | tf_op jit(solution)/shard_map/ppermute | solution.py:586
  291.4 110.9 %all-to-all-start.2 = ((s16[8,400,256]{2,1,0:T(8,128)(2,1)}), s16[8,400,256]{2,1,0:T(8,128)(2,1)S(1)}, u32[]{:S(2)}, u32[]{:S(2)}) async-start(s16[8,400,256]{2,1,0:T(8,128)(2,1)} %get-tuple-element.86), calls=%async_computation.2 | async-start | bytes 3276800 | tf_op jit(solution)/shard_map/all_to_all | solution.py:580
  317.6 55.6 %collective-permute-start.10 = (s16[784,256]{1,0:T(8,128)(2,1)}, s16[784,256]{1,0:T(8,128)(2,1)S(1)}, u32[]{:S(2)}, u32[]{:S(2)}) collective-permute-start(s16[784,256]{1,0:T(8,128)(2,1)} %get-tuple-element.91), channel_id=1, source_target_pairs={{0,4},{1,5},{2,6},{3,7},{4,0},{5,1},{6,2},{7,3},{8,12},{9,13},{10,... | collective-permute-start | bytes 1204232 | tf_op jit(solution)/shard_map/ppermute | solution.py:586
  319.2 62.7 %collective-permute-start.11 = (s16[784,256]{1,0:T(8,128)(2,1)}, s16[784,256]{1,0:T(8,128)(2,1)S(1)}, u32[]{:S(2)}, u32[]{:S(2)}) collective-permute-start(s16[784,256]{1,0:T(8,128)(2,1)} %get-tuple-element.92), channel_id=1, source_target_pairs={{0,5},{1,4},{2,7},{3,6},{4,1},{5,0},{6,3},{7,2},{8,13},{9,12},{10,... | collective-permute-start | bytes 1204232 | tf_op jit(solution)/shard_map/ppermute | solution.py:586
  320.1 72.0 %collective-permute-start.12 = (s16[784,256]{1,0:T(8,128)(2,1)}, s16[784,256]{1,0:T(8,128)(2,1)S(1)}, u32[]{:S(2)}, u32[]{:S(2)}) collective-permute-start(s16[784,256]{1,0:T(8,128)(2,1)} %get-tuple-element.93), channel_id=1, source_target_pairs={{0,6},{1,7},{2,4},{3,5},{4,2},{5,3},{6,0},{7,1},{8,14},{9,15},{10,... | collective-permute-start | bytes 1204232 | tf_op jit(solution)/shard_map/ppermute | solution.py:586
  321.2 79.6 %collective-permute-start.13 = (s16[784,256]{1,0:T(8,128)(2,1)}, s16[784,256]{1,0:T(8,128)(2,1)S(1)}, u32[]{:S(2)}, u32[]{:S(2)}) collective-permute-start(s16[784,256]{1,0:T(8,128)(2,1)} %get-tuple-element.94), channel_id=1, source_target_pairs={{0,7},{1,6},{2,5},{3,4},{4,3},{5,2},{6,1},{7,0},{8,15},{9,14},{10,... | collective-permute-start | bytes 1204232 | tf_op jit(solution)/shard_map/ppermute | solution.py:586
  322.0 78.8 %collective-permute-start.7 = (s16[784,256]{1,0:T(8,128)(2,1)}, s16[784,256]{1,0:T(8,128)(2,1)S(1)}, u32[]{:S(2)}, u32[]{:S(2)}) collective-permute-start(s16[784,256]{1,0:T(8,128)(2,1)} %get-tuple-element.88), channel_id=1, source_target_pairs={{0,1},{1,0},{2,3},{3,2},{4,5},{5,4},{6,7},{7,6},{8,9},{9,8},{10,11... | collective-permute-start | bytes 1204232 | tf_op jit(solution)/shard_map/ppermute | solution.py:586
  373.2 27.6 %collective-permute-start.8 = (s16[784,256]{1,0:T(8,128)(2,1)}, s16[784,256]{1,0:T(8,128)(2,1)S(1)}, u32[]{:S(2)}, u32[]{:S(2)}) collective-permute-start(s16[784,256]{1,0:T(8,128)(2,1)} %get-tuple-element.89), channel_id=1, source_target_pairs={{0,2},{1,3},{2,0},{3,1},{4,6},{5,7},{6,4},{7,5},{8,10},{9,11},{10,... | collective-permute-start | bytes 1204232 | tf_op jit(solution)/shard_map/ppermute | solution.py:586
  381.9 20.5 %collective-permute-start.9 = (s16[784,256]{1,0:T(8,128)(2,1)}, s16[784,256]{1,0:T(8,128)(2,1)}, u32[]{:S(2)}, u32[]{:S(2)}) collective-permute-start(s16[784,256]{1,0:T(8,128)(2,1)} %get-tuple-element.90), channel_id=1, source_target_pairs={{0,3},{1,2},{2,1},{3,0},{4,7},{5,6},{6,5},{7,4},{8,11},{9,10},{10,... | collective-permute-start | bytes 1204232 | tf_op jit(solution)/shard_map/ppermute | solution.py:586
  413.0 110.1 %all-to-all-start.3 = ((s16[8,400,256]{2,1,0:T(8,128)(2,1)}), s16[8,400,256]{2,1,0:T(8,128)(2,1)S(1)}, u32[]{:S(2)}, u32[]{:S(2)}) async-start(s16[8,400,256]{2,1,0:T(8,128)(2,1)} %explicit.8), calls=%async_computation.3 | async-start | bytes 3276800 | tf_op jit(solution)/shard_map/all_to_all | solution.py:580
  432.7 4.8 collective-permute-start.14
  433.0 19.9 %collective-permute-start.15 = (s16[784,256]{1,0:T(8,128)(2,1)}, s16[784,256]{1,0:T(8,128)(2,1)S(1)}, u32[]{:S(2)}, u32[]{:S(2)}) collective-permute-start(s16[784,256]{1,0:T(8,128)(2,1)} %get-tuple-element.101), channel_id=1, source_target_pairs={{0,2},{1,3},{2,0},{3,1},{4,6},{5,7},{6,4},{7,5},{8,10},{9,11},{10,... | collective-permute-start | bytes 1204232 | tf_op jit(solution)/shard_map/ppermute | solution.py:586
  433.0 37.7 %collective-permute-start.16 = (s16[784,256]{1,0:T(8,128)(2,1)}, s16[784,256]{1,0:T(8,128)(2,1)S(1)}, u32[]{:S(2)}, u32[]{:S(2)}) collective-permute-start(s16[784,256]{1,0:T(8,128)(2,1)} %get-tuple-element.102), channel_id=1, source_target_pairs={{0,3},{1,2},{2,1},{3,0},{4,7},{5,6},{6,5},{7,4},{8,11},{9,10},{10,... | collective-permute-start | bytes 1204232 | tf_op jit(solution)/shard_map/ppermute | solution.py:586
  434.9 37.2 %collective-permute-start.17 = (s16[784,256]{1,0:T(8,128)(2,1)}, s16[784,256]{1,0:T(8,128)(2,1)S(1)}, u32[]{:S(2)}, u32[]{:S(2)}) collective-permute-start(s16[784,256]{1,0:T(8,128)(2,1)} %get-tuple-element.103), channel_id=1, source_target_pairs={{0,4},{1,5},{2,6},{3,7},{4,0},{5,1},{6,2},{7,3},{8,12},{9,13},{10,... | collective-permute-start | bytes 1204232 | tf_op jit(solution)/shard_map/ppermute | solution.py:586
  436.9 67.1 %collective-permute-start.18 = (s16[784,256]{1,0:T(8,128)(2,1)}, s16[784,256]{1,0:T(8,128)(2,1)S(1)}, u32[]{:S(2)}, u32[]{:S(2)}) collective-permute-start(s16[784,256]{1,0:T(8,128)(2,1)} %get-tuple-element.104), channel_id=1, source_target_pairs={{0,5},{1,4},{2,7},{3,6},{4,1},{5,0},{6,3},{7,2},{8,13},{9,12},{10,... | collective-permute-start | bytes 1204232 | tf_op jit(solution)/shard_map/ppermute | solution.py:586
  437.4 85.7 %copy-start.11 = (s16[784,256]{1,0:T(8,128)(2,1)}, s16[784,256]{1,0:T(8,128)(2,1)S(1)}, u32[]{:S(2)}) copy-start(s16[784,256]{1,0:T(8,128)(2,1)S(1)} %collective-permute-done.14.refs_2_.refs_11_) | copy-start | bytes 1204228
  437.4 76.8 %collective-permute-start.19 = (s16[784,256]{1,0:T(8,128)(2,1)}, s16[784,256]{1,0:T(8,128)(2,1)S(1)}, u32[]{:S(2)}, u32[]{:S(2)}) collective-permute-start(s16[784,256]{1,0:T(8,128)(2,1)} %get-tuple-element.105), channel_id=1, source_target_pairs={{0,6},{1,7},{2,4},{3,5},{4,2},{5,3},{6,0},{7,1},{8,14},{9,15},{10,... | collective-permute-start | bytes 1204232 | tf_op jit(solution)/shard_map/ppermute | solution.py:586
  452.9 70.2 %copy-start.12 = (s16[784,256]{1,0:T(8,128)(2,1)}, s16[784,256]{1,0:T(8,128)(2,1)S(1)}, u32[]{:S(2)}) copy-start(s16[784,256]{1,0:T(8,128)(2,1)S(1)} %collective-permute-done.15.refs_3_.refs_12_) | copy-start | bytes 1204228
  452.9 70.2 %collective-permute-start.20 = (s16[784,256]{1,0:T(8,128)(2,1)}, s16[784,256]{1,0:T(8,128)(2,1)}, u32[]{:S(2)}, u32[]{:S(2)}) collective-permute-start(s16[784,256]{1,0:T(8,128)(2,1)} %get-tuple-element.106), channel_id=1, source_target_pairs={{0,7},{1,6},{2,5},{3,4},{4,3},{5,2},{6,1},{7,0},{8,15},{9,14},{10,... | collective-permute-start | bytes 1204232 | tf_op jit(solution)/shard_map/ppermute | solution.py:586
  470.8 52.4 %copy-start.13 = (s16[784,256]{1,0:T(8,128)(2,1)}, s16[784,256]{1,0:T(8,128)(2,1)S(1)}, u32[]{:S(2)}) copy-start(s16[784,256]{1,0:T(8,128)(2,1)S(1)} %collective-permute-done.16.refs_4_.refs_13_) | copy-start | bytes 1204228
  472.1 51.1 %copy-start.14 = (s16[784,256]{1,0:T(8,128)(2,1)}, s16[784,256]{1,0:T(8,128)(2,1)S(1)}, u32[]{:S(2)}) copy-start(s16[784,256]{1,0:T(8,128)(2,1)S(1)} %collective-permute-done.17.refs_5_.refs_14_) | copy-start | bytes 1204228
  538.6 109.8 %all-to-all-start.4 = ((s16[8,400,256]{2,1,0:T(8,128)(2,1)}), s16[8,400,256]{2,1,0:T(8,128)(2,1)S(1)}, u32[]{:S(2)}, u32[]{:S(2)}) async-start(s16[8,400,256]{2,1,0:T(8,128)(2,1)} %get-tuple-element.109), calls=%async_computation.4 | async-start | bytes 3276800 | tf_op jit(solution)/shard_map/all_to_all | solution.py:580
  564.8 4.7 collective-permute-start.21
  565.0 25.0 %collective-permute-start.22 = (s16[784,256]{1,0:T(8,128)(2,1)}, s16[784,256]{1,0:T(8,128)(2,1)S(1)}, u32[]{:S(2)}, u32[]{:S(2)}) collective-permute-start(s16[784,256]{1,0:T(8,128)(2,1)} %get-tuple-element.114), channel_id=1, source_target_pairs={{0,2},{1,3},{2,0},{3,1},{4,6},{5,7},{6,4},{7,5},{8,10},{9,11},{10,... | collective-permute-start | bytes 1204232 | tf_op jit(solution)/shard_map/ppermute | solution.py:586
  565.0 33.6 %collective-permute-start.23 = (s16[784,256]{1,0:T(8,128)(2,1)}, s16[784,256]{1,0:T(8,128)(2,1)S(1)}, u32[]{:S(2)}, u32[]{:S(2)}) collective-permute-start(s16[784,256]{1,0:T(8,128)(2,1)} %get-tuple-element.115), channel_id=1, source_target_pairs={{0,3},{1,2},{2,1},{3,0},{4,7},{5,6},{6,5},{7,4},{8,11},{9,10},{10,... | collective-permute-start | bytes 1204232 | tf_op jit(solution)/shard_map/ppermute | solution.py:586
  567.0 31.7 %collective-permute-start.24 = (s16[784,256]{1,0:T(8,128)(2,1)}, s16[784,256]{1,0:T(8,128)(2,1)S(1)}, u32[]{:S(2)}, u32[]{:S(2)}) collective-permute-start(s16[784,256]{1,0:T(8,128)(2,1)} %get-tuple-element.116), channel_id=1, source_target_pairs={{0,4},{1,5},{2,6},{3,7},{4,0},{5,1},{6,2},{7,3},{8,12},{9,13},{10,... | collective-permute-start | bytes 1204232 | tf_op jit(solution)/shard_map/ppermute | solution.py:586
  568.8 60.5 %collective-permute-start.25 = (s16[784,256]{1,0:T(8,128)(2,1)}, s16[784,256]{1,0:T(8,128)(2,1)S(1)}, u32[]{:S(2)}, u32[]{:S(2)}) collective-permute-start(s16[784,256]{1,0:T(8,128)(2,1)} %get-tuple-element.117), channel_id=1, source_target_pairs={{0,5},{1,4},{2,7},{3,6},{4,1},{5,0},{6,3},{7,2},{8,13},{9,12},{10,... | collective-permute-start | bytes 1204232 | tf_op jit(solution)/shard_map/ppermute | solution.py:586
  569.4 79.0 %copy-start.27 = (s16[784,256]{1,0:T(8,128)(2,1)}, s16[784,256]{1,0:T(8,128)(2,1)S(1)}, u32[]{:S(2)}) copy-start(s16[784,256]{1,0:T(8,128)(2,1)S(1)} %collective-permute-done.21.refs_2_) | copy-start | bytes 1204228
  569.4 70.1 %collective-permute-start.26 = (s16[784,256]{1,0:T(8,128)(2,1)}, s16[784,256]{1,0:T(8,128)(2,1)S(1)}, u32[]{:S(2)}, u32[]{:S(2)}) collective-permute-start(s16[784,256]{1,0:T(8,128)(2,1)} %get-tuple-element.118), channel_id=1, source_target_pairs={{0,6},{1,7},{2,4},{3,5},{4,2},{5,3},{6,0},{7,1},{8,14},{9,15},{10,... | collective-permute-start | bytes 1204232 | tf_op jit(solution)/shard_map/ppermute | solution.py:586
  590.1 58.4 %copy-start.28 = (s16[784,256]{1,0:T(8,128)(2,1)}, s16[784,256]{1,0:T(8,128)(2,1)S(1)}, u32[]{:S(2)}) copy-start(s16[784,256]{1,0:T(8,128)(2,1)S(1)} %collective-permute-done.22.refs_3_) | copy-start | bytes 1204228
  590.1 58.4 %collective-permute-start.27 = (s16[784,256]{1,0:T(8,128)(2,1)}, s16[784,256]{1,0:T(8,128)(2,1)}, u32[]{:S(2)}, u32[]{:S(2)}) collective-permute-start(s16[784,256]{1,0:T(8,128)(2,1)} %get-tuple-element.119), channel_id=1, source_target_pairs={{0,7},{1,6},{2,5},{3,4},{4,3},{5,2},{6,1},{7,0},{8,15},{9,14},{10,... | collective-permute-start | bytes 1204232 | tf_op jit(solution)/shard_map/ppermute | solution.py:586
  659.2 109.8 %all-to-all-start.5 = ((s16[8,400,256]{2,1,0:T(8,128)(2,1)}), s16[8,400,256]{2,1,0:T(8,128)(2,1)S(1)}, u32[]{:S(2)}, u32[]{:S(2)}) async-start(s16[8,400,256]{2,1,0:T(8,128)(2,1)} %explicit.10), calls=%async_computation.5 | async-start | bytes 3276800 | tf_op jit(solution)/shard_map/all_to_all | solution.py:580
  678.5 4.7 collective-permute-start.28
  678.8 20.1 %collective-permute-start.29 = (s16[784,256]{1,0:T(8,128)(2,1)}, s16[784,256]{1,0:T(8,128)(2,1)S(1)}, u32[]{:S(2)}, u32[]{:S(2)}) collective-permute-start(s16[784,256]{1,0:T(8,128)(2,1)} %get-tuple-element.122), channel_id=1, source_target_pairs={{0,2},{1,3},{2,0},{3,1},{4,6},{5,7},{6,4},{7,5},{8,10},{9,11},{10,... | collective-permute-start | bytes 1204232 | tf_op jit(solution)/shard_map/ppermute | solution.py:586
  678.8 37.8 %collective-permute-start.30 = (s16[784,256]{1,0:T(8,128)(2,1)}, s16[784,256]{1,0:T(8,128)(2,1)S(1)}, u32[]{:S(2)}, u32[]{:S(2)}) collective-permute-start(s16[784,256]{1,0:T(8,128)(2,1)} %get-tuple-element.123), channel_id=1, source_target_pairs={{0,3},{1,2},{2,1},{3,0},{4,7},{5,6},{6,5},{7,4},{8,11},{9,10},{10,... | collective-permute-start | bytes 1204232 | tf_op jit(solution)/shard_map/ppermute | solution.py:586
  680.7 37.2 %collective-permute-start.31 = (s16[784,256]{1,0:T(8,128)(2,1)}, s16[784,256]{1,0:T(8,128)(2,1)S(1)}, u32[]{:S(2)}, u32[]{:S(2)}) collective-permute-start(s16[784,256]{1,0:T(8,128)(2,1)} %get-tuple-element.124), channel_id=1, source_target_pairs={{0,4},{1,5},{2,6},{3,7},{4,0},{5,1},{6,2},{7,3},{8,12},{9,13},{10,... | collective-permute-start | bytes 1204232 | tf_op jit(solution)/shard_map/ppermute | solution.py:586
  682.6 67.3 %collective-permute-start.32 = (s16[784,256]{1,0:T(8,128)(2,1)}, s16[784,256]{1,0:T(8,128)(2,1)S(1)}, u32[]{:S(2)}, u32[]{:S(2)}) collective-permute-start(s16[784,256]{1,0:T(8,128)(2,1)} %get-tuple-element.125), channel_id=1, source_target_pairs={{0,5},{1,4},{2,7},{3,6},{4,1},{5,0},{6,3},{7,2},{8,13},{9,12},{10,... | collective-permute-start | bytes 1204232 | tf_op jit(solution)/shard_map/ppermute | solution.py:586
  683.2 85.8 %copy-start.15 = (s16[784,256]{1,0:T(8,128)(2,1)}, s16[784,256]{1,0:T(8,128)(2,1)S(1)}, u32[]{:S(2)}) copy-start(s16[784,256]{1,0:T(8,128)(2,1)S(1)} %collective-permute-done.28.refs_2_.refs_11_) | copy-start | bytes 1204228
  683.2 76.9 %collective-permute-start.33 = (s16[784,256]{1,0:T(8,128)(2,1)}, s16[784,256]{1,0:T(8,128)(2,1)S(1)}, u32[]{:S(2)}, u32[]{:S(2)}) collective-permute-start(s16[784,256]{1,0:T(8,128)(2,1)} %get-tuple-element.126), channel_id=1, source_target_pairs={{0,6},{1,7},{2,4},{3,5},{4,2},{5,3},{6,0},{7,1},{8,14},{9,15},{10,... | collective-permute-start | bytes 1204232 | tf_op jit(solution)/shard_map/ppermute | solution.py:586
  698.9 70.1 %copy-start.17 = (s16[784,256]{1,0:T(8,128)(2,1)}, s16[784,256]{1,0:T(8,128)(2,1)S(1)}, u32[]{:S(2)}) copy-start(s16[784,256]{1,0:T(8,128)(2,1)S(1)} %collective-permute-done.29.refs_3_.refs_12_) | copy-start | bytes 1204228
  698.9 70.1 %collective-permute-start.34 = (s16[784,256]{1,0:T(8,128)(2,1)}, s16[784,256]{1,0:T(8,128)(2,1)}, u32[]{:S(2)}, u32[]{:S(2)}) collective-permute-start(s16[784,256]{1,0:T(8,128)(2,1)} %get-tuple-element.127), channel_id=1, source_target_pairs={{0,7},{1,6},{2,5},{3,4},{4,3},{5,2},{6,1},{7,0},{8,15},{9,14},{10,... | collective-permute-start | bytes 1204232 | tf_op jit(solution)/shard_map/ppermute | solution.py:586
  716.5 52.5 %copy-start.18 = (s16[784,256]{1,0:T(8,128)(2,1)}, s16[784,256]{1,0:T(8,128)(2,1)S(1)}, u32[]{:S(2)}) copy-start(s16[784,256]{1,0:T(8,128)(2,1)S(1)} %collective-permute-done.30.refs_4_.refs_13_) | copy-start | bytes 1204228
  717.9 51.1 %copy-start.19 = (s16[784,256]{1,0:T(8,128)(2,1)}, s16[784,256]{1,0:T(8,128)(2,1)S(1)}, u32[]{:S(2)}) copy-start(s16[784,256]{1,0:T(8,128)(2,1)S(1)} %collective-permute-done.31.refs_5_.refs_14_) | copy-start | bytes 1204228
  780.1 109.8 %all-to-all-start.6 = ((s16[8,400,256]{2,1,0:T(8,128)(2,1)}), s16[8,400,256]{2,1,0:T(8,128)(2,1)S(1)}, u32[]{:S(2)}, u32[]{:S(2)}) async-start(s16[8,400,256]{2,1,0:T(8,128)(2,1)} %advance_lines.10), calls=%async_computation.6 | async-start | bytes 3276800 | tf_op jit(solution)/shard_map/all_to_all | solution.py:580
  800.6 4.7 collective-permute-start.35
  800.9 18.9 %collective-permute-start.36 = (s16[784,256]{1,0:T(8,128)(2,1)}, s16[784,256]{1,0:T(8,128)(2,1)S(1)}, u32[]{:S(2)}, u32[]{:S(2)}) collective-permute-start(s16[784,256]{1,0:T(8,128)(2,1)} %get-tuple-element.132), channel_id=1, source_target_pairs={{0,2},{1,3},{2,0},{3,1},{4,6},{5,7},{6,4},{7,5},{8,10},{9,11},{10,... | collective-permute-start | bytes 1204232 | tf_op jit(solution)/shard_map/ppermute | solution.py:586
  800.9 37.2 %collective-permute-start.37 = (s16[784,256]{1,0:T(8,128)(2,1)}, s16[784,256]{1,0:T(8,128)(2,1)S(1)}, u32[]{:S(2)}, u32[]{:S(2)}) collective-permute-start(s16[784,256]{1,0:T(8,128)(2,1)} %get-tuple-element.133), channel_id=1, source_target_pairs={{0,3},{1,2},{2,1},{3,0},{4,7},{5,6},{6,5},{7,4},{8,11},{9,10},{10,... | collective-permute-start | bytes 1204232 | tf_op jit(solution)/shard_map/ppermute | solution.py:586
  802.9 35.9 %collective-permute-start.38 = (s16[784,256]{1,0:T(8,128)(2,1)}, s16[784,256]{1,0:T(8,128)(2,1)S(1)}, u32[]{:S(2)}, u32[]{:S(2)}) collective-permute-start(s16[784,256]{1,0:T(8,128)(2,1)} %get-tuple-element.134), channel_id=1, source_target_pairs={{0,4},{1,5},{2,6},{3,7},{4,0},{5,1},{6,2},{7,3},{8,12},{9,13},{10,... | collective-permute-start | bytes 1204232 | tf_op jit(solution)/shard_map/ppermute | solution.py:586
  804.5 66.3 %collective-permute-start.39 = (s16[784,256]{1,0:T(8,128)(2,1)}, s16[784,256]{1,0:T(8,128)(2,1)}, u32[]{:S(2)}, u32[]{:S(2)}) collective-permute-start(s16[784,256]{1,0:T(8,128)(2,1)} %get-tuple-element.135), channel_id=1, source_target_pairs={{0,5},{1,4},{2,7},{3,6},{4,1},{5,0},{6,3},{7,2},{8,13},{9,12},{10,... | collective-permute-start | bytes 1204232 | tf_op jit(solution)/shard_map/ppermute | solution.py:586
  805.3 84.6 %copy-start.23 = (s16[784,256]{1,0:T(8,128)(2,1)}, s16[784,256]{1,0:T(8,128)(2,1)S(1)}, u32[]{:S(2)}) copy-start(s16[784,256]{1,0:T(8,128)(2,1)S(1)} %collective-permute-done.35.refs_2_) | copy-start | bytes 1204228
  805.3 75.8 %collective-permute-start.40 = (s16[784,256]{1,0:T(8,128)(2,1)}, s16[784,256]{1,0:T(8,128)(2,1)}, u32[]{:S(2)}, u32[]{:S(2)}) collective-permute-start(s16[784,256]{1,0:T(8,128)(2,1)} %get-tuple-element.136), channel_id=1, source_target_pairs={{0,6},{1,7},{2,4},{3,5},{4,2},{5,3},{6,0},{7,1},{8,14},{9,15},{10,... | collective-permute-start | bytes 1204232 | tf_op jit(solution)/shard_map/ppermute | solution.py:586
  819.8 70.1 %copy-start.24 = (s16[784,256]{1,0:T(8,128)(2,1)}, s16[784,256]{1,0:T(8,128)(2,1)S(1)}, u32[]{:S(2)}) copy-start(s16[784,256]{1,0:T(8,128)(2,1)S(1)} %collective-permute-done.36.refs_3_) | copy-start | bytes 1204228
  819.8 70.1 %collective-permute-start.41 = (s16[784,256]{1,0:T(8,128)(2,1)}, s16[784,256]{1,0:T(8,128)(2,1)}, u32[]{:S(2)}, u32[]{:S(2)}) collective-permute-start(s16[784,256]{1,0:T(8,128)(2,1)} %get-tuple-element.137), channel_id=1, source_target_pairs={{0,7},{1,6},{2,5},{3,4},{4,3},{5,2},{6,1},{7,0},{8,15},{9,14},{10,... | collective-permute-start | bytes 1204232 | tf_op jit(solution)/shard_map/ppermute | solution.py:586
  838.2 51.8 %copy-start.25 = (s16[784,256]{1,0:T(8,128)(2,1)}, s16[784,256]{1,0:T(8,128)(2,1)S(1)}, u32[]{:S(2)}) copy-start(s16[784,256]{1,0:T(8,128)(2,1)S(1)} %collective-permute-done.37.refs_4_) | copy-start | bytes 1204228
  838.8 51.1 %copy-start.26 = (s16[784,256]{1,0:T(8,128)(2,1)}, s16[784,256]{1,0:T(8,128)(2,1)S(1)}, u32[]{:S(2)}) copy-start(s16[784,256]{1,0:T(8,128)(2,1)S(1)} %collective-permute-done.38.refs_5_) | copy-start | bytes 1204228
  (26 other events, 408.1 us)
Sparse Core Ops, SparseCore 0:
  18.4 334.1 all-gather.2

commit v3 on v2

--- a/solution.py
+++ b/solution.py
@@ -59,8 +59,8 @@
         self.depth = nz // self.cuts
         self.lines = rows * parts
         self.scale_rows = -(-rows // 16) * 16
-        early = max(rows // 3, 1)
-        self.spans = ((0, early), (early, rows - early))
+        early = max(rows // 4, 1)
+        self.early, self.late = early, rows - early
 
     def rows_of(self, fields, rows=None):
         return fields * (rows or self.rows) * self.width
@@ -191,7 +191,7 @@
     return [each(plan, whole, blocks) for whole, blocks in zip(WHOLE, lists)], rest
 
 
-def explicit_kernel(plan, which, received, me_ref, *refs):
+def explicit_kernel(plan, late, received, me_ref, *refs):
     parts, nx = plan.parts, plan.nx
     if received:
         sources, refs = blockwise(plan, refs)
@@ -201,9 +201,15 @@
     refs = refs[4:]
     if received:
         base_dx_ref, base_dz_ref, refs = refs[0], refs[1], refs[2:]
-    whole, (above, rows) = WHOLE[which], plan.spans[which]
-    count = pieces(plan, whole)
-    outs, refs = each(plan, whole, refs[:count]), refs[count:]
+    if late:
+        above, rows, whole, groups = plan.early, plan.late, False, GROUPS
+    else:
+        above, rows, whole, groups = 0, plan.early, True, ((0, 1, 2),)
+    outs = []
+    for _ in groups:
+        count = pieces(plan, whole)
+        outs.append(each(plan, whole, refs[:count]))
+        refs = refs[count:]
     if not received:
         base_dx_ref, base_dz_ref, refs = refs[0], refs[1], refs[2:]
     speed, term, codes = refs[:3]
@@ -242,15 +248,17 @@
         values = [term[c, along, across] for c in range(3)]
         code = scale_code(column_max(values))
         factor = encode(code)
-        for c, value in enumerate(values):
-            start = pl.multiple_of((c * rows + row) * plan.width, plan.width)
-            outs[d][pl.ds(start, plan.width), :] = to_short(value * factor)
+        for group, blocks in zip(groups, outs):
+            for k, c in enumerate(group):
+                start = pl.multiple_of((k * rows + row) * plan.width, plan.width)
+                blocks[d][pl.ds(start, plan.width), :] = to_short(values[c] * factor)
         codes[d, pl.ds(row, 1), :] = code
 
     @pl.when(row == rows - 1)
     def _():
         for d in range(parts):
-            outs[d][plan.rows_of(3, rows) :, :] = codes[d].astype(jnp.int32).astype(jnp.int16)
+            shorts = codes[d].astype(jnp.int32).astype(jnp.int16)
+            outs[0][d][plan.rows_of(len(groups[0]), rows) :, :] = shorts
 
 
 def whole_blocks(plan):
@@ -262,11 +270,15 @@
     return specs
 
 
-def explicit(plan, which, me, velocity, flow, shear, dx, dz, bases=None):
+def explicit(plan, late, me, velocity, flow, shear, dx, dz, bases=None):
     received = bases is not None
     parts = plan.parts
-    whole, (above, rows) = WHOLE[which], plan.spans[which]
-    height = plan.rows_of(3, rows) + plan.scale_rows
+    if late:
+        above, rows, whole = plan.early, plan.late, False
+        heights = [plan.rows_of(len(group), rows) for group in GROUPS]
+    else:
+        above, rows, whole, heights = 0, plan.early, True, [plan.rows_of(3, plan.early)]
+    heights[0] += plan.scale_rows
     block = (3, 1, plan.nx, plan.nz)
     field = pl.BlockSpec(block, lambda j, *_: (0, above + j, 0, 0))
     own = pl.BlockSpec(block, lambda j, *_: (0, j, 0, 0))
@@ -275,8 +287,10 @@
         pltpu.VMEM((3, plan.nx, plan.nz), F32),
         pltpu.VMEM((parts, plan.scale_rows, plan.depth), F32),
     ]
-    out_specs = block_specs(plan, whole, height, plan.depth, lambda j: 0)
-    out_shape = block_shapes(plan, whole, height)
+    out_specs, out_shape = [], []
+    for height in heights:
+        out_specs += block_specs(plan, whole, height, plan.depth, lambda j: 0)
+        out_shape += block_shapes(plan, whole, height)
     if received:
         first, more = whole_blocks(plan), [own, own]
         velocity = flat(velocity)
@@ -286,7 +300,7 @@
         out_specs += [own, own]
         out_shape += [jax.ShapeDtypeStruct((3, rows, plan.nx, plan.nz), F32)] * 2
     results = pl.pallas_call(
-        functools.partial(explicit_kernel, plan, which, received),
+        functools.partial(explicit_kernel, plan, late, received),
         grid_spec=pltpu.PrefetchScalarGridSpec(
             num_scalar_prefetch=1,
             grid=(rows,),
@@ -309,7 +323,8 @@
         name="explicit",
     )(me, *velocity, flow, shear, dx, dz, *bases)
     count = pieces(plan, whole)
-    return exchange(plan, whole, results[:count]), results[count:]
+    blocks = [list(results[i * count : (i + 1) * count]) for i in range(len(heights))]
+    return blocks, results[count * len(heights) :]
 
 
 def stacked(matrices):
@@ -432,8 +447,9 @@
         table[...] = stacked(tables)
         codes[...] = jnp.zeros_like(codes)
 
-    for g in range(len(WHOLE)):
-        unpack_lines(plan, WHOLE[g], me, plan.spans[g], values[g], scales[g], field)
+    spans = ((0, plan.early), (plan.early, plan.late))
+    for kind, span, blocks, codings in zip((True, False), spans, values, scales):
+        unpack_lines(plan, kind, me, span, blocks, codings, field)
 
     def line(r, carry):
         here = pl.ds(r, lines, stride=plan.width)
@@ -479,11 +495,14 @@
     last = section == SECTIONS - 1
     height = plan.rows_of(len(group)) + 16
     skip = group[0] if right.shape[0] == 3 else 0
-    value_specs, scale_specs = [], []
-    for kind, (_, rows) in zip(WHOLE, plan.spans):
-        at = plan.rows_of(3, rows) // plan.scale_rows
-        value_specs += block_specs(plan, kind, plan.rows_of(1, rows), depth, lambda c: c + group[0])
-        scale_specs += block_specs(plan, kind, plan.scale_rows, depth, lambda c, at=at: at)
+    early, first_late, late = blocks
+    early_at = plan.rows_of(3, plan.early) // plan.scale_rows
+    late_at = plan.rows_of(len(GROUPS[0]), plan.late) // plan.scale_rows
+    rows = plan.rows_of(1, plan.early), plan.rows_of(1, plan.late)
+    value_specs = block_specs(plan, True, rows[0], depth, lambda c: c + group[0])
+    value_specs += block_specs(plan, False, rows[1], depth, lambda c: c)
+    scale_specs = block_specs(plan, True, plan.scale_rows, depth, lambda c: early_at)
+    scale_specs += block_specs(plan, False, plan.scale_rows, depth, lambda c: late_at)
     state_spec = pl.BlockSpec((1, width, lines, depth), lambda c, *_: (c, 0, 0, 0))
     read_spec = pl.BlockSpec((1, width, lines, depth), lambda c, *_: (c + skip, 0, 0, 0))
     in_specs = (
@@ -495,7 +514,7 @@
             read_spec,
         ]
     )
-    args = [me, *flat(blocks), *flat(blocks), wall, solves, right]
+    args = [me, *early, *late, *early, *first_late, wall, solves, right]
     out_specs = block_specs(plan, whole, height, depth, lambda c: 0)
     out_shape = block_shapes(plan, whole, height)
     copies = 2
@@ -535,44 +554,65 @@
     return results[:count], results[count:]
 
 
-def result_kernel(plan, me_ref, shift_ref, successor_ref, *refs):
-    sources, refs = blockwise(plan, refs)
-    follower_ref, out_ref, speed = refs[:3]
-    scales = refs[3:]
-    row = pl.program_id(0)
-
-    @pl.when(row == 0)
+def result_kernel(plan, group, whole, me_ref, shift_ref, successor_ref, *refs):
+    count = pieces(plan, whole)
+    blocks, refs = each(plan, whole, refs[:count]), refs[count:]
+    follower_ref, (out_ref, speed, factors) = refs[0], refs[-3:]
+    component, row = pl.program_id(0), pl.program_id(1)
+
+    @pl.when((component == 0) & (row == 0))
     def _():
-        prepare(plan, sources, scales)
-
-    receive(plan, me_ref[0], row, sources, scales, speed)
-    for c in range(3):
-        out_ref[c, 0] = pltpu.roll(speed[c], shift_ref[0], axis=1) - follower_ref[0, c, 0]
-
-
-def result(plan, me, shift, successor, blocks, tangents):
-    parts = plan.parts
-    block = (3, 1, plan.nx, plan.nz)
+        for d in range(plan.parts):
+            factors[d] = decode(from_short(blocks[d][plan.rows_of(len(group)) :, :]))
+
+    for d in range(plan.parts):
+        along, across = plan.piece(partner(whole, me_ref[0], d))
+        start = pl.multiple_of((component * plan.rows + row) * plan.width, plan.width)
+        value = from_short(blocks[d][pl.ds(start, plan.width), :])
+        speed[along, across] = value * factors[d, pl.ds(component, 1), :]
+    rolled = pltpu.roll(speed[...], shift_ref[0], axis=1)
+    out_ref[0, 0] = rolled - follower_ref[0, 0, 0]
+
+
+def result(plan, group, whole, me, shift, successor, blocks, tangents, before):
+    height = plan.rows_of(len(group)) + 16
+    specs = block_specs(
+        plan, whole, height, plan.depth, lambda c: 0, pipeline_mode=pl.Buffered(1)
+    )
+    specs.append(
+        pl.BlockSpec(
+            (1, 1, 1, plan.nx, plan.nz),
+            lambda c, j, me, shift, successor: (successor[0], c + group[0], j, 0, 0),
+        )
+    )
+    args = [me, shift, successor, *blocks, tangents]
+    aliases = {}
+    if before is not None:
+        specs.append(pl.BlockSpec(memory_space=pl.ANY))
+        aliases[len(args)] = 0
+        args.append(before)
     return pl.pallas_call(
-        functools.partial(result_kernel, plan),
+        functools.partial(result_kernel, plan, group, whole),
         grid_spec=pltpu.PrefetchScalarGridSpec(
             num_scalar_prefetch=3,
-            grid=(plan.rows,),
-            in_specs=whole_blocks(plan)
-            + [
-                pl.BlockSpec(
-                    (1, *block), lambda j, me, shift, successor: (successor[0], 0, j, 0, 0)
-                )
+            grid=(len(group), plan.rows),
+            in_specs=specs,
+            out_specs=pl.BlockSpec(
+                (1, 1, plan.nx, plan.nz), lambda c, j, *_: (c + group[0], j, 0, 0)
+            ),
+            scratch_shapes=[
+                pltpu.VMEM((plan.nx, plan.nz), F32),
+                pltpu.VMEM((plan.parts, 16, plan.depth), F32),
             ],
-            out_specs=pl.BlockSpec(block, lambda j, *_: (0, j, 0, 0)),
-            scratch_shapes=[pltpu.VMEM((3, plan.nx, plan.nz), F32)]
-            + [pltpu.VMEM((parts, 16, plan.depth), F32)] * len(GROUPS),
         ),
         out_shape=jax.ShapeDtypeStruct((3, plan.rows, plan.nx, plan.nz), F32),
+        input_output_aliases=aliases,
         compiler_params=pltpu.CompilerParams(vmem_limit_bytes=VMEM_LIMIT),
-        cost_estimate=pl.CostEstimate(flops=0, transcendentals=0, bytes_accessed=25_000_000),
+        cost_estimate=pl.CostEstimate(
+            flops=0, transcendentals=0, bytes_accessed=8_000_000 * len(group)
+        ),
         name="result",
-    )(me, shift, successor, *flat(blocks), tangents)
+    )(*args)
 
 
 def exchange(plan, whole, blocks):
@@ -602,9 +642,13 @@
     later, start, following = lax.optimization_barrier((me, start, tangent))
     tangents = lax.all_gather(following, "seg")
     (start,) = exchange(plan, True, [start])
-    term, bases = zip(
-        *(explicit(plan, i, later, tangent, flow, shear, dx, dz) for i in range(len(WHOLE)))
-    )
+    bases = []
+    early, base = explicit(plan, False, later, tangent, flow, shear, dx, dz)
+    bases.append(base)
+    late, base = explicit(plan, True, later, tangent, flow, shear, dx, dz)
+    bases.append(base)
+    early[0][0], late[0][0] = lax.optimization_barrier((early[0][0], late[0][0]))
+    term = [exchange(plan, True, early[0]), [exchange(plan, False, blocks) for blocks in late]]
     right, turned, wall_flow = first_lines(plan, start, wall_derivative)
     states = [(right, turned) for _ in GROUPS]
     for section in range(SECTIONS):
@@ -616,19 +660,24 @@
                 group,
                 whole,
                 me,
-                term,
+                [term[0], term[1][0], term[1][g]],
                 wall_derivative,
                 implicit_inverse,
                 *(states[g] if section < SECTIONS - 1 else (states[g][0], None)),
                 wall_flow,
             )
+            if g == 0:
+                blocks, term[1][1] = lax.optimization_barrier((blocks, term[1][1]))
             value.append(exchange(plan, whole, blocks))
         if section < SECTIONS - 1:
-            term = [
-                explicit(plan, i, me, value, flow, shear, dx, dz, bases[i])[0]
-                for i in range(len(WHOLE))
-            ]
-    return result(plan, me, spanwise_shift, ahead, value, tangents)[None]
+            early, _ = explicit(plan, False, me, value, flow, shear, dx, dz, bases[0])
+            early = exchange(plan, True, early[0])
+            late, _ = explicit(plan, True, me, value, flow, shear, dx, dz, bases[1])
+            term = [early, [exchange(plan, False, blocks) for blocks in late]]
+    out = None
+    for group, whole, blocks in zip(GROUPS, WHOLE, value):
+        out = result(plan, group, whole, me, spanwise_shift, ahead, blocks, tangents, out)
+    return out[None]
 
 
 def solution(mesh):

time: 915 us -> 898 us (0.981)
  waiting for transfers between devices: 574 us -> 519 us
  starting transfers between devices: 85.9 us -> 111 us
  Pallas kernels: 227 us -> 241 us
    ppermute x42 -> x63, waiting for transfers between devices: 447 us -> 410 us  [exchange(): lax.ppermute(blocks[d], 'grid', [(i, i ^ d) for i in range(parts)])]
    ppermute x42 -> x63, starting transfers between devices: 55 us -> 79.7 us  [exchange(): lax.ppermute(blocks[d], 'grid', [(i, i ^ d) for i in range(parts)])]
    all_to_all x7, waiting for transfers between devices: 128 us -> 109 us  [exchange(): lax.all_to_all(blocks[0], 'grid', split_axis=0, concat_axis=0, tiled=True)]
    pallas_call x7 -> x8, Pallas kernels: 93.6 us -> 108 us  [the longest x6 80.2 us: explicit(): pl.pallas_call(functools.partial(explicit_kernel, plan, late, received),...]
  transfers between devices with their start and end apart: 50 -> 71, of which waited for: 32 -> 40; matrix products, arithmetic and copies ran while one was open for 0% -> 0% of each run, Pallas kernels for 22% -> 24%
where the time goes in v3:
time: 898 us; the launch traced here: 896 us
  waiting for transfers between devices  519 us (58%)
  Pallas kernels  241 us (27%)
  starting transfers between devices  111 us (12%)
  between operations  14.7 us (2%)
  local copies, waits for them, and re-layouts  9.59 us (1%)
    ppermute x63, waiting for transfers between devices, exchange(): lax.ppermute(blocks[d], 'grid', [(i, i ^ d) for i in range(parts)])  410 us
    all_to_all x7, waiting for transfers between devices, exchange(): lax.all_to_all(blocks[0], 'grid', split_axis=0, concat_axis=0, tiled=True)  109 us
    pallas_call x6, Pallas kernels, advance_lines(): pl.pallas_call(functools.partial(lines_kernel, plan, section, group, whol...  100 us
    pallas_call x6, Pallas kernels, explicit(): pl.pallas_call(functools.partial(explicit_kernel, plan, late, received),...  80.2 us
    ppermute x63, starting transfers between devices, exchange(): lax.ppermute(blocks[d], 'grid', [(i, i ^ d) for i in range(parts)])  79.7 us
    all_to_all x7, starting transfers between devices, exchange(): lax.all_to_all(blocks[0], 'grid', split_axis=0, concat_axis=0, tiled=True)  30.9 us
    pallas_call x2, Pallas kernels, result(): pl.pallas_call(functools.partial(result_kernel, plan, group, whole), grid...  27.6 us
    pallas_call x1, Pallas kernels, first_lines(): pl.pallas_call(functools.partial(first_lines_kernel, plan), grid=(3,), in...  21.4 us
  transfers between devices with their start and end apart: 71, of which 40 were waited for; matrix products, arithmetic and copies ran while one was open for 0% of the time, Pallas kernels for 24%

profile of v3, /device:TPU:9, one launch (start us, length us, event | category | flops | bytes accessed | tf_op | source)
XLA Modules:
  0.0 895.6 jit_solution(9430301266652777895)
XLA Ops:
  6.5 11.7 %pack_start.1 = s16[8,1568,256]{2,1,0:T(8,128)(2,1)} custom-call(f32[3,12,256,256]{3,2,1,0:T(8,128)} %bitcast.8, bf16[3,12,256,256]{3,2,1,0:T(8,128)(2,1)} %bitcast.12), custom_call_target="tpu_custom_call" | custom-call | bytes 20000000 | tf_op jit(solution)/shard_map/pack_start/pallas_call | solution.py:125
  18.3 5.7 all-to-all-start.1
  24.0 8.7 explicit.6
  32.6 20.4 %explicit.7 = (s16[304,256]{1,0:T(8,128)(2,1)}, s16[304,256]{1,0:T(8,128)(2,1)}, s16[304,256]{1,0:T(8,128)(2,1)}, s16[304,256]{1,0:T(8,128)(2,1)}, s16[304,256]{...) custom-call(s32[1]{0:T(128)} %bitcast.me_ref, ...), custom_call_target="tpu_custom_call" | custom-call | flops 8999999488 | bytes 36000000 | tf_op jit(solution)/shard_map/explicit/pallas_call | solution.py:302
  53.0 109.2 %all-to-all-done.1.refs_0_.refs_1_.refs_2_.refs_3_ = s16[8,1568,256]{2,1,0:T(8,128)(2,1)} async-done(((s16[8,1568,256]{2,1,0:T(8,128)(2,1)}), s16[8,1568,256]{2,1,0:T(8,128)(2,1)}, u32[]{:S(2)}, u32[]{:S(2)}) %all-to-all-start.1) | async-done | bytes 6422560 | tf_op jit(solution)/shard_map/all_to_all | solution.py:620
  162.2 7.1 all-to-all-start
  173.8 2.6 collective-permute-start.11
  176.5 17.7 %collective-permute-done.1.refs_3_.refs_12_ = s16[304,256]{1,0:T(8,128)(2,1)S(1)} collective-permute-done((s16[304,256]{1,0:T(8,128)(2,1)}, s16[304,256]{1,0:T(8,128)(2,1)S(1)}, u32[]{:S(2)}, u32[]{:S(2)}) %collective-permute-start.1) | collective-permute-done | bytes 155680 | tf_op jit(solution)/shard_map/ppermute | solution.py:626
  200.5 22.1 %collective-permute-done.3.refs_5_.refs_14_ = s16[304,256]{1,0:T(8,128)(2,1)S(1)} collective-permute-done((s16[304,256]{1,0:T(8,128)(2,1)}, s16[304,256]{1,0:T(8,128)(2,1)S(1)}, u32[]{:S(2)}, u32[]{:S(2)}) %collective-permute-start.3) | collective-permute-done | bytes 155680 | tf_op jit(solution)/shard_map/ppermute | solution.py:626
  224.7 17.1 %collective-permute-done.4.refs_6_.refs_15_ = s16[304,256]{1,0:T(8,128)(2,1)S(1)} collective-permute-done((s16[304,256]{1,0:T(8,128)(2,1)}, s16[304,256]{1,0:T(8,128)(2,1)S(1)}, u32[]{:S(2)}, u32[]{:S(2)}) %collective-permute-start.4) | collective-permute-done | bytes 155680 | tf_op jit(solution)/shard_map/ppermute | solution.py:626
  242.8 4.1 collective-permute-done.5.refs_7_.refs_16_
  247.7 16.1 %collective-permute-done.6.refs_8_.refs_17_ = s16[304,256]{1,0:T(8,128)(2,1)S(1)} collective-permute-done((s16[304,256]{1,0:T(8,128)(2,1)}, s16[304,256]{1,0:T(8,128)(2,1)S(1)}, u32[]{:S(2)}, u32[]{:S(2)}) %collective-permute-start.6) | collective-permute-done | bytes 155680 | tf_op jit(solution)/shard_map/ppermute | solution.py:626
  266.0 21.4 %first_lines.1 = (f32[3,32,96,256]{3,2,1,0:T(8,128)}, f32[3,32,96,256]{3,2,1,0:T(8,128)}, f32[32,96,256]{2,1,0:T(8,128)}) custom-call(s16[8,1568,256]{2,1,0:T(8,128)(2,1)} %all-to-all-done.1.refs_0_.refs_1_.refs_2_.refs_3_, s16[8,1568,256]{2,1,0:T(8,128)(2,1)} %all-to-all-done.1.refs_0_.refs_1_.refs_2_.refs_3_, ...), custom_call_target="tpu_custom_call" | custom-call | flops 1000000000 | bytes 30000000 | tf_op jit(solution)/shard_map/first_lines/pallas_call | solution.py:400
  288.6 14.3 %advance_lines.6 = (s16[8,400,256]{2,1,0:T(8,128)(2,1)}, f32[1,32,96,256]{3,2,1,0:T(8,128)}, f32[1,32,96,256]{3,2,1,0:T(8,128)}) custom-call(s32[1]{0:T(128)} %bitcast.me_ref, s16[8,304,256]{2,1,0:T(8,128)(2,1)} %copy-done.2, s16[304,256]{1,0:T(8,128)(2,1)} %get-tuple-element.129.refs_1_.refs_10_, s16[304,256]{1,0:T(8,128)(2,1)} %copy-done.20, ...), custom_call_target="tpu_custom_call" | custom-call | flops 700000000 | bytes 17000000 | tf_op jit(solution)/shard_map/advance_lines/pallas_call | solution.py:531
  303.6 3.7 all-to-all-start.2
  307.3 22.5 %advance_lines.7 = (s16[784,256]{1,0:T(8,128)(2,1)}, s16[784,256]{1,0:T(8,128)(2,1)}, s16[784,256]{1,0:T(8,128)(2,1)}, s16[784,256]{1,0:T(8,128)(2,1)}, s16[784,...) custom-call(s32[1]{0:T(128)} %bitcast.me_ref, ...), custom_call_target="tpu_custom_call" | custom-call | flops 1400000000 | bytes 34000000 | tf_op jit(solution)/shard_map/advance_lines/pallas_call | solution.py:531
  335.7 19.6 %collective-permute-done.15.refs_3_ = s16[784,256]{1,0:T(8,128)(2,1)S(1)} collective-permute-done((s16[784,256]{1,0:T(8,128)(2,1)}, s16[784,256]{1,0:T(8,128)(2,1)S(1)}, u32[]{:S(2)}, u32[]{:S(2)}) %collective-permute-start.15) | collective-permute-done | bytes 401440 | tf_op jit(solution)/shard_map/ppermute | solution.py:626
  357.9 6.0 collective-permute-done.16.refs_4_
  363.9 30.7 %collective-permute-done.18.refs_6_ = s16[784,256]{1,0:T(8,128)(2,1)S(1)} collective-permute-done((s16[784,256]{1,0:T(8,128)(2,1)}, s16[784,256]{1,0:T(8,128)(2,1)S(1)}, u32[]{:S(2)}, u32[]{:S(2)}) %collective-permute-start.18) | collective-permute-done | bytes 401440 | tf_op jit(solution)/shard_map/ppermute | solution.py:626
  394.6 10.2 %collective-permute-done.19.refs_7_ = s16[784,256]{1,0:T(8,128)(2,1)S(1)} collective-permute-done((s16[784,256]{1,0:T(8,128)(2,1)}, s16[784,256]{1,0:T(8,128)(2,1)S(1)}, u32[]{:S(2)}, u32[]{:S(2)}) %collective-permute-start.19) | collective-permute-done | bytes 401440 | tf_op jit(solution)/shard_map/ppermute | solution.py:626
  405.5 8.1 collective-permute-done.20.refs_8_
  414.9 8.1 explicit.8
  423.0 3.5 all-to-all-start.3
  426.5 17.5 %explicit.9 = (s16[304,256]{1,0:T(8,128)(2,1)}, s16[304,256]{1,0:T(8,128)(2,1)}, s16[304,256]{1,0:T(8,128)(2,1)}, s16[304,256]{1,0:T(8,128)(2,1)}, s16[304,256]{...) custom-call(s32[1]{0:T(128)} %bitcast.me_ref, ...), custom_call_target="tpu_custom_call" | custom-call | flops 8999999488 | bytes 36000000 | tf_op jit(solution)/shard_map/explicit/pallas_call | solution.py:302
  451.1 7.4 collective-permute-start.25
  460.3 6.1 collective-permute-start.27
  466.4 3.3 collective-permute-done.25.refs_6_.refs_15_
  469.8 8.6 collective-permute-done.26.refs_7_.refs_16_
  478.3 17.2 %collective-permute-done.27.refs_8_.refs_17_ = s16[304,256]{1,0:T(8,128)(2,1)S(1)} collective-permute-done((s16[304,256]{1,0:T(8,128)(2,1)}, s16[304,256]{1,0:T(8,128)(2,1)S(1)}, u32[]{:S(2)}, u32[]{:S(2)}) %collective-permute-start.27) | collective-permute-done | bytes 155680 | tf_op jit(solution)/shard_map/ppermute | solution.py:626
  496.9 14.3 %advance_lines.8 = (s16[8,400,256]{2,1,0:T(8,128)(2,1)}, f32[1,32,96,256]{3,2,1,0:T(8,128)}, f32[1,32,96,256]{3,2,1,0:T(8,128)}) custom-call(s32[1]{0:T(128)} %bitcast.me_ref, s16[8,304,256]{2,1,0:T(8,128)(2,1)} %copy-done, s16[304,256]{1,0:T(8,128)(2,1)} %get-tuple-element.171.refs_1_.refs_10_, s16[304,256]{1,0:T(8,128)(2,1)} %copy-done.6, ...), custom_call_target="tpu_custom_call" | custom-call | flops 700000000 | bytes 17000000 | tf_op jit(solution)/shard_map/advance_lines/pallas_call | solution.py:531
  511.2 6.3 collective-permute-done.32.refs_6_
  517.5 8.5 collective-permute-done.33.refs_7_
  526.0 6.8 collective-permute-done.34.refs_8_
  532.8 3.8 all-to-all-start.4
  536.6 22.7 %advance_lines.9 = (s16[784,256]{1,0:T(8,128)(2,1)}, s16[784,256]{1,0:T(8,128)(2,1)}, s16[784,256]{1,0:T(8,128)(2,1)}, s16[784,256]{1,0:T(8,128)(2,1)}, s16[784,...) custom-call(s32[1]{0:T(128)} %bitcast.me_ref, ...), custom_call_target="tpu_custom_call" | custom-call | flops 1400000000 | bytes 34000000 | tf_op jit(solution)/shard_map/advance_lines/pallas_call | solution.py:531
  564.5 19.5 %collective-permute-done.36.refs_3_ = s16[784,256]{1,0:T(8,128)(2,1)S(1)} collective-permute-done((s16[784,256]{1,0:T(8,128)(2,1)}, s16[784,256]{1,0:T(8,128)(2,1)S(1)}, u32[]{:S(2)}, u32[]{:S(2)}) %collective-permute-start.36) | collective-permute-done | bytes 401440 | tf_op jit(solution)/shard_map/ppermute | solution.py:626
  584.0 2.6 collective-permute-start.41
  586.7 6.0 collective-permute-done.37.refs_4_
  592.6 30.6 %collective-permute-done.39.refs_6_ = s16[784,256]{1,0:T(8,128)(2,1)S(1)} collective-permute-done((s16[784,256]{1,0:T(8,128)(2,1)}, s16[784,256]{1,0:T(8,128)(2,1)S(1)}, u32[]{:S(2)}, u32[]{:S(2)}) %collective-permute-start.39) | collective-permute-done | bytes 401440 | tf_op jit(solution)/shard_map/ppermute | solution.py:626
  623.2 10.1 %collective-permute-done.40.refs_7_ = s16[784,256]{1,0:T(8,128)(2,1)S(1)} collective-permute-done((s16[784,256]{1,0:T(8,128)(2,1)}, s16[784,256]{1,0:T(8,128)(2,1)S(1)}, u32[]{:S(2)}, u32[]{:S(2)}) %collective-permute-start.40) | collective-permute-done | bytes 401440 | tf_op jit(solution)/shard_map/ppermute | solution.py:626
  634.1 8.1 collective-permute-done.41.refs_8_
  643.4 8.1 explicit.10
  651.5 3.5 all-to-all-start.5
  655.1 17.4 %explicit.11 = (s16[304,256]{1,0:T(8,128)(2,1)}, s16[304,256]{1,0:T(8,128)(2,1)}, s16[304,256]{1,0:T(8,128)(2,1)}, s16[304,256]{1,0:T(8,128)(2,1)}, s16[304,256]...) custom-call(s32[1]{0:T(128)} %bitcast.me_ref, ...), custom_call_target="tpu_custom_call" | custom-call | flops 8999999488 | bytes 36000000 | tf_op jit(solution)/shard_map/explicit/pallas_call | solution.py:302
  679.7 7.3 collective-permute-start.46
  689.0 6.0 collective-permute-start.48
  694.9 3.5 collective-permute-done.46.refs_6_.refs_15_
  698.5 8.5 collective-permute-done.47.refs_7_.refs_16_
  707.0 17.2 %collective-permute-done.48.refs_8_.refs_17_ = s16[304,256]{1,0:T(8,128)(2,1)S(1)} collective-permute-done((s16[304,256]{1,0:T(8,128)(2,1)}, s16[304,256]{1,0:T(8,128)(2,1)S(1)}, u32[]{:S(2)}, u32[]{:S(2)}) %collective-permute-start.48) | collective-permute-done | bytes 155680 | tf_op jit(solution)/shard_map/ppermute | solution.py:626
  725.4 9.9 %advance_lines.10 = s16[8,400,256]{2,1,0:T(8,128)(2,1)} custom-call(s32[1]{0:T(128)} %bitcast.me_ref, s16[8,304,256]{2,1,0:T(8,128)(2,1)} %copy-done.1, s16[304,256]{1,0:T(8,128)(2,1)} %get-tuple-element.209.refs_1_.refs_10_, s16[304,256]{1,0:T(8,128)(2,1)} %copy-done.10, s16[304,256]{1,0:T(8,128)(2,1)} %copy-done.11, s16[304,256]{1,0:T(8,128)(2,1)} %copy-done.12, ...), custom_call_target="tpu_custom_call" | custom-call | flops 700000000 | bytes 17000000 | tf_op jit(solution)/shard_map/advance_lines/pallas_call | solution.py:531
  735.3 4.5 collective-permute-done.52.refs_5_
  739.8 6.3 collective-permute-done.53.refs_6_
  746.1 8.5 collective-permute-done.54.refs_7_
  754.6 6.8 collective-permute-done.55.refs_8_
  761.4 3.5 all-to-all-start.6
  765.0 16.7 %advance_lines.11 = (s16[784,256]{1,0:T(8,128)(2,1)}, s16[784,256]{1,0:T(8,128)(2,1)}, s16[784,256]{1,0:T(8,128)(2,1)}, s16[784,256]{1,0:T(8,128)(2,1)}, s16[784...) custom-call(s32[1]{0:T(128)} %bitcast.me_ref, ...), custom_call_target="tpu_custom_call" | custom-call | flops 1400000000 | bytes 34000000 | tf_op jit(solution)/shard_map/advance_lines/pallas_call | solution.py:531
  787.2 13.6 %collective-permute-done.57.refs_2_ = s16[784,256]{1,0:T(8,128)(2,1)S(1)} collective-permute-done((s16[784,256]{1,0:T(8,128)(2,1)}, s16[784,256]{1,0:T(8,128)(2,1)S(1)}, u32[]{:S(2)}, u32[]{:S(2)}) %collective-permute-start.57) | collective-permute-done | bytes 401440 | tf_op jit(solution)/shard_map/ppermute | solution.py:626
  800.8 3.3 collective-permute-start.62
  806.5 9.8 %result.2.refs_9_ = f32[3,12,256,256]{3,2,1,0:T(8,128)} custom-call(s32[1]{0:T(128)} %bitcast.me_ref, s32[1]{0:T(128)S(6)} %copy.12.shift_ref, s32[1]{0:T(128)} %dynamic_slice.3.successor_ref, s16[8,400,256]{2,1,0:T(8,128)(2,1)} %copy-done.5, f32[4,3,12,256,256]{4,3,2,1,0:T(8,128)} %bitcast.6), custom_call_target="tpu_custom_call" | custom-call | bytes 8000000 | tf_op jit(solution)/shard_map/result/pallas_call | solution.py:594
  816.3 2.7 collective-permute-done.58.refs_3_
  819.8 32.1 %collective-permute-done.60.refs_5_ = s16[784,256]{1,0:T(8,128)(2,1)} collective-permute-done((s16[784,256]{1,0:T(8,128)(2,1)}, s16[784,256]{1,0:T(8,128)(2,1)}, u32[]{:S(2)}, u32[]{:S(2)}) %collective-permute-start.60) | collective-permute-done | bytes 401440 | tf_op jit(solution)/shard_map/ppermute | solution.py:626
  851.8 10.3 %collective-permute-done.61.refs_6_ = s16[784,256]{1,0:T(8,128)(2,1)} collective-permute-done((s16[784,256]{1,0:T(8,128)(2,1)}, s16[784,256]{1,0:T(8,128)(2,1)}, u32[]{:S(2)}, u32[]{:S(2)}) %collective-permute-start.61) | collective-permute-done | bytes 401440 | tf_op jit(solution)/shard_map/ppermute | solution.py:626
  862.1 8.8 collective-permute-done.62.refs_7_
  870.9 17.8 %result.3 = f32[3,12,256,256]{3,2,1,0:T(8,128)} custom-call(s32[1]{0:T(128)} %bitcast.me_ref, s32[1]{0:T(128)S(6)} %copy.12.shift_ref, s32[1]{0:T(128)} %dynamic_slice.3.successor_ref, s16[784,256]{1,0:T(8,128)(2,1)} %get-tuple-element.235.refs_0_, s16[784,256]{1,0:T(8,128)(2,1)} %copy-done.27, ...), custom_call_target="tpu_custom_call", output_to_operand_aliasing={{}: (12, {})} | custom-call | bytes 16000000 | tf_op jit(solution)/shard_map/result/pallas_call | solution.py:594
  (202 shorter events, 64.8 us)
Async XLA Ops:
  6.5 798.8 %all-gather.3.cloned.1.call-start = ((), (), s32[]{:S(2)}) async-start(), calls=%async_computation.7 | async-start | bytes 47185920 | tf_op jit(solution)/shard_map/all_gather | solution.py:643
  18.3 143.9 %all-to-all-start.1 = ((s16[8,1568,256]{2,1,0:T(8,128)(2,1)}), s16[8,1568,256]{2,1,0:T(8,128)(2,1)}, u32[]{:S(2)}, u32[]{:S(2)}) async-start(s16[8,1568,256]{2,1,0:T(8,128)(2,1)} %pack_start.1), calls=%async_computation.1 | async-start | bytes 12845056 | tf_op jit(solution)/shard_map/all_to_all | solution.py:620
  162.2 125.3 %all-to-all-start = ((s16[8,304,256]{2,1,0:T(8,128)(2,1)}), s16[8,304,256]{2,1,0:T(8,128)(2,1)S(1)}, u32[]{:S(2)}, u32[]{:S(2)}) async-start(s16[8,304,256]{2,1,0:T(8,128)(2,1)} %get-tuple-element.128), calls=%async_computation | async-start | bytes 2490368 | tf_op jit(solution)/shard_map/all_to_all | solution.py:620
  169.7 24.5 %collective-permute-start.1 = (s16[304,256]{1,0:T(8,128)(2,1)}, s16[304,256]{1,0:T(8,128)(2,1)S(1)}, u32[]{:S(2)}, u32[]{:S(2)}) collective-permute-start(s16[304,256]{1,0:T(8,128)(2,1)} %get-tuple-element.131), channel_id=1, source_target_pairs={{0,2},{1,3},{2,0},{3,1},{4,6},{5,7},{6,4},{7,5},{8,10},{9,11},{10,... | collective-permute-start | bytes 466952 | tf_op jit(solution)/shard_map/ppermute | solution.py:626
  169.7 28.3 %collective-permute-start.2 = (s16[304,256]{1,0:T(8,128)(2,1)}, s16[304,256]{1,0:T(8,128)(2,1)S(1)}, u32[]{:S(2)}, u32[]{:S(2)}) collective-permute-start(s16[304,256]{1,0:T(8,128)(2,1)} %get-tuple-element.132), channel_id=1, source_target_pairs={{0,3},{1,2},{2,1},{3,0},{4,7},{5,6},{6,5},{7,4},{8,11},{9,10},{10,... | collective-permute-start | bytes 466952 | tf_op jit(solution)/shard_map/ppermute | solution.py:626
  171.5 51.1 %collective-permute-start.3 = (s16[304,256]{1,0:T(8,128)(2,1)}, s16[304,256]{1,0:T(8,128)(2,1)S(1)}, u32[]{:S(2)}, u32[]{:S(2)}) collective-permute-start(s16[304,256]{1,0:T(8,128)(2,1)} %get-tuple-element.133), channel_id=1, source_target_pairs={{0,4},{1,5},{2,6},{3,7},{4,0},{5,1},{6,2},{7,3},{8,12},{9,13},{10,... | collective-permute-start | bytes 466952 | tf_op jit(solution)/shard_map/ppermute | solution.py:626
  173.6 90.3 %collective-permute-start.10 = (s16[576,256]{1,0:T(8,128)(2,1)}, s16[576,256]{1,0:T(8,128)(2,1)S(1)}, u32[]{:S(2)}, u32[]{:S(2)}) collective-permute-start(s16[576,256]{1,0:T(8,128)(2,1)} %get-tuple-element.146), channel_id=1, source_target_pairs={{0,4},{1,5},{2,6},{3,7},{4,0},{5,1},{6,2},{7,3},{8,12},{9,13},{10,... | collective-permute-start | bytes 884744 | tf_op jit(solution)/shard_map/ppermute | solution.py:626
  173.8 90.1 %collective-permute-start.11 = (s16[576,256]{1,0:T(8,128)(2,1)}, s16[576,256]{1,0:T(8,128)(2,1)S(1)}, u32[]{:S(2)}, u32[]{:S(2)}) collective-permute-start(s16[576,256]{1,0:T(8,128)(2,1)} %get-tuple-element.147), channel_id=1, source_target_pairs={{0,5},{1,4},{2,7},{3,6},{4,1},{5,0},{6,3},{7,2},{8,13},{9,12},{10,... | collective-permute-start | bytes 884744 | tf_op jit(solution)/shard_map/ppermute | solution.py:626
  194.1 47.8 %collective-permute-start.4 = (s16[304,256]{1,0:T(8,128)(2,1)}, s16[304,256]{1,0:T(8,128)(2,1)S(1)}, u32[]{:S(2)}, u32[]{:S(2)}) collective-permute-start(s16[304,256]{1,0:T(8,128)(2,1)} %get-tuple-element.134), channel_id=1, source_target_pairs={{0,5},{1,4},{2,7},{3,6},{4,1},{5,0},{6,3},{7,2},{8,13},{9,12},{10,... | collective-permute-start | bytes 466952 | tf_op jit(solution)/shard_map/ppermute | solution.py:626
  197.9 49.0 %collective-permute-start.5 = (s16[304,256]{1,0:T(8,128)(2,1)}, s16[304,256]{1,0:T(8,128)(2,1)S(1)}, u32[]{:S(2)}, u32[]{:S(2)}) collective-permute-start(s16[304,256]{1,0:T(8,128)(2,1)} %get-tuple-element.135), channel_id=1, source_target_pairs={{0,6},{1,7},{2,4},{3,5},{4,2},{5,3},{6,0},{7,1},{8,14},{9,15},{10,... | collective-permute-start | bytes 466952 | tf_op jit(solution)/shard_map/ppermute | solution.py:626
  222.6 41.2 %collective-permute-start.6 = (s16[304,256]{1,0:T(8,128)(2,1)}, s16[304,256]{1,0:T(8,128)(2,1)S(1)}, u32[]{:S(2)}, u32[]{:S(2)}) collective-permute-start(s16[304,256]{1,0:T(8,128)(2,1)} %get-tuple-element.136), channel_id=1, source_target_pairs={{0,7},{1,6},{2,5},{3,4},{4,3},{5,2},{6,1},{7,0},{8,15},{9,14},{10,... | collective-permute-start | bytes 466952 | tf_op jit(solution)/shard_map/ppermute | solution.py:626
  241.9 61.0 %collective-permute-start.12 = (s16[576,256]{1,0:T(8,128)(2,1)}, s16[576,256]{1,0:T(8,128)(2,1)S(1)}, u32[]{:S(2)}, u32[]{:S(2)}) collective-permute-start(s16[576,256]{1,0:T(8,128)(2,1)} %get-tuple-element.148), channel_id=1, source_target_pairs={{0,6},{1,7},{2,4},{3,5},{4,2},{5,3},{6,0},{7,1},{8,14},{9,15},{10,... | collective-permute-start | bytes 884744 | tf_op jit(solution)/shard_map/ppermute | solution.py:626
  246.9 56.0 %collective-permute-start.13 = (s16[576,256]{1,0:T(8,128)(2,1)}, s16[576,256]{1,0:T(8,128)(2,1)}, u32[]{:S(2)}, u32[]{:S(2)}) collective-permute-start(s16[576,256]{1,0:T(8,128)(2,1)} %get-tuple-element.149), channel_id=1, source_target_pairs={{0,7},{1,6},{2,5},{3,4},{4,3},{5,2},{6,1},{7,0},{8,15},{9,14},{10,... | collective-permute-start | bytes 884744 | tf_op jit(solution)/shard_map/ppermute | solution.py:626
  263.8 39.1 %collective-permute-start.7 = (s16[576,256]{1,0:T(8,128)(2,1)}, s16[576,256]{1,0:T(8,128)(2,1)}, u32[]{:S(2)}, u32[]{:S(2)}) collective-permute-start(s16[576,256]{1,0:T(8,128)(2,1)} %get-tuple-element.143), channel_id=1, source_target_pairs={{0,1},{1,0},{2,3},{3,2},{4,5},{5,4},{6,7},{7,6},{8,9},{9,8},{10,11... | collective-permute-start | bytes 884744 | tf_op jit(solution)/shard_map/ppermute | solution.py:626
  263.8 39.1 %collective-permute-start.8 = (s16[576,256]{1,0:T(8,128)(2,1)}, s16[576,256]{1,0:T(8,128)(2,1)}, u32[]{:S(2)}, u32[]{:S(2)}) collective-permute-start(s16[576,256]{1,0:T(8,128)(2,1)} %get-tuple-element.144), channel_id=1, source_target_pairs={{0,2},{1,3},{2,0},{3,1},{4,6},{5,7},{6,4},{7,5},{8,10},{9,11},{10,... | collective-permute-start | bytes 884744 | tf_op jit(solution)/shard_map/ppermute | solution.py:626
  263.9 39.0 %collective-permute-start.9 = (s16[576,256]{1,0:T(8,128)(2,1)}, s16[576,256]{1,0:T(8,128)(2,1)}, u32[]{:S(2)}, u32[]{:S(2)}) collective-permute-start(s16[576,256]{1,0:T(8,128)(2,1)} %get-tuple-element.145), channel_id=1, source_target_pairs={{0,3},{1,2},{2,1},{3,0},{4,7},{5,6},{6,5},{7,4},{8,11},{9,10},{10,... | collective-permute-start | bytes 884744 | tf_op jit(solution)/shard_map/ppermute | solution.py:626
  303.6 110.1 %all-to-all-start.2 = ((s16[8,400,256]{2,1,0:T(8,128)(2,1)}), s16[8,400,256]{2,1,0:T(8,128)(2,1)S(1)}, u32[]{:S(2)}, u32[]{:S(2)}) async-start(s16[8,400,256]{2,1,0:T(8,128)(2,1)} %get-tuple-element.150), calls=%async_computation.2 | async-start | bytes 3276800 | tf_op jit(solution)/shard_map/all_to_all | solution.py:620
  330.1 25.2 %collective-permute-start.15 = (s16[784,256]{1,0:T(8,128)(2,1)}, s16[784,256]{1,0:T(8,128)(2,1)S(1)}, u32[]{:S(2)}, u32[]{:S(2)}) collective-permute-start(s16[784,256]{1,0:T(8,128)(2,1)} %get-tuple-element.161), channel_id=1, source_target_pairs={{0,2},{1,3},{2,0},{3,1},{4,6},{5,7},{6,4},{7,5},{8,10},{9,11},{10,... | collective-permute-start | bytes 1204232 | tf_op jit(solution)/shard_map/ppermute | solution.py:626
  330.2 33.7 %collective-permute-start.16 = (s16[784,256]{1,0:T(8,128)(2,1)}, s16[784,256]{1,0:T(8,128)(2,1)S(1)}, u32[]{:S(2)}, u32[]{:S(2)}) collective-permute-start(s16[784,256]{1,0:T(8,128)(2,1)} %get-tuple-element.162), channel_id=1, source_target_pairs={{0,3},{1,2},{2,1},{3,0},{4,7},{5,6},{6,5},{7,4},{8,11},{9,10},{10,... | collective-permute-start | bytes 1204232 | tf_op jit(solution)/shard_map/ppermute | solution.py:626
  332.0 31.9 %collective-permute-start.17 = (s16[784,256]{1,0:T(8,128)(2,1)}, s16[784,256]{1,0:T(8,128)(2,1)S(1)}, u32[]{:S(2)}, u32[]{:S(2)}) collective-permute-start(s16[784,256]{1,0:T(8,128)(2,1)} %get-tuple-element.163), channel_id=1, source_target_pairs={{0,4},{1,5},{2,6},{3,7},{4,0},{5,1},{6,2},{7,3},{8,12},{9,13},{10,... | collective-permute-start | bytes 1204232 | tf_op jit(solution)/shard_map/ppermute | solution.py:626
  334.0 60.6 %collective-permute-start.18 = (s16[784,256]{1,0:T(8,128)(2,1)}, s16[784,256]{1,0:T(8,128)(2,1)S(1)}, u32[]{:S(2)}, u32[]{:S(2)}) collective-permute-start(s16[784,256]{1,0:T(8,128)(2,1)} %get-tuple-element.164), channel_id=1, source_target_pairs={{0,5},{1,4},{2,7},{3,6},{4,1},{5,0},{6,3},{7,2},{8,13},{9,12},{10,... | collective-permute-start | bytes 1204232 | tf_op jit(solution)/shard_map/ppermute | solution.py:626
  334.5 70.3 %collective-permute-start.19 = (s16[784,256]{1,0:T(8,128)(2,1)}, s16[784,256]{1,0:T(8,128)(2,1)S(1)}, u32[]{:S(2)}, u32[]{:S(2)}) collective-permute-start(s16[784,256]{1,0:T(8,128)(2,1)} %get-tuple-element.165), channel_id=1, source_target_pairs={{0,6},{1,7},{2,4},{3,5},{4,2},{5,3},{6,0},{7,1},{8,14},{9,15},{10,... | collective-permute-start | bytes 1204232 | tf_op jit(solution)/shard_map/ppermute | solution.py:626
  355.3 58.4 %collective-permute-start.20 = (s16[784,256]{1,0:T(8,128)(2,1)}, s16[784,256]{1,0:T(8,128)(2,1)}, u32[]{:S(2)}, u32[]{:S(2)}) collective-permute-start(s16[784,256]{1,0:T(8,128)(2,1)} %get-tuple-element.166), channel_id=1, source_target_pairs={{0,7},{1,6},{2,5},{3,4},{4,3},{5,2},{6,1},{7,0},{8,15},{9,14},{10,... | collective-permute-start | bytes 1204232 | tf_op jit(solution)/shard_map/ppermute | solution.py:626
  423.0 72.7 %all-to-all-start.3 = ((s16[8,304,256]{2,1,0:T(8,128)(2,1)}), s16[8,304,256]{2,1,0:T(8,128)(2,1)S(1)}, u32[]{:S(2)}, u32[]{:S(2)}) async-start(s16[8,304,256]{2,1,0:T(8,128)(2,1)} %explicit.8), calls=%async_computation.3 | async-start | bytes 2490368 | tf_op jit(solution)/shard_map/all_to_all | solution.py:620
  444.3 14.2 %collective-permute-start.23 = (s16[304,256]{1,0:T(8,128)(2,1)}, s16[304,256]{1,0:T(8,128)(2,1)S(1)}, u32[]{:S(2)}, u32[]{:S(2)}) collective-permute-start(s16[304,256]{1,0:T(8,128)(2,1)} %get-tuple-element.174), channel_id=1, source_target_pairs={{0,3},{1,2},{2,1},{3,0},{4,7},{5,6},{6,5},{7,4},{8,11},{9,10},{10,... | collective-permute-start | bytes 466952 | tf_op jit(solution)/shard_map/ppermute | solution.py:626
  446.2 14.1 %collective-permute-start.24 = (s16[304,256]{1,0:T(8,128)(2,1)}, s16[304,256]{1,0:T(8,128)(2,1)S(1)}, u32[]{:S(2)}, u32[]{:S(2)}) collective-permute-start(s16[304,256]{1,0:T(8,128)(2,1)} %get-tuple-element.175), channel_id=1, source_target_pairs={{0,4},{1,5},{2,6},{3,7},{4,0},{5,1},{6,2},{7,3},{8,12},{9,13},{10,... | collective-permute-start | bytes 466952 | tf_op jit(solution)/shard_map/ppermute | solution.py:626
  448.1 47.4 %collective-permute-start.28 = (s16[576,256]{1,0:T(8,128)(2,1)}, s16[576,256]{1,0:T(8,128)(2,1)S(1)}, u32[]{:S(2)}, u32[]{:S(2)}) collective-permute-start(s16[576,256]{1,0:T(8,128)(2,1)} %get-tuple-element.183), channel_id=1, source_target_pairs={{0,1},{1,0},{2,3},{3,2},{4,5},{5,4},{6,7},{7,6},{8,9},{9,8},{10,11... | collective-permute-start | bytes 884744 | tf_op jit(solution)/shard_map/ppermute | solution.py:626
  448.5 47.1 %collective-permute-start.29 = (s16[576,256]{1,0:T(8,128)(2,1)}, s16[576,256]{1,0:T(8,128)(2,1)S(1)}, u32[]{:S(2)}, u32[]{:S(2)}) collective-permute-start(s16[576,256]{1,0:T(8,128)(2,1)} %get-tuple-element.184), channel_id=1, source_target_pairs={{0,2},{1,3},{2,0},{3,1},{4,6},{5,7},{6,4},{7,5},{8,10},{9,11},{10,... | collective-permute-start | bytes 884744 | tf_op jit(solution)/shard_map/ppermute | solution.py:626
  451.1 18.7 %collective-permute-start.25 = (s16[304,256]{1,0:T(8,128)(2,1)}, s16[304,256]{1,0:T(8,128)(2,1)S(1)}, u32[]{:S(2)}, u32[]{:S(2)}) collective-permute-start(s16[304,256]{1,0:T(8,128)(2,1)} %get-tuple-element.176), channel_id=1, source_target_pairs={{0,5},{1,4},{2,7},{3,6},{4,1},{5,0},{6,3},{7,2},{8,13},{9,12},{10,... | collective-permute-start | bytes 466952 | tf_op jit(solution)/shard_map/ppermute | solution.py:626
  458.5 19.8 %collective-permute-start.26 = (s16[304,256]{1,0:T(8,128)(2,1)}, s16[304,256]{1,0:T(8,128)(2,1)S(1)}, u32[]{:S(2)}, u32[]{:S(2)}) collective-permute-start(s16[304,256]{1,0:T(8,128)(2,1)} %get-tuple-element.177), channel_id=1, source_target_pairs={{0,6},{1,7},{2,4},{3,5},{4,2},{5,3},{6,0},{7,1},{8,14},{9,15},{10,... | collective-permute-start | bytes 466952 | tf_op jit(solution)/shard_map/ppermute | solution.py:626
  460.3 35.2 %collective-permute-start.27 = (s16[304,256]{1,0:T(8,128)(2,1)}, s16[304,256]{1,0:T(8,128)(2,1)S(1)}, u32[]{:S(2)}, u32[]{:S(2)}) collective-permute-start(s16[304,256]{1,0:T(8,128)(2,1)} %get-tuple-element.178), channel_id=1, source_target_pairs={{0,7},{1,6},{2,5},{3,4},{4,3},{5,2},{6,1},{7,0},{8,15},{9,14},{10,... | collective-permute-start | bytes 466952 | tf_op jit(solution)/shard_map/ppermute | solution.py:626
  469.8 41.4 %collective-permute-start.30 = (s16[576,256]{1,0:T(8,128)(2,1)}, s16[576,256]{1,0:T(8,128)(2,1)S(1)}, u32[]{:S(2)}, u32[]{:S(2)}) collective-permute-start(s16[576,256]{1,0:T(8,128)(2,1)} %get-tuple-element.185), channel_id=1, source_target_pairs={{0,3},{1,2},{2,1},{3,0},{4,7},{5,6},{6,5},{7,4},{8,11},{9,10},{10,... | collective-permute-start | bytes 884744 | tf_op jit(solution)/shard_map/ppermute | solution.py:626
  478.3 32.8 %collective-permute-start.31 = (s16[576,256]{1,0:T(8,128)(2,1)}, s16[576,256]{1,0:T(8,128)(2,1)}, u32[]{:S(2)}, u32[]{:S(2)}) collective-permute-start(s16[576,256]{1,0:T(8,128)(2,1)} %get-tuple-element.186), channel_id=1, source_target_pairs={{0,4},{1,5},{2,6},{3,7},{4,0},{5,1},{6,2},{7,3},{8,12},{9,13},{10,... | collective-permute-start | bytes 884744 | tf_op jit(solution)/shard_map/ppermute | solution.py:626
  495.5 22.0 %collective-permute-start.32 = (s16[576,256]{1,0:T(8,128)(2,1)}, s16[576,256]{1,0:T(8,128)(2,1)}, u32[]{:S(2)}, u32[]{:S(2)}) collective-permute-start(s16[576,256]{1,0:T(8,128)(2,1)} %get-tuple-element.187), channel_id=1, source_target_pairs={{0,5},{1,4},{2,7},{3,6},{4,1},{5,0},{6,3},{7,2},{8,13},{9,12},{10,... | collective-permute-start | bytes 884744 | tf_op jit(solution)/shard_map/ppermute | solution.py:626
  495.5 30.5 %collective-permute-start.33 = (s16[576,256]{1,0:T(8,128)(2,1)}, s16[576,256]{1,0:T(8,128)(2,1)}, u32[]{:S(2)}, u32[]{:S(2)}) collective-permute-start(s16[576,256]{1,0:T(8,128)(2,1)} %get-tuple-element.188), channel_id=1, source_target_pairs={{0,6},{1,7},{2,4},{3,5},{4,2},{5,3},{6,0},{7,1},{8,14},{9,15},{10,... | collective-permute-start | bytes 884744 | tf_op jit(solution)/shard_map/ppermute | solution.py:626
  495.6 37.2 %collective-permute-start.34 = (s16[576,256]{1,0:T(8,128)(2,1)}, s16[576,256]{1,0:T(8,128)(2,1)}, u32[]{:S(2)}, u32[]{:S(2)}) collective-permute-start(s16[576,256]{1,0:T(8,128)(2,1)} %get-tuple-element.189), channel_id=1, source_target_pairs={{0,7},{1,6},{2,5},{3,4},{4,3},{5,2},{6,1},{7,0},{8,15},{9,14},{10,... | collective-permute-start | bytes 884744 | tf_op jit(solution)/shard_map/ppermute | solution.py:626
  532.8 109.5 %all-to-all-start.4 = ((s16[8,400,256]{2,1,0:T(8,128)(2,1)}), s16[8,400,256]{2,1,0:T(8,128)(2,1)S(1)}, u32[]{:S(2)}, u32[]{:S(2)}) async-start(s16[8,400,256]{2,1,0:T(8,128)(2,1)} %get-tuple-element.190), calls=%async_computation.4 | async-start | bytes 3276800 | tf_op jit(solution)/shard_map/all_to_all | solution.py:620
  559.3 24.7 %collective-permute-start.36 = (s16[784,256]{1,0:T(8,128)(2,1)}, s16[784,256]{1,0:T(8,128)(2,1)S(1)}, u32[]{:S(2)}, u32[]{:S(2)}) collective-permute-start(s16[784,256]{1,0:T(8,128)(2,1)} %get-tuple-element.203), channel_id=1, source_target_pairs={{0,2},{1,3},{2,0},{3,1},{4,6},{5,7},{6,4},{7,5},{8,10},{9,11},{10,... | collective-permute-start | bytes 1204232 | tf_op jit(solution)/shard_map/ppermute | solution.py:626
  559.4 33.2 %collective-permute-start.37 = (s16[784,256]{1,0:T(8,128)(2,1)}, s16[784,256]{1,0:T(8,128)(2,1)S(1)}, u32[]{:S(2)}, u32[]{:S(2)}) collective-permute-start(s16[784,256]{1,0:T(8,128)(2,1)} %get-tuple-element.204), channel_id=1, source_target_pairs={{0,3},{1,2},{2,1},{3,0},{4,7},{5,6},{6,5},{7,4},{8,11},{9,10},{10,... | collective-permute-start | bytes 1204232 | tf_op jit(solution)/shard_map/ppermute | solution.py:626
  561.4 31.2 %collective-permute-start.38 = (s16[784,256]{1,0:T(8,128)(2,1)}, s16[784,256]{1,0:T(8,128)(2,1)S(1)}, u32[]{:S(2)}, u32[]{:S(2)}) collective-permute-start(s16[784,256]{1,0:T(8,128)(2,1)} %get-tuple-element.205), channel_id=1, source_target_pairs={{0,4},{1,5},{2,6},{3,7},{4,0},{5,1},{6,2},{7,3},{8,12},{9,13},{10,... | collective-permute-start | bytes 1204232 | tf_op jit(solution)/shard_map/ppermute | solution.py:626
  562.8 60.4 %collective-permute-start.39 = (s16[784,256]{1,0:T(8,128)(2,1)}, s16[784,256]{1,0:T(8,128)(2,1)S(1)}, u32[]{:S(2)}, u32[]{:S(2)}) collective-permute-start(s16[784,256]{1,0:T(8,128)(2,1)} %get-tuple-element.206), channel_id=1, source_target_pairs={{0,5},{1,4},{2,7},{3,6},{4,1},{5,0},{6,3},{7,2},{8,13},{9,12},{10,... | collective-permute-start | bytes 1204232 | tf_op jit(solution)/shard_map/ppermute | solution.py:626
  563.8 69.6 %collective-permute-start.40 = (s16[784,256]{1,0:T(8,128)(2,1)}, s16[784,256]{1,0:T(8,128)(2,1)S(1)}, u32[]{:S(2)}, u32[]{:S(2)}) collective-permute-start(s16[784,256]{1,0:T(8,128)(2,1)} %get-tuple-element.207), channel_id=1, source_target_pairs={{0,6},{1,7},{2,4},{3,5},{4,2},{5,3},{6,0},{7,1},{8,14},{9,15},{10,... | collective-permute-start | bytes 1204232 | tf_op jit(solution)/shard_map/ppermute | solution.py:626
  584.0 58.2 %collective-permute-start.41 = (s16[784,256]{1,0:T(8,128)(2,1)}, s16[784,256]{1,0:T(8,128)(2,1)}, u32[]{:S(2)}, u32[]{:S(2)}) collective-permute-start(s16[784,256]{1,0:T(8,128)(2,1)} %get-tuple-element.208), channel_id=1, source_target_pairs={{0,7},{1,6},{2,5},{3,4},{4,3},{5,2},{6,1},{7,0},{8,15},{9,14},{10,... | collective-permute-start | bytes 1204232 | tf_op jit(solution)/shard_map/ppermute | solution.py:626
  651.5 72.8 %all-to-all-start.5 = ((s16[8,304,256]{2,1,0:T(8,128)(2,1)}), s16[8,304,256]{2,1,0:T(8,128)(2,1)S(1)}, u32[]{:S(2)}, u32[]{:S(2)}) async-start(s16[8,304,256]{2,1,0:T(8,128)(2,1)} %explicit.10), calls=%async_computation.5 | async-start | bytes 2490368 | tf_op jit(solution)/shard_map/all_to_all | solution.py:620
  672.7 6.9 collective-permute-start.43
  672.7 14.3 %collective-permute-start.44 = (s16[304,256]{1,0:T(8,128)(2,1)}, s16[304,256]{1,0:T(8,128)(2,1)S(1)}, u32[]{:S(2)}, u32[]{:S(2)}) collective-permute-start(s16[304,256]{1,0:T(8,128)(2,1)} %get-tuple-element.212), channel_id=1, source_target_pairs={{0,3},{1,2},{2,1},{3,0},{4,7},{5,6},{6,5},{7,4},{8,11},{9,10},{10,... | collective-permute-start | bytes 466952 | tf_op jit(solution)/shard_map/ppermute | solution.py:626
  674.7 14.3 %collective-permute-start.45 = (s16[304,256]{1,0:T(8,128)(2,1)}, s16[304,256]{1,0:T(8,128)(2,1)S(1)}, u32[]{:S(2)}, u32[]{:S(2)}) collective-permute-start(s16[304,256]{1,0:T(8,128)(2,1)} %get-tuple-element.213), channel_id=1, source_target_pairs={{0,4},{1,5},{2,6},{3,7},{4,0},{5,1},{6,2},{7,3},{8,12},{9,13},{10,... | collective-permute-start | bytes 466952 | tf_op jit(solution)/shard_map/ppermute | solution.py:626
  676.6 47.5 %collective-permute-start.49 = (s16[576,256]{1,0:T(8,128)(2,1)}, s16[576,256]{1,0:T(8,128)(2,1)S(1)}, u32[]{:S(2)}, u32[]{:S(2)}) collective-permute-start(s16[576,256]{1,0:T(8,128)(2,1)} %get-tuple-element.219), channel_id=1, source_target_pairs={{0,1},{1,0},{2,3},{3,2},{4,5},{5,4},{6,7},{7,6},{8,9},{9,8},{10,11... | collective-permute-start | bytes 884744 | tf_op jit(solution)/shard_map/ppermute | solution.py:626
  677.0 47.3 %collective-permute-start.50 = (s16[576,256]{1,0:T(8,128)(2,1)}, s16[576,256]{1,0:T(8,128)(2,1)S(1)}, u32[]{:S(2)}, u32[]{:S(2)}) collective-permute-start(s16[576,256]{1,0:T(8,128)(2,1)} %get-tuple-element.220), channel_id=1, source_target_pairs={{0,2},{1,3},{2,0},{3,1},{4,6},{5,7},{6,4},{7,5},{8,10},{9,11},{10,... | collective-permute-start | bytes 884744 | tf_op jit(solution)/shard_map/ppermute | solution.py:626
  679.7 18.8 %collective-permute-start.46 = (s16[304,256]{1,0:T(8,128)(2,1)}, s16[304,256]{1,0:T(8,128)(2,1)S(1)}, u32[]{:S(2)}, u32[]{:S(2)}) collective-permute-start(s16[304,256]{1,0:T(8,128)(2,1)} %get-tuple-element.214), channel_id=1, source_target_pairs={{0,5},{1,4},{2,7},{3,6},{4,1},{5,0},{6,3},{7,2},{8,13},{9,12},{10,... | collective-permute-start | bytes 466952 | tf_op jit(solution)/shard_map/ppermute | solution.py:626
  687.0 19.9 %collective-permute-start.47 = (s16[304,256]{1,0:T(8,128)(2,1)}, s16[304,256]{1,0:T(8,128)(2,1)S(1)}, u32[]{:S(2)}, u32[]{:S(2)}) collective-permute-start(s16[304,256]{1,0:T(8,128)(2,1)} %get-tuple-element.215), channel_id=1, source_target_pairs={{0,6},{1,7},{2,4},{3,5},{4,2},{5,3},{6,0},{7,1},{8,14},{9,15},{10,... | collective-permute-start | bytes 466952 | tf_op jit(solution)/shard_map/ppermute | solution.py:626
  689.0 35.2 %collective-permute-start.48 = (s16[304,256]{1,0:T(8,128)(2,1)}, s16[304,256]{1,0:T(8,128)(2,1)S(1)}, u32[]{:S(2)}, u32[]{:S(2)}) collective-permute-start(s16[304,256]{1,0:T(8,128)(2,1)} %get-tuple-element.216), channel_id=1, source_target_pairs={{0,7},{1,6},{2,5},{3,4},{4,3},{5,2},{6,1},{7,0},{8,15},{9,14},{10,... | collective-permute-start | bytes 466952 | tf_op jit(solution)/shard_map/ppermute | solution.py:626
  698.5 36.8 %collective-permute-start.51 = (s16[576,256]{1,0:T(8,128)(2,1)}, s16[576,256]{1,0:T(8,128)(2,1)S(1)}, u32[]{:S(2)}, u32[]{:S(2)}) collective-permute-start(s16[576,256]{1,0:T(8,128)(2,1)} %get-tuple-element.221), channel_id=1, source_target_pairs={{0,3},{1,2},{2,1},{3,0},{4,7},{5,6},{6,5},{7,4},{8,11},{9,10},{10,... | collective-permute-start | bytes 884744 | tf_op jit(solution)/shard_map/ppermute | solution.py:626
  707.0 32.8 %collective-permute-start.52 = (s16[576,256]{1,0:T(8,128)(2,1)}, s16[576,256]{1,0:T(8,128)(2,1)}, u32[]{:S(2)}, u32[]{:S(2)}) collective-permute-start(s16[576,256]{1,0:T(8,128)(2,1)} %get-tuple-element.222), channel_id=1, source_target_pairs={{0,4},{1,5},{2,6},{3,7},{4,0},{5,1},{6,2},{7,3},{8,12},{9,13},{10,... | collective-permute-start | bytes 884744 | tf_op jit(solution)/shard_map/ppermute | solution.py:626
  724.1 22.0 %collective-permute-start.53 = (s16[576,256]{1,0:T(8,128)(2,1)}, s16[576,256]{1,0:T(8,128)(2,1)}, u32[]{:S(2)}, u32[]{:S(2)}) collective-permute-start(s16[576,256]{1,0:T(8,128)(2,1)} %get-tuple-element.223), channel_id=1, source_target_pairs={{0,5},{1,4},{2,7},{3,6},{4,1},{5,0},{6,3},{7,2},{8,13},{9,12},{10,... | collective-permute-start | bytes 884744 | tf_op jit(solution)/shard_map/ppermute | solution.py:626
  724.1 30.5 %collective-permute-start.54 = (s16[576,256]{1,0:T(8,128)(2,1)}, s16[576,256]{1,0:T(8,128)(2,1)}, u32[]{:S(2)}, u32[]{:S(2)}) collective-permute-start(s16[576,256]{1,0:T(8,128)(2,1)} %get-tuple-element.224), channel_id=1, source_target_pairs={{0,6},{1,7},{2,4},{3,5},{4,2},{5,3},{6,0},{7,1},{8,14},{9,15},{10,... | collective-permute-start | bytes 884744 | tf_op jit(solution)/shard_map/ppermute | solution.py:626
  724.2 37.2 %collective-permute-start.55 = (s16[576,256]{1,0:T(8,128)(2,1)}, s16[576,256]{1,0:T(8,128)(2,1)}, u32[]{:S(2)}, u32[]{:S(2)}) collective-permute-start(s16[576,256]{1,0:T(8,128)(2,1)} %get-tuple-element.225), channel_id=1, source_target_pairs={{0,7},{1,6},{2,5},{3,4},{4,3},{5,2},{6,1},{7,0},{8,15},{9,14},{10,... | collective-permute-start | bytes 884744 | tf_op jit(solution)/shard_map/ppermute | solution.py:626
  761.4 44.0 %all-to-all-start.6 = ((s16[8,400,256]{2,1,0:T(8,128)(2,1)}), s16[8,400,256]{2,1,0:T(8,128)(2,1)S(1)}, u32[]{:S(2)}, u32[]{:S(2)}) async-start(s16[8,400,256]{2,1,0:T(8,128)(2,1)} %advance_lines.10), calls=%async_computation.6 | async-start | bytes 3276800 | tf_op jit(solution)/shard_map/all_to_all | solution.py:620
  781.8 19.0 %collective-permute-start.57 = (s16[784,256]{1,0:T(8,128)(2,1)}, s16[784,256]{1,0:T(8,128)(2,1)S(1)}, u32[]{:S(2)}, u32[]{:S(2)}) collective-permute-start(s16[784,256]{1,0:T(8,128)(2,1)} %get-tuple-element.237), channel_id=1, source_target_pairs={{0,2},{1,3},{2,0},{3,1},{4,6},{5,7},{6,4},{7,5},{8,10},{9,11},{10,... | collective-permute-start | bytes 1204232 | tf_op jit(solution)/shard_map/ppermute | solution.py:626
  781.8 37.2 %collective-permute-start.58 = (s16[784,256]{1,0:T(8,128)(2,1)}, s16[784,256]{1,0:T(8,128)(2,1)S(1)}, u32[]{:S(2)}, u32[]{:S(2)}) collective-permute-start(s16[784,256]{1,0:T(8,128)(2,1)} %get-tuple-element.238), channel_id=1, source_target_pairs={{0,3},{1,2},{2,1},{3,0},{4,7},{5,6},{6,5},{7,4},{8,11},{9,10},{10,... | collective-permute-start | bytes 1204232 | tf_op jit(solution)/shard_map/ppermute | solution.py:626
  783.9 35.9 %collective-permute-start.59 = (s16[784,256]{1,0:T(8,128)(2,1)}, s16[784,256]{1,0:T(8,128)(2,1)S(1)}, u32[]{:S(2)}, u32[]{:S(2)}) collective-permute-start(s16[784,256]{1,0:T(8,128)(2,1)} %get-tuple-element.239), channel_id=1, source_target_pairs={{0,4},{1,5},{2,6},{3,7},{4,0},{5,1},{6,2},{7,3},{8,12},{9,13},{10,... | collective-permute-start | bytes 1204232 | tf_op jit(solution)/shard_map/ppermute | solution.py:626
  785.5 66.3 %collective-permute-start.60 = (s16[784,256]{1,0:T(8,128)(2,1)}, s16[784,256]{1,0:T(8,128)(2,1)}, u32[]{:S(2)}, u32[]{:S(2)}) collective-permute-start(s16[784,256]{1,0:T(8,128)(2,1)} %get-tuple-element.240), channel_id=1, source_target_pairs={{0,5},{1,4},{2,7},{3,6},{4,1},{5,0},{6,3},{7,2},{8,13},{9,12},{10,... | collective-permute-start | bytes 1204232 | tf_op jit(solution)/shard_map/ppermute | solution.py:626
  786.2 75.9 %collective-permute-start.61 = (s16[784,256]{1,0:T(8,128)(2,1)}, s16[784,256]{1,0:T(8,128)(2,1)}, u32[]{:S(2)}, u32[]{:S(2)}) collective-permute-start(s16[784,256]{1,0:T(8,128)(2,1)} %get-tuple-element.241), channel_id=1, source_target_pairs={{0,6},{1,7},{2,4},{3,5},{4,2},{5,3},{6,0},{7,1},{8,14},{9,15},{10,... | collective-permute-start | bytes 1204232 | tf_op jit(solution)/shard_map/ppermute | solution.py:626
  800.8 70.1 %collective-permute-start.62 = (s16[784,256]{1,0:T(8,128)(2,1)}, s16[784,256]{1,0:T(8,128)(2,1)}, u32[]{:S(2)}, u32[]{:S(2)}) collective-permute-start(s16[784,256]{1,0:T(8,128)(2,1)} %get-tuple-element.242), channel_id=1, source_target_pairs={{0,7},{1,6},{2,5},{3,4},{4,3},{5,2},{6,1},{7,0},{8,15},{9,14},{10,... | collective-permute-start | bytes 1204232 | tf_op jit(solution)/shard_map/ppermute | solution.py:626
  (60 other events, 1871.6 us)
Sparse Core Ops, SparseCore 0:
  18.4 334.1 all-gather.2

commit v4 on v3

--- a/solution.py
+++ b/solution.py
@@ -47,8 +47,15 @@
     return value if isinstance(value, int) else pl.multiple_of(value, multiple)
 
 
-def partner(whole, me, d):
-    return d if whole else me ^ d
+def bits_of(parts):
+    half = parts // 2
+    far = list(range(half, parts))
+    near = [d for d in range(1, half) if d != half // 2][::-1]
+    return [0, half // 2, *far, *near] if parts > 2 else list(range(parts))
+
+
+def partner(plan, whole, me, d):
+    return d if whole else me ^ plan.bits[d]
 
 
 class Plan:
@@ -58,6 +65,7 @@
         self.width = nx * self.cuts // parts
         self.depth = nz // self.cuts
         self.lines = rows * parts
+        self.bits = bits_of(parts)
         self.scale_rows = -(-rows // 16) * 16
         early = max(rows // 4, 1)
         self.early, self.late = early, rows - early
@@ -173,7 +181,7 @@
 def receive(plan, me, row, sources, scales, speed):
     for whole, group, blocks, factors in zip(WHOLE, GROUPS, sources, scales):
         for d in range(plan.parts):
-            along, across = plan.piece(partner(whole, me, d))
+            along, across = plan.piece(partner(plan, whole, me, d))
             for k, c in enumerate(group):
                 start = pl.multiple_of((k * plan.rows + row) * plan.width, plan.width)
                 value = from_short(blocks[d][pl.ds(start, plan.width), :])
@@ -244,7 +252,7 @@
         )
         term[c] = -(carried + sheared)
     for d in range(parts):
-        along, across = plan.piece(partner(whole, me, d))
+        along, across = plan.piece(partner(plan, whole, me, d))
         values = [term[c, along, across] for c in range(3)]
         code = scale_code(column_max(values))
         factor = encode(code)
@@ -355,7 +363,7 @@
     above, rows = span
     for d, (source, scale) in enumerate(zip(sources, scales)):
         scale = decode(from_short(scale[...]))
-        first = aligned(partner(whole, me, d) * plan.rows_of(1), plan.width)
+        first = aligned(partner(plan, whole, me, d) * plan.rows_of(1), plan.width)
         for j in range(rows):
             value = from_short(source[j * plan.width : (j + 1) * plan.width, :])
             here = pl.ds(first + (above + j) * plan.width, plan.width)
@@ -473,7 +481,7 @@
     lax.fori_loop(0, plan.width, line, 0, unroll=4)
 
     for d in range(parts):
-        first = aligned(partner(whole, me, d) * plan.rows_of(1), plan.width)
+        first = aligned(partner(plan, whole, me, d) * plan.rows_of(1), plan.width)
         chunk = [
             get(field, pl.ds(first + j * plan.width, plan.width)) for j in range(plan.rows)
         ]
@@ -558,30 +566,34 @@
     count = pieces(plan, whole)
     blocks, refs = each(plan, whole, refs[:count]), refs[count:]
     follower_ref, (out_ref, speed, factors) = refs[0], refs[-3:]
-    component, row = pl.program_id(0), pl.program_id(1)
-
-    @pl.when((component == 0) & (row == 0))
+    component, step = pl.program_id(0), pl.program_id(1)
+
+    @pl.when((component == 0) & (step == 0))
     def _():
         for d in range(plan.parts):
             factors[d] = decode(from_short(blocks[d][plan.rows_of(len(group)) :, :]))
 
-    for d in range(plan.parts):
-        along, across = plan.piece(partner(whole, me_ref[0], d))
-        start = pl.multiple_of((component * plan.rows + row) * plan.width, plan.width)
-        value = from_short(blocks[d][pl.ds(start, plan.width), :])
-        speed[along, across] = value * factors[d, pl.ds(component, 1), :]
-    rolled = pltpu.roll(speed[...], shift_ref[0], axis=1)
-    out_ref[0, 0] = rolled - follower_ref[0, 0, 0]
+    rows = out_ref.shape[1]
+    for j in range(rows):
+        row = component * plan.rows + step * rows + j
+        for d in range(plan.parts):
+            along, across = plan.piece(partner(plan, whole, me_ref[0], d))
+            start = pl.multiple_of(row * plan.width, plan.width)
+            value = from_short(blocks[d][pl.ds(start, plan.width), :])
+            speed[j, along, across] = value * factors[d, pl.ds(component, 1), :]
+        rolled = pltpu.roll(speed[j], shift_ref[0], axis=1)
+        out_ref[0, j] = rolled - follower_ref[0, 0, j]
 
 
 def result(plan, group, whole, me, shift, successor, blocks, tangents, before):
     height = plan.rows_of(len(group)) + 16
+    rows = next(r for r in (4, 3, 2, 1) if plan.rows % r == 0)
     specs = block_specs(
         plan, whole, height, plan.depth, lambda c: 0, pipeline_mode=pl.Buffered(1)
     )
     specs.append(
         pl.BlockSpec(
-            (1, 1, 1, plan.nx, plan.nz),
+            (1, 1, rows, plan.nx, plan.nz),
             lambda c, j, me, shift, successor: (successor[0], c + group[0], j, 0, 0),
         )
     )
@@ -595,13 +607,13 @@
         functools.partial(result_kernel, plan, group, whole),
         grid_spec=pltpu.PrefetchScalarGridSpec(
             num_scalar_prefetch=3,
-            grid=(len(group), plan.rows),
+            grid=(len(group), plan.rows // rows),
             in_specs=specs,
             out_specs=pl.BlockSpec(
-                (1, 1, plan.nx, plan.nz), lambda c, j, *_: (c + group[0], j, 0, 0)
+                (1, rows, plan.nx, plan.nz), lambda c, j, *_: (c + group[0], j, 0, 0)
             ),
             scratch_shapes=[
-                pltpu.VMEM((plan.nx, plan.nz), F32),
+                pltpu.VMEM((rows, plan.nx, plan.nz), F32),
                 pltpu.VMEM((plan.parts, 16, plan.depth), F32),
             ],
         ),
@@ -618,12 +630,10 @@
 def exchange(plan, whole, blocks):
     if whole:
         return [lax.all_to_all(blocks[0], "grid", split_axis=0, concat_axis=0, tiled=True)]
-    parts = plan.parts
     moved = list(blocks)
-    half = parts // 2
-    order = [half // 2, *range(half, parts)] + [d for d in range(1, half) if d != half // 2][::-1]
-    for d in order:
-        moved[d] = lax.ppermute(blocks[d], "grid", [(i, i ^ d) for i in range(parts)])
+    for d in range(1, plan.parts):
+        route = [(i, i ^ plan.bits[d]) for i in range(plan.parts)]
+        moved[d] = lax.ppermute(blocks[d], "grid", route)
     return moved
 
 
@@ -647,9 +657,11 @@
     bases.append(base)
     late, base = explicit(plan, True, later, tangent, flow, shear, dx, dz)
     bases.append(base)
-    early[0][0], late[0][0] = lax.optimization_barrier((early[0][0], late[0][0]))
-    term = [exchange(plan, True, early[0]), [exchange(plan, False, blocks) for blocks in late]]
     right, turned, wall_flow = first_lines(plan, start, wall_derivative)
+    early[0][0], late = lax.optimization_barrier((early[0][0], late))
+    early = exchange(plan, True, early[0])
+    late, wall_flow = lax.optimization_barrier((late, wall_flow))
+    term = [early, [exchange(plan, False, blocks) for blocks in late]]
     states = [(right, turned) for _ in GROUPS]
     for section in range(SECTIONS):
         value = []

time: 898 us -> 875 us (0.974)
  waiting for transfers between devices: 519 us -> 494 us
  starting transfers between devices: 111 us -> 125 us
  Pallas kernels: 241 us -> 229 us
    ppermute x63, waiting for transfers between devices: 410 us -> 385 us  [exchange(): moved[d] = lax.ppermute(blocks[d], 'grid', route)]
    pallas_call x2, Pallas kernels: 27.6 us -> 15.7 us  [result(): pl.pallas_call(functools.partial(result_kernel, plan, group, whole), grid...]
    ppermute x63, starting transfers between devices: 79.7 us -> 90.7 us  [exchange(): moved[d] = lax.ppermute(blocks[d], 'grid', route)]
  transfers between devices with their start and end apart: 71 -> 71, of which waited for: 40 -> 38; matrix products, arithmetic and copies ran while one was open for 0% -> 0% of each run, Pallas kernels for 24% -> 24%
where the time goes in v4:
time: 875 us; the launch traced here: 873 us
  waiting for transfers between devices  494 us (56%)
  Pallas kernels  229 us (26%)
  starting transfers between devices  125 us (14%)
  between operations  14.6 us (2%)
  local copies, waits for them, and re-layouts  10.3 us (1%)
    ppermute x63, waiting for transfers between devices, exchange(): moved[d] = lax.ppermute(blocks[d], 'grid', route)  385 us
    all_to_all x7, waiting for transfers between devices, exchange(): lax.all_to_all(blocks[0], 'grid', split_axis=0, concat_axis=0, tiled=True)  109 us
    pallas_call x6, Pallas kernels, advance_lines(): pl.pallas_call(functools.partial(lines_kernel, plan, section, group, whol...  100 us
    ppermute x63, starting transfers between devices, exchange(): moved[d] = lax.ppermute(blocks[d], 'grid', route)  90.7 us
    pallas_call x6, Pallas kernels, explicit(): pl.pallas_call(functools.partial(explicit_kernel, plan, late, received),...  80.1 us
    all_to_all x7, starting transfers between devices, exchange(): lax.all_to_all(blocks[0], 'grid', split_axis=0, concat_axis=0, tiled=True)  34.3 us
    pallas_call x1, Pallas kernels, first_lines(): pl.pallas_call(functools.partial(first_lines_kernel, plan), grid=(3,), in...  21.5 us
  transfers between devices with their start and end apart: 71, of which 38 were waited for; matrix products, arithmetic and copies ran while one was open for 0% of the time, Pallas kernels for 24%

profile of v4, /device:TPU:9, one launch (start us, length us, event | category | flops | bytes accessed | tf_op | source)
XLA Modules:
  0.0 873.1 jit_solution(12633172889388635401)
XLA Ops:
  6.5 11.7 %pack_start.1 = s16[8,1568,256]{2,1,0:T(8,128)(2,1)} custom-call(f32[3,12,256,256]{3,2,1,0:T(8,128)} %bitcast.8, bf16[3,12,256,256]{3,2,1,0:T(8,128)(2,1)} %bitcast.12), custom_call_target="tpu_custom_call" | custom-call | bytes 20000000 | tf_op jit(solution)/shard_map/pack_start/pallas_call | solution.py:133
  18.3 5.7 all-to-all-start.1
  24.0 8.7 explicit.6
  32.6 20.3 %explicit.7 = (s16[304,256]{1,0:T(8,128)(2,1)}, s16[304,256]{1,0:T(8,128)(2,1)}, s16[304,256]{1,0:T(8,128)(2,1)}, s16[304,256]{1,0:T(8,128)(2,1)}, s16[304,256]{...) custom-call(s32[1]{0:T(128)} %bitcast.me_ref, ...), custom_call_target="tpu_custom_call" | custom-call | flops 8999999488 | bytes 36000000 | tf_op jit(solution)/shard_map/explicit/pallas_call | solution.py:310
  53.0 109.2 %all-to-all-done.1.refs_0_.refs_1_.refs_2_.refs_3_ = s16[8,1568,256]{2,1,0:T(8,128)(2,1)} async-done(((s16[8,1568,256]{2,1,0:T(8,128)(2,1)}), s16[8,1568,256]{2,1,0:T(8,128)(2,1)}, u32[]{:S(2)}, u32[]{:S(2)}) %all-to-all-start.1) | async-done | bytes 6422560 | tf_op jit(solution)/shard_map/all_to_all | solution.py:632
  162.2 7.1 all-to-all-start
  169.4 21.5 %first_lines.1 = (f32[3,32,96,256]{3,2,1,0:T(8,128)}, f32[3,32,96,256]{3,2,1,0:T(8,128)}, f32[32,96,256]{2,1,0:T(8,128)}) custom-call(s16[8,1568,256]{2,1,0:T(8,128)(2,1)} %all-to-all-done.1.refs_0_.refs_1_.refs_2_.refs_3_, s16[8,1568,256]{2,1,0:T(8,128)(2,1)} %all-to-all-done.1.refs_0_.refs_1_.refs_2_.refs_3_, ...), custom_call_target="tpu_custom_call" | custom-call | flops 1000000000 | bytes 30000000 | tf_op jit(solution)/shard_map/first_lines/pallas_call | solution.py:408
  200.6 21.8 %collective-permute-done.1.refs_3_.refs_12_ = s16[304,256]{1,0:T(8,128)(2,1)S(1)} collective-permute-done((s16[304,256]{1,0:T(8,128)(2,1)S(1)}, s16[304,256]{1,0:T(8,128)(2,1)S(1)}, u32[]{:S(2)}, u32[]{:S(2)}) %collective-permute-start.1) | collective-permute-done | bytes 155680 | tf_op jit(solution)/shard_map/ppermute | solution.py:636
  225.8 3.2 collective-permute-start.5
  229.0 5.3 collective-permute-done.3.refs_5_.refs_14_
  235.5 15.2 %collective-permute-done.4.refs_6_.refs_15_ = s16[304,256]{1,0:T(8,128)(2,1)S(1)} collective-permute-done((s16[304,256]{1,0:T(8,128)(2,1)S(1)}, s16[304,256]{1,0:T(8,128)(2,1)S(1)}, u32[]{:S(2)}, u32[]{:S(2)}) %collective-permute-start.4) | collective-permute-done | bytes 155680 | tf_op jit(solution)/shard_map/ppermute | solution.py:636
  252.7 2.9 collective-permute-start.9
  256.7 14.3 %advance_lines.6 = (s16[8,400,256]{2,1,0:T(8,128)(2,1)}, f32[1,32,96,256]{3,2,1,0:T(8,128)}, f32[1,32,96,256]{3,2,1,0:T(8,128)}) custom-call(s32[1]{0:T(128)} %bitcast.me_ref, s16[8,304,256]{2,1,0:T(8,128)(2,1)} %copy-done.2, s16[304,256]{1,0:T(8,128)(2,1)} %get-tuple-element.194.refs_1_.refs_10_, s16[304,256]{1,0:T(8,128)(2,1)} %copy-done.20, ...), custom_call_target="tpu_custom_call" | custom-call | flops 700000000 | bytes 17000000 | tf_op jit(solution)/shard_map/advance_lines/pallas_call | solution.py:539
  271.0 4.1 collective-permute-done.7.refs_2_
  275.1 3.6 collective-permute-done.9.refs_4_
  278.8 6.2 all-to-all-start.2
  285.0 22.5 %advance_lines.7 = (s16[784,256]{1,0:T(8,128)(2,1)}, s16[784,256]{1,0:T(8,128)(2,1)}, s16[784,256]{1,0:T(8,128)(2,1)}, s16[784,256]{1,0:T(8,128)(2,1)}, s16[784,...) custom-call(s32[1]{0:T(128)} %bitcast.me_ref, ...), custom_call_target="tpu_custom_call" | custom-call | flops 1400000000 | bytes 34000000 | tf_op jit(solution)/shard_map/advance_lines/pallas_call | solution.py:539
  313.0 11.6 %collective-permute-done.14.refs_2_ = s16[784,256]{1,0:T(8,128)(2,1)S(1)} collective-permute-done((s16[784,256]{1,0:T(8,128)(2,1)}, s16[784,256]{1,0:T(8,128)(2,1)S(1)}, u32[]{:S(2)}, u32[]{:S(2)}) %collective-permute-start.14) | collective-permute-done | bytes 401440 | tf_op jit(solution)/shard_map/ppermute | solution.py:636
  327.2 36.6 %collective-permute-done.15.refs_3_ = s16[784,256]{1,0:T(8,128)(2,1)S(1)} collective-permute-done((s16[784,256]{1,0:T(8,128)(2,1)}, s16[784,256]{1,0:T(8,128)(2,1)S(1)}, u32[]{:S(2)}, u32[]{:S(2)}) %collective-permute-start.15) | collective-permute-done | bytes 401440 | tf_op jit(solution)/shard_map/ppermute | solution.py:636
  364.6 7.8 collective-permute-done.16.refs_4_
  372.3 10.2 %collective-permute-done.17.refs_5_ = s16[784,256]{1,0:T(8,128)(2,1)S(1)} collective-permute-done((s16[784,256]{1,0:T(8,128)(2,1)}, s16[784,256]{1,0:T(8,128)(2,1)S(1)}, u32[]{:S(2)}, u32[]{:S(2)}) %collective-permute-start.17) | collective-permute-done | bytes 401440 | tf_op jit(solution)/shard_map/ppermute | solution.py:636
  382.5 8.8 %collective-permute-done.18.refs_6_ = s16[784,256]{1,0:T(8,128)(2,1)S(1)} collective-permute-done((s16[784,256]{1,0:T(8,128)(2,1)}, s16[784,256]{1,0:T(8,128)(2,1)S(1)}, u32[]{:S(2)}, u32[]{:S(2)}) %collective-permute-start.18) | collective-permute-done | bytes 401440 | tf_op jit(solution)/shard_map/ppermute | solution.py:636
  394.0 8.1 explicit.8
  402.1 3.5 all-to-all-start.3
  405.6 17.5 %explicit.9 = (s16[304,256]{1,0:T(8,128)(2,1)}, s16[304,256]{1,0:T(8,128)(2,1)}, s16[304,256]{1,0:T(8,128)(2,1)}, s16[304,256]{1,0:T(8,128)(2,1)}, s16[304,256]{...) custom-call(s32[1]{0:T(128)} %bitcast.me_ref, ...), custom_call_target="tpu_custom_call" | custom-call | flops 8999999488 | bytes 36000000 | tf_op jit(solution)/shard_map/explicit/pallas_call | solution.py:310
  432.0 14.1 %collective-permute-done.22.refs_3_.refs_12_ = s16[304,256]{1,0:T(8,128)(2,1)S(1)} collective-permute-done((s16[304,256]{1,0:T(8,128)(2,1)}, s16[304,256]{1,0:T(8,128)(2,1)S(1)}, u32[]{:S(2)}, u32[]{:S(2)}) %collective-permute-start.22) | collective-permute-done | bytes 155680 | tf_op jit(solution)/shard_map/ppermute | solution.py:636
  448.2 7.6 collective-permute-done.23.refs_4_.refs_13_
  455.8 6.3 collective-permute-start.26
  465.3 8.5 collective-permute-done.25.refs_6_.refs_15_
  475.8 3.5 collective-permute-start.33
  480.8 14.3 %advance_lines.8 = (s16[8,400,256]{2,1,0:T(8,128)(2,1)}, f32[1,32,96,256]{3,2,1,0:T(8,128)}, f32[1,32,96,256]{3,2,1,0:T(8,128)}) custom-call(s32[1]{0:T(128)} %bitcast.me_ref, s16[8,304,256]{2,1,0:T(8,128)(2,1)} %copy-done, s16[304,256]{1,0:T(8,128)(2,1)} %get-tuple-element.235.refs_1_.refs_10_, s16[304,256]{1,0:T(8,128)(2,1)} %copy-done.6, ...), custom_call_target="tpu_custom_call" | custom-call | flops 700000000 | bytes 17000000 | tf_op jit(solution)/shard_map/advance_lines/pallas_call | solution.py:539
  495.1 4.6 collective-permute-done.30.refs_4_
  499.7 7.2 collective-permute-done.31.refs_5_
  506.9 6.5 collective-permute-done.32.refs_6_
  513.5 4.1 all-to-all-start.4
  517.6 22.7 %advance_lines.9 = (s16[784,256]{1,0:T(8,128)(2,1)}, s16[784,256]{1,0:T(8,128)(2,1)}, s16[784,256]{1,0:T(8,128)(2,1)}, s16[784,256]{1,0:T(8,128)(2,1)}, s16[784,...) custom-call(s32[1]{0:T(128)} %bitcast.me_ref, ...), custom_call_target="tpu_custom_call" | custom-call | flops 1400000000 | bytes 34000000 | tf_op jit(solution)/shard_map/advance_lines/pallas_call | solution.py:539
  543.3 2.6 collective-permute-start.38
  545.9 11.2 %collective-permute-done.35.refs_2_ = s16[784,256]{1,0:T(8,128)(2,1)S(1)} collective-permute-done((s16[784,256]{1,0:T(8,128)(2,1)}, s16[784,256]{1,0:T(8,128)(2,1)S(1)}, u32[]{:S(2)}, u32[]{:S(2)}) %collective-permute-start.35) | collective-permute-done | bytes 401440 | tf_op jit(solution)/shard_map/ppermute | solution.py:636
  557.1 2.6 collective-permute-start.40
  559.7 36.7 %collective-permute-done.36.refs_3_ = s16[784,256]{1,0:T(8,128)(2,1)S(1)} collective-permute-done((s16[784,256]{1,0:T(8,128)(2,1)}, s16[784,256]{1,0:T(8,128)(2,1)S(1)}, u32[]{:S(2)}, u32[]{:S(2)}) %collective-permute-start.36) | collective-permute-done | bytes 401440 | tf_op jit(solution)/shard_map/ppermute | solution.py:636
  596.9 8.1 collective-permute-done.37.refs_4_
  605.0 10.2 %collective-permute-done.38.refs_5_ = s16[784,256]{1,0:T(8,128)(2,1)S(1)} collective-permute-done((s16[784,256]{1,0:T(8,128)(2,1)}, s16[784,256]{1,0:T(8,128)(2,1)S(1)}, u32[]{:S(2)}, u32[]{:S(2)}) %collective-permute-start.38) | collective-permute-done | bytes 401440 | tf_op jit(solution)/shard_map/ppermute | solution.py:636
  615.2 8.8 %collective-permute-done.39.refs_6_ = s16[784,256]{1,0:T(8,128)(2,1)S(1)} collective-permute-done((s16[784,256]{1,0:T(8,128)(2,1)}, s16[784,256]{1,0:T(8,128)(2,1)S(1)}, u32[]{:S(2)}, u32[]{:S(2)}) %collective-permute-start.39) | collective-permute-done | bytes 401440 | tf_op jit(solution)/shard_map/ppermute | solution.py:636
  626.6 8.1 explicit.10
  634.7 3.5 all-to-all-start.5
  638.2 17.4 %explicit.11 = (s16[304,256]{1,0:T(8,128)(2,1)}, s16[304,256]{1,0:T(8,128)(2,1)}, s16[304,256]{1,0:T(8,128)(2,1)}, s16[304,256]{1,0:T(8,128)(2,1)}, s16[304,256]...) custom-call(s32[1]{0:T(128)} %bitcast.me_ref, ...), custom_call_target="tpu_custom_call" | custom-call | flops 8999999488 | bytes 36000000 | tf_op jit(solution)/shard_map/explicit/pallas_call | solution.py:310
  664.3 14.3 %collective-permute-done.43.refs_3_.refs_12_ = s16[304,256]{1,0:T(8,128)(2,1)S(1)} collective-permute-done((s16[304,256]{1,0:T(8,128)(2,1)}, s16[304,256]{1,0:T(8,128)(2,1)S(1)}, u32[]{:S(2)}, u32[]{:S(2)}) %collective-permute-start.43) | collective-permute-done | bytes 155680 | tf_op jit(solution)/shard_map/ppermute | solution.py:636
  680.8 7.6 collective-permute-done.44.refs_4_.refs_13_
  688.4 6.3 collective-permute-start.47
  697.9 8.5 collective-permute-done.46.refs_6_.refs_15_
  708.4 3.5 collective-permute-start.54
  713.3 9.9 %advance_lines.10 = s16[8,400,256]{2,1,0:T(8,128)(2,1)} custom-call(s32[1]{0:T(128)} %bitcast.me_ref, s16[8,304,256]{2,1,0:T(8,128)(2,1)} %copy-done.1, s16[304,256]{1,0:T(8,128)(2,1)} %get-tuple-element.273.refs_1_.refs_10_, s16[304,256]{1,0:T(8,128)(2,1)} %copy-done.10, s16[304,256]{1,0:T(8,128)(2,1)} %copy-done.11, s16[304,256]{1,0:T(8,128)(2,1)} %copy-done.12, ...), custom_call_target="tpu_custom_call" | custom-call | flops 700000000 | bytes 17000000 | tf_op jit(solution)/shard_map/advance_lines/pallas_call | solution.py:539
  723.2 9.1 %collective-permute-done.51.refs_4_ = s16[576,256]{1,0:T(8,128)(2,1)S(1)} collective-permute-done((s16[576,256]{1,0:T(8,128)(2,1)}, s16[576,256]{1,0:T(8,128)(2,1)S(1)}, u32[]{:S(2)}, u32[]{:S(2)}) %collective-permute-start.51) | collective-permute-done | bytes 294944 | tf_op jit(solution)/shard_map/ppermute | solution.py:636
  732.3 7.2 collective-permute-done.52.refs_5_
  739.5 6.5 collective-permute-done.53.refs_6_
  746.1 4.1 all-to-all-start.6
  750.3 16.7 %advance_lines.11 = (s16[784,256]{1,0:T(8,128)(2,1)}, s16[784,256]{1,0:T(8,128)(2,1)}, s16[784,256]{1,0:T(8,128)(2,1)}, s16[784,256]{1,0:T(8,128)(2,1)}, s16[784...) custom-call(s32[1]{0:T(128)} %bitcast.me_ref, ...), custom_call_target="tpu_custom_call" | custom-call | flops 1400000000 | bytes 34000000 | tf_op jit(solution)/shard_map/advance_lines/pallas_call | solution.py:539
  770.0 2.6 collective-permute-start.59
  772.6 14.0 %collective-permute-done.56.refs_1_ = s16[784,256]{1,0:T(8,128)(2,1)S(1)} collective-permute-done((s16[784,256]{1,0:T(8,128)(2,1)}, s16[784,256]{1,0:T(8,128)(2,1)S(1)}, u32[]{:S(2)}, u32[]{:S(2)}) %collective-permute-start.56) | collective-permute-done | bytes 401440 | tf_op jit(solution)/shard_map/ppermute | solution.py:636
  786.6 42.3 %collective-permute-done.57.refs_2_ = s16[784,256]{1,0:T(8,128)(2,1)S(1)} collective-permute-done((s16[784,256]{1,0:T(8,128)(2,1)}, s16[784,256]{1,0:T(8,128)(2,1)S(1)}, u32[]{:S(2)}, u32[]{:S(2)}) %collective-permute-start.57) | collective-permute-done | bytes 401440 | tf_op jit(solution)/shard_map/ppermute | solution.py:636
  831.8 6.1 result.2.refs_9_
  838.0 9.8 %collective-permute-done.59.refs_4_ = s16[784,256]{1,0:T(8,128)(2,1)S(1)} collective-permute-done((s16[784,256]{1,0:T(8,128)(2,1)}, s16[784,256]{1,0:T(8,128)(2,1)S(1)}, u32[]{:S(2)}, u32[]{:S(2)}) %collective-permute-start.59) | collective-permute-done | bytes 401440 | tf_op jit(solution)/shard_map/ppermute | solution.py:636
  847.7 8.9 %collective-permute-done.60.refs_5_ = s16[784,256]{1,0:T(8,128)(2,1)} collective-permute-done((s16[784,256]{1,0:T(8,128)(2,1)}, s16[784,256]{1,0:T(8,128)(2,1)}, u32[]{:S(2)}, u32[]{:S(2)}) %collective-permute-start.60) | collective-permute-done | bytes 401440 | tf_op jit(solution)/shard_map/ppermute | solution.py:636
  856.6 9.6 %result.3 = f32[3,12,256,256]{3,2,1,0:T(8,128)} custom-call(s32[1]{0:T(128)} %bitcast.me_ref, s32[1]{0:T(128)S(6)} %copy.12.shift_ref, s32[1]{0:T(128)} %dynamic_slice.3.successor_ref, s16[784,256]{1,0:T(8,128)(2,1)} %get-tuple-element.299.refs_0_, s16[784,256]{1,0:T(8,128)(2,1)} %copy-done.27, ...), custom_call_target="tpu_custom_call", output_to_operand_aliasing={{}: (12, {})} | custom-call | bytes 16000000 | tf_op jit(solution)/shard_map/result/pallas_call | solution.py:606
  (218 shorter events, 75.4 us)
Async XLA Ops:
  6.5 824.2 %all-gather.3.cloned.1.call-start = ((), (), s32[]{:S(2)}) async-start(), calls=%async_computation.7 | async-start | bytes 47185920 | tf_op jit(solution)/shard_map/all_gather | solution.py:653
  18.3 143.9 %all-to-all-start.1 = ((s16[8,1568,256]{2,1,0:T(8,128)(2,1)}), s16[8,1568,256]{2,1,0:T(8,128)(2,1)}, u32[]{:S(2)}, u32[]{:S(2)}) async-start(s16[8,1568,256]{2,1,0:T(8,128)(2,1)} %pack_start.1), calls=%async_computation.1 | async-start | bytes 12845056 | tf_op jit(solution)/shard_map/all_to_all | solution.py:632
  162.2 93.4 %all-to-all-start = ((s16[8,304,256]{2,1,0:T(8,128)(2,1)}), s16[8,304,256]{2,1,0:T(8,128)(2,1)S(1)}, u32[]{:S(2)}, u32[]{:S(2)}) async-start(s16[8,304,256]{2,1,0:T(8,128)(2,1)} %get-tuple-element.175), calls=%async_computation | async-start | bytes 2490368 | tf_op jit(solution)/shard_map/all_to_all | solution.py:632
  191.1 31.4 %collective-permute-start.1 = (s16[304,256]{1,0:T(8,128)(2,1)S(1)}, s16[304,256]{1,0:T(8,128)(2,1)S(1)}, u32[]{:S(2)}, u32[]{:S(2)}) collective-permute-start(s16[304,256]{1,0:T(8,128)(2,1)S(1)} %copy-done.58), channel_id=1, source_target_pairs={{0,4},{1,5},{2,6},{3,7},{4,0},{5,1},{6,2},{7,3},{8,12},{9,13},{10,... | collective-permute-start | bytes 466952 | tf_op jit(solution)/shard_map/ppermute | solution.py:636
  193.4 32.5 %collective-permute-start.2 = (s16[304,256]{1,0:T(8,128)(2,1)S(1)}, s16[304,256]{1,0:T(8,128)(2,1)S(1)}, u32[]{:S(2)}, u32[]{:S(2)}) collective-permute-start(s16[304,256]{1,0:T(8,128)(2,1)S(1)} %copy-done.57), channel_id=1, source_target_pairs={{0,5},{1,4},{2,7},{3,6},{4,1},{5,0},{6,3},{7,2},{8,13},{9,12},{10,... | collective-permute-start | bytes 466952 | tf_op jit(solution)/shard_map/ppermute | solution.py:636
  194.0 40.3 %collective-permute-start.3 = (s16[304,256]{1,0:T(8,128)(2,1)S(1)}, s16[304,256]{1,0:T(8,128)(2,1)S(1)}, u32[]{:S(2)}, u32[]{:S(2)}) collective-permute-start(s16[304,256]{1,0:T(8,128)(2,1)S(1)} %copy-done.56), channel_id=1, source_target_pairs={{0,6},{1,7},{2,4},{3,5},{4,2},{5,3},{6,0},{7,1},{8,14},{9,15},{10,... | collective-permute-start | bytes 466952 | tf_op jit(solution)/shard_map/ppermute | solution.py:636
  196.6 56.1 %collective-permute-start.10 = (s16[576,256]{1,0:T(8,128)(2,1)}, s16[576,256]{1,0:T(8,128)(2,1)S(1)}, u32[]{:S(2)}, u32[]{:S(2)}) collective-permute-start(s16[576,256]{1,0:T(8,128)(2,1)} %get-tuple-element.210), channel_id=1, source_target_pairs={{0,6},{1,7},{2,4},{3,5},{4,2},{5,3},{6,0},{7,1},{8,14},{9,15},{10,... | collective-permute-start | bytes 884744 | tf_op jit(solution)/shard_map/ppermute | solution.py:636
  198.3 54.3 %collective-permute-start.11 = (s16[576,256]{1,0:T(8,128)(2,1)S(1)}, s16[576,256]{1,0:T(8,128)(2,1)S(1)}, u32[]{:S(2)}, u32[]{:S(2)}) collective-permute-start(s16[576,256]{1,0:T(8,128)(2,1)S(1)} %copy-done.52), channel_id=1, source_target_pairs={{0,7},{1,6},{2,5},{3,4},{4,3},{5,2},{6,1},{7,0},{8,15},{9,14},{10,... | collective-permute-start | bytes 884744 | tf_op jit(solution)/shard_map/ppermute | solution.py:636
  222.5 28.3 %collective-permute-start.4 = (s16[304,256]{1,0:T(8,128)(2,1)S(1)}, s16[304,256]{1,0:T(8,128)(2,1)S(1)}, u32[]{:S(2)}, u32[]{:S(2)}) collective-permute-start(s16[304,256]{1,0:T(8,128)(2,1)S(1)} %copy-done.55), channel_id=1, source_target_pairs={{0,7},{1,6},{2,5},{3,4},{4,3},{5,2},{6,1},{7,0},{8,15},{9,14},{10,... | collective-permute-start | bytes 466952 | tf_op jit(solution)/shard_map/ppermute | solution.py:636
  225.8 24.9 %collective-permute-start.5 = (s16[304,256]{1,0:T(8,128)(2,1)S(1)}, s16[304,256]{1,0:T(8,128)(2,1)S(1)}, u32[]{:S(2)}, u32[]{:S(2)}) collective-permute-start(s16[304,256]{1,0:T(8,128)(2,1)S(1)} %copy-done.54), channel_id=1, source_target_pairs={{0,3},{1,2},{2,1},{3,0},{4,7},{5,6},{6,5},{7,4},{8,11},{9,10},{10,... | collective-permute-start | bytes 466952 | tf_op jit(solution)/shard_map/ppermute | solution.py:636
  250.8 20.2 %collective-permute-start.12 = (s16[576,256]{1,0:T(8,128)(2,1)}, s16[576,256]{1,0:T(8,128)(2,1)S(1)}, u32[]{:S(2)}, u32[]{:S(2)}) collective-permute-start(s16[576,256]{1,0:T(8,128)(2,1)} %get-tuple-element.212), channel_id=1, source_target_pairs={{0,3},{1,2},{2,1},{3,0},{4,7},{5,6},{6,5},{7,4},{8,11},{9,10},{10,... | collective-permute-start | bytes 884744 | tf_op jit(solution)/shard_map/ppermute | solution.py:636
  250.8 20.2 %collective-permute-start.13 = (s16[576,256]{1,0:T(8,128)(2,1)}, s16[576,256]{1,0:T(8,128)(2,1)}, u32[]{:S(2)}, u32[]{:S(2)}) collective-permute-start(s16[576,256]{1,0:T(8,128)(2,1)} %get-tuple-element.213), channel_id=1, source_target_pairs={{0,1},{1,0},{2,3},{3,2},{4,5},{5,4},{6,7},{7,6},{8,9},{9,8},{10,11... | collective-permute-start | bytes 884744 | tf_op jit(solution)/shard_map/ppermute | solution.py:636
  250.9 24.3 %collective-permute-start.7 = (s16[576,256]{1,0:T(8,128)(2,1)}, s16[576,256]{1,0:T(8,128)(2,1)}, u32[]{:S(2)}, u32[]{:S(2)}) collective-permute-start(s16[576,256]{1,0:T(8,128)(2,1)} %get-tuple-element.207), channel_id=1, source_target_pairs={{0,2},{1,3},{2,0},{3,1},{4,6},{5,7},{6,4},{7,5},{8,10},{9,11},{10,... | collective-permute-start | bytes 884744 | tf_op jit(solution)/shard_map/ppermute | solution.py:636
  252.6 22.5 %collective-permute-start.8 = (s16[576,256]{1,0:T(8,128)(2,1)}, s16[576,256]{1,0:T(8,128)(2,1)}, u32[]{:S(2)}, u32[]{:S(2)}) collective-permute-start(s16[576,256]{1,0:T(8,128)(2,1)} %get-tuple-element.208), channel_id=1, source_target_pairs={{0,4},{1,5},{2,6},{3,7},{4,0},{5,1},{6,2},{7,3},{8,12},{9,13},{10,... | collective-permute-start | bytes 884744 | tf_op jit(solution)/shard_map/ppermute | solution.py:636
  252.7 26.1 %collective-permute-start.9 = (s16[576,256]{1,0:T(8,128)(2,1)}, s16[576,256]{1,0:T(8,128)(2,1)}, u32[]{:S(2)}, u32[]{:S(2)}) collective-permute-start(s16[576,256]{1,0:T(8,128)(2,1)} %get-tuple-element.209), channel_id=1, source_target_pairs={{0,5},{1,4},{2,7},{3,6},{4,1},{5,0},{6,3},{7,2},{8,13},{9,12},{10,... | collective-permute-start | bytes 884744 | tf_op jit(solution)/shard_map/ppermute | solution.py:636
  278.8 114.0 %all-to-all-start.2 = ((s16[8,400,256]{2,1,0:T(8,128)(2,1)}), s16[8,400,256]{2,1,0:T(8,128)(2,1)S(1)}, u32[]{:S(2)}, u32[]{:S(2)}) async-start(s16[8,400,256]{2,1,0:T(8,128)(2,1)} %get-tuple-element.214), calls=%async_computation.2 | async-start | bytes 3276800 | tf_op jit(solution)/shard_map/all_to_all | solution.py:632
  307.4 17.2 %collective-permute-start.14 = (s16[784,256]{1,0:T(8,128)(2,1)}, s16[784,256]{1,0:T(8,128)(2,1)S(1)}, u32[]{:S(2)}, u32[]{:S(2)}) collective-permute-start(s16[784,256]{1,0:T(8,128)(2,1)} %get-tuple-element.224), channel_id=1, source_target_pairs={{0,2},{1,3},{2,0},{3,1},{4,6},{5,7},{6,4},{7,5},{8,10},{9,11},{10,... | collective-permute-start | bytes 1204232 | tf_op jit(solution)/shard_map/ppermute | solution.py:636
  308.0 55.7 %collective-permute-start.15 = (s16[784,256]{1,0:T(8,128)(2,1)}, s16[784,256]{1,0:T(8,128)(2,1)S(1)}, u32[]{:S(2)}, u32[]{:S(2)}) collective-permute-start(s16[784,256]{1,0:T(8,128)(2,1)} %get-tuple-element.225), channel_id=1, source_target_pairs={{0,4},{1,5},{2,6},{3,7},{4,0},{5,1},{6,2},{7,3},{8,12},{9,13},{10,... | collective-permute-start | bytes 1204232 | tf_op jit(solution)/shard_map/ppermute | solution.py:636
  309.9 62.5 %collective-permute-start.16 = (s16[784,256]{1,0:T(8,128)(2,1)}, s16[784,256]{1,0:T(8,128)(2,1)S(1)}, u32[]{:S(2)}, u32[]{:S(2)}) collective-permute-start(s16[784,256]{1,0:T(8,128)(2,1)} %get-tuple-element.226), channel_id=1, source_target_pairs={{0,5},{1,4},{2,7},{3,6},{4,1},{5,0},{6,3},{7,2},{8,13},{9,12},{10,... | collective-permute-start | bytes 1204232 | tf_op jit(solution)/shard_map/ppermute | solution.py:636
  310.7 71.8 %collective-permute-start.17 = (s16[784,256]{1,0:T(8,128)(2,1)}, s16[784,256]{1,0:T(8,128)(2,1)S(1)}, u32[]{:S(2)}, u32[]{:S(2)}) collective-permute-start(s16[784,256]{1,0:T(8,128)(2,1)} %get-tuple-element.227), channel_id=1, source_target_pairs={{0,6},{1,7},{2,4},{3,5},{4,2},{5,3},{6,0},{7,1},{8,14},{9,15},{10,... | collective-permute-start | bytes 1204232 | tf_op jit(solution)/shard_map/ppermute | solution.py:636
  313.0 78.2 %collective-permute-start.18 = (s16[784,256]{1,0:T(8,128)(2,1)}, s16[784,256]{1,0:T(8,128)(2,1)S(1)}, u32[]{:S(2)}, u32[]{:S(2)}) collective-permute-start(s16[784,256]{1,0:T(8,128)(2,1)} %get-tuple-element.228), channel_id=1, source_target_pairs={{0,7},{1,6},{2,5},{3,4},{4,3},{5,2},{6,1},{7,0},{8,15},{9,14},{10,... | collective-permute-start | bytes 1204232 | tf_op jit(solution)/shard_map/ppermute | solution.py:636
  324.6 66.7 %collective-permute-start.19 = (s16[784,256]{1,0:T(8,128)(2,1)}, s16[784,256]{1,0:T(8,128)(2,1)S(1)}, u32[]{:S(2)}, u32[]{:S(2)}) collective-permute-start(s16[784,256]{1,0:T(8,128)(2,1)} %get-tuple-element.229), channel_id=1, source_target_pairs={{0,3},{1,2},{2,1},{3,0},{4,7},{5,6},{6,5},{7,4},{8,11},{9,10},{10,... | collective-permute-start | bytes 1204232 | tf_op jit(solution)/shard_map/ppermute | solution.py:636
  363.7 29.1 %collective-permute-start.20 = (s16[784,256]{1,0:T(8,128)(2,1)}, s16[784,256]{1,0:T(8,128)(2,1)}, u32[]{:S(2)}, u32[]{:S(2)}) collective-permute-start(s16[784,256]{1,0:T(8,128)(2,1)} %get-tuple-element.230), channel_id=1, source_target_pairs={{0,1},{1,0},{2,3},{3,2},{4,5},{5,4},{6,7},{7,6},{8,9},{9,8},{10,11... | collective-permute-start | bytes 1204232 | tf_op jit(solution)/shard_map/ppermute | solution.py:636
  402.1 77.6 %all-to-all-start.3 = ((s16[8,304,256]{2,1,0:T(8,128)(2,1)}), s16[8,304,256]{2,1,0:T(8,128)(2,1)S(1)}, u32[]{:S(2)}, u32[]{:S(2)}) async-start(s16[8,304,256]{2,1,0:T(8,128)(2,1)} %explicit.8), calls=%async_computation.3 | async-start | bytes 2490368 | tf_op jit(solution)/shard_map/all_to_all | solution.py:632
  423.2 22.8 %collective-permute-start.22 = (s16[304,256]{1,0:T(8,128)(2,1)}, s16[304,256]{1,0:T(8,128)(2,1)S(1)}, u32[]{:S(2)}, u32[]{:S(2)}) collective-permute-start(s16[304,256]{1,0:T(8,128)(2,1)} %get-tuple-element.237), channel_id=1, source_target_pairs={{0,4},{1,5},{2,6},{3,7},{4,0},{5,1},{6,2},{7,3},{8,12},{9,13},{10,... | collective-permute-start | bytes 466952 | tf_op jit(solution)/shard_map/ppermute | solution.py:636
  425.4 30.4 %collective-permute-start.23 = (s16[304,256]{1,0:T(8,128)(2,1)}, s16[304,256]{1,0:T(8,128)(2,1)S(1)}, u32[]{:S(2)}, u32[]{:S(2)}) collective-permute-start(s16[304,256]{1,0:T(8,128)(2,1)} %get-tuple-element.238), channel_id=1, source_target_pairs={{0,5},{1,4},{2,7},{3,6},{4,1},{5,0},{6,3},{7,2},{8,13},{9,12},{10,... | collective-permute-start | bytes 466952 | tf_op jit(solution)/shard_map/ppermute | solution.py:636
  426.0 37.9 %collective-permute-start.24 = (s16[304,256]{1,0:T(8,128)(2,1)}, s16[304,256]{1,0:T(8,128)(2,1)S(1)}, u32[]{:S(2)}, u32[]{:S(2)}) collective-permute-start(s16[304,256]{1,0:T(8,128)(2,1)} %get-tuple-element.239), channel_id=1, source_target_pairs={{0,6},{1,7},{2,4},{3,5},{4,2},{5,3},{6,0},{7,1},{8,14},{9,15},{10,... | collective-permute-start | bytes 466952 | tf_op jit(solution)/shard_map/ppermute | solution.py:636
  428.5 47.3 %collective-permute-start.28 = (s16[576,256]{1,0:T(8,128)(2,1)}, s16[576,256]{1,0:T(8,128)(2,1)S(1)}, u32[]{:S(2)}, u32[]{:S(2)}) collective-permute-start(s16[576,256]{1,0:T(8,128)(2,1)} %get-tuple-element.247), channel_id=1, source_target_pairs={{0,2},{1,3},{2,0},{3,1},{4,6},{5,7},{6,4},{7,5},{8,10},{9,11},{10,... | collective-permute-start | bytes 884744 | tf_op jit(solution)/shard_map/ppermute | solution.py:636
  430.2 49.1 %collective-permute-start.29 = (s16[576,256]{1,0:T(8,128)(2,1)}, s16[576,256]{1,0:T(8,128)(2,1)S(1)}, u32[]{:S(2)}, u32[]{:S(2)}) collective-permute-start(s16[576,256]{1,0:T(8,128)(2,1)} %get-tuple-element.248), channel_id=1, source_target_pairs={{0,4},{1,5},{2,6},{3,7},{4,0},{5,1},{6,2},{7,3},{8,12},{9,13},{10,... | collective-permute-start | bytes 884744 | tf_op jit(solution)/shard_map/ppermute | solution.py:636
  446.0 27.8 %collective-permute-start.25 = (s16[304,256]{1,0:T(8,128)(2,1)}, s16[304,256]{1,0:T(8,128)(2,1)S(1)}, u32[]{:S(2)}, u32[]{:S(2)}) collective-permute-start(s16[304,256]{1,0:T(8,128)(2,1)} %get-tuple-element.240), channel_id=1, source_target_pairs={{0,7},{1,6},{2,5},{3,4},{4,3},{5,2},{6,1},{7,0},{8,15},{9,14},{10,... | collective-permute-start | bytes 466952 | tf_op jit(solution)/shard_map/ppermute | solution.py:636
  455.8 18.1 %collective-permute-start.26 = (s16[304,256]{1,0:T(8,128)(2,1)}, s16[304,256]{1,0:T(8,128)(2,1)S(1)}, u32[]{:S(2)}, u32[]{:S(2)}) collective-permute-start(s16[304,256]{1,0:T(8,128)(2,1)} %get-tuple-element.241), channel_id=1, source_target_pairs={{0,3},{1,2},{2,1},{3,0},{4,7},{5,6},{6,5},{7,4},{8,11},{9,10},{10,... | collective-permute-start | bytes 466952 | tf_op jit(solution)/shard_map/ppermute | solution.py:636
  473.9 25.8 %collective-permute-start.30 = (s16[576,256]{1,0:T(8,128)(2,1)}, s16[576,256]{1,0:T(8,128)(2,1)S(1)}, u32[]{:S(2)}, u32[]{:S(2)}) collective-permute-start(s16[576,256]{1,0:T(8,128)(2,1)} %get-tuple-element.249), channel_id=1, source_target_pairs={{0,5},{1,4},{2,7},{3,6},{4,1},{5,0},{6,3},{7,2},{8,13},{9,12},{10,... | collective-permute-start | bytes 884744 | tf_op jit(solution)/shard_map/ppermute | solution.py:636
  473.9 33.1 %collective-permute-start.31 = (s16[576,256]{1,0:T(8,128)(2,1)}, s16[576,256]{1,0:T(8,128)(2,1)}, u32[]{:S(2)}, u32[]{:S(2)}) collective-permute-start(s16[576,256]{1,0:T(8,128)(2,1)} %get-tuple-element.250), channel_id=1, source_target_pairs={{0,6},{1,7},{2,4},{3,5},{4,2},{5,3},{6,0},{7,1},{8,14},{9,15},{10,... | collective-permute-start | bytes 884744 | tf_op jit(solution)/shard_map/ppermute | solution.py:636
  474.3 39.1 %collective-permute-start.32 = (s16[576,256]{1,0:T(8,128)(2,1)}, s16[576,256]{1,0:T(8,128)(2,1)}, u32[]{:S(2)}, u32[]{:S(2)}) collective-permute-start(s16[576,256]{1,0:T(8,128)(2,1)} %get-tuple-element.251), channel_id=1, source_target_pairs={{0,7},{1,6},{2,5},{3,4},{4,3},{5,2},{6,1},{7,0},{8,15},{9,14},{10,... | collective-permute-start | bytes 884744 | tf_op jit(solution)/shard_map/ppermute | solution.py:636
  475.8 37.7 %collective-permute-start.33 = (s16[576,256]{1,0:T(8,128)(2,1)}, s16[576,256]{1,0:T(8,128)(2,1)}, u32[]{:S(2)}, u32[]{:S(2)}) collective-permute-start(s16[576,256]{1,0:T(8,128)(2,1)} %get-tuple-element.252), channel_id=1, source_target_pairs={{0,3},{1,2},{2,1},{3,0},{4,7},{5,6},{6,5},{7,4},{8,11},{9,10},{10,... | collective-permute-start | bytes 884744 | tf_op jit(solution)/shard_map/ppermute | solution.py:636
  479.3 34.2 %collective-permute-start.34 = (s16[576,256]{1,0:T(8,128)(2,1)}, s16[576,256]{1,0:T(8,128)(2,1)}, u32[]{:S(2)}, u32[]{:S(2)}) collective-permute-start(s16[576,256]{1,0:T(8,128)(2,1)} %get-tuple-element.253), channel_id=1, source_target_pairs={{0,1},{1,0},{2,3},{3,2},{4,5},{5,4},{6,7},{7,6},{8,9},{9,8},{10,11... | collective-permute-start | bytes 884744 | tf_op jit(solution)/shard_map/ppermute | solution.py:636
  513.5 112.0 %all-to-all-start.4 = ((s16[8,400,256]{2,1,0:T(8,128)(2,1)}), s16[8,400,256]{2,1,0:T(8,128)(2,1)S(1)}, u32[]{:S(2)}, u32[]{:S(2)}) async-start(s16[8,400,256]{2,1,0:T(8,128)(2,1)} %get-tuple-element.254), calls=%async_computation.4 | async-start | bytes 3276800 | tf_op jit(solution)/shard_map/all_to_all | solution.py:632
  540.4 55.9 %collective-permute-start.36 = (s16[784,256]{1,0:T(8,128)(2,1)}, s16[784,256]{1,0:T(8,128)(2,1)S(1)}, u32[]{:S(2)}, u32[]{:S(2)}) collective-permute-start(s16[784,256]{1,0:T(8,128)(2,1)} %get-tuple-element.267), channel_id=1, source_target_pairs={{0,4},{1,5},{2,6},{3,7},{4,0},{5,1},{6,2},{7,3},{8,12},{9,13},{10,... | collective-permute-start | bytes 1204232 | tf_op jit(solution)/shard_map/ppermute | solution.py:636
  542.7 62.2 %collective-permute-start.37 = (s16[784,256]{1,0:T(8,128)(2,1)}, s16[784,256]{1,0:T(8,128)(2,1)S(1)}, u32[]{:S(2)}, u32[]{:S(2)}) collective-permute-start(s16[784,256]{1,0:T(8,128)(2,1)} %get-tuple-element.268), channel_id=1, source_target_pairs={{0,5},{1,4},{2,7},{3,6},{4,1},{5,0},{6,3},{7,2},{8,13},{9,12},{10,... | collective-permute-start | bytes 1204232 | tf_op jit(solution)/shard_map/ppermute | solution.py:636
  543.3 71.8 %collective-permute-start.38 = (s16[784,256]{1,0:T(8,128)(2,1)}, s16[784,256]{1,0:T(8,128)(2,1)S(1)}, u32[]{:S(2)}, u32[]{:S(2)}) collective-permute-start(s16[784,256]{1,0:T(8,128)(2,1)} %get-tuple-element.269), channel_id=1, source_target_pairs={{0,6},{1,7},{2,4},{3,5},{4,2},{5,3},{6,0},{7,1},{8,14},{9,15},{10,... | collective-permute-start | bytes 1204232 | tf_op jit(solution)/shard_map/ppermute | solution.py:636
  545.9 78.0 %collective-permute-start.39 = (s16[784,256]{1,0:T(8,128)(2,1)}, s16[784,256]{1,0:T(8,128)(2,1)S(1)}, u32[]{:S(2)}, u32[]{:S(2)}) collective-permute-start(s16[784,256]{1,0:T(8,128)(2,1)} %get-tuple-element.270), channel_id=1, source_target_pairs={{0,7},{1,6},{2,5},{3,4},{4,3},{5,2},{6,1},{7,0},{8,15},{9,14},{10,... | collective-permute-start | bytes 1204232 | tf_op jit(solution)/shard_map/ppermute | solution.py:636
  557.1 66.9 %collective-permute-start.40 = (s16[784,256]{1,0:T(8,128)(2,1)}, s16[784,256]{1,0:T(8,128)(2,1)S(1)}, u32[]{:S(2)}, u32[]{:S(2)}) collective-permute-start(s16[784,256]{1,0:T(8,128)(2,1)} %get-tuple-element.271), channel_id=1, source_target_pairs={{0,3},{1,2},{2,1},{3,0},{4,7},{5,6},{6,5},{7,4},{8,11},{9,10},{10,... | collective-permute-start | bytes 1204232 | tf_op jit(solution)/shard_map/ppermute | solution.py:636
  596.4 29.1 %collective-permute-start.41 = (s16[784,256]{1,0:T(8,128)(2,1)}, s16[784,256]{1,0:T(8,128)(2,1)}, u32[]{:S(2)}, u32[]{:S(2)}) collective-permute-start(s16[784,256]{1,0:T(8,128)(2,1)} %get-tuple-element.272), channel_id=1, source_target_pairs={{0,1},{1,0},{2,3},{3,2},{4,5},{5,4},{6,7},{7,6},{8,9},{9,8},{10,11... | collective-permute-start | bytes 1204232 | tf_op jit(solution)/shard_map/ppermute | solution.py:636
  634.7 77.6 %all-to-all-start.5 = ((s16[8,304,256]{2,1,0:T(8,128)(2,1)}), s16[8,304,256]{2,1,0:T(8,128)(2,1)S(1)}, u32[]{:S(2)}, u32[]{:S(2)}) async-start(s16[8,304,256]{2,1,0:T(8,128)(2,1)} %explicit.10), calls=%async_computation.5 | async-start | bytes 2490368 | tf_op jit(solution)/shard_map/all_to_all | solution.py:632
  655.7 22.9 %collective-permute-start.43 = (s16[304,256]{1,0:T(8,128)(2,1)}, s16[304,256]{1,0:T(8,128)(2,1)S(1)}, u32[]{:S(2)}, u32[]{:S(2)}) collective-permute-start(s16[304,256]{1,0:T(8,128)(2,1)} %get-tuple-element.275), channel_id=1, source_target_pairs={{0,4},{1,5},{2,6},{3,7},{4,0},{5,1},{6,2},{7,3},{8,12},{9,13},{10,... | collective-permute-start | bytes 466952 | tf_op jit(solution)/shard_map/ppermute | solution.py:636
  657.9 30.5 %collective-permute-start.44 = (s16[304,256]{1,0:T(8,128)(2,1)}, s16[304,256]{1,0:T(8,128)(2,1)S(1)}, u32[]{:S(2)}, u32[]{:S(2)}) collective-permute-start(s16[304,256]{1,0:T(8,128)(2,1)} %get-tuple-element.276), channel_id=1, source_target_pairs={{0,5},{1,4},{2,7},{3,6},{4,1},{5,0},{6,3},{7,2},{8,13},{9,12},{10,... | collective-permute-start | bytes 466952 | tf_op jit(solution)/shard_map/ppermute | solution.py:636
  658.5 38.1 %collective-permute-start.45 = (s16[304,256]{1,0:T(8,128)(2,1)}, s16[304,256]{1,0:T(8,128)(2,1)S(1)}, u32[]{:S(2)}, u32[]{:S(2)}) collective-permute-start(s16[304,256]{1,0:T(8,128)(2,1)} %get-tuple-element.277), channel_id=1, source_target_pairs={{0,6},{1,7},{2,4},{3,5},{4,2},{5,3},{6,0},{7,1},{8,14},{9,15},{10,... | collective-permute-start | bytes 466952 | tf_op jit(solution)/shard_map/ppermute | solution.py:636
  661.0 47.4 %collective-permute-start.49 = (s16[576,256]{1,0:T(8,128)(2,1)}, s16[576,256]{1,0:T(8,128)(2,1)S(1)}, u32[]{:S(2)}, u32[]{:S(2)}) collective-permute-start(s16[576,256]{1,0:T(8,128)(2,1)} %get-tuple-element.283), channel_id=1, source_target_pairs={{0,2},{1,3},{2,0},{3,1},{4,6},{5,7},{6,4},{7,5},{8,10},{9,11},{10,... | collective-permute-start | bytes 884744 | tf_op jit(solution)/shard_map/ppermute | solution.py:636
  662.8 49.1 %collective-permute-start.50 = (s16[576,256]{1,0:T(8,128)(2,1)}, s16[576,256]{1,0:T(8,128)(2,1)S(1)}, u32[]{:S(2)}, u32[]{:S(2)}) collective-permute-start(s16[576,256]{1,0:T(8,128)(2,1)} %get-tuple-element.284), channel_id=1, source_target_pairs={{0,4},{1,5},{2,6},{3,7},{4,0},{5,1},{6,2},{7,3},{8,12},{9,13},{10,... | collective-permute-start | bytes 884744 | tf_op jit(solution)/shard_map/ppermute | solution.py:636
  678.6 27.8 %collective-permute-start.46 = (s16[304,256]{1,0:T(8,128)(2,1)}, s16[304,256]{1,0:T(8,128)(2,1)S(1)}, u32[]{:S(2)}, u32[]{:S(2)}) collective-permute-start(s16[304,256]{1,0:T(8,128)(2,1)} %get-tuple-element.278), channel_id=1, source_target_pairs={{0,7},{1,6},{2,5},{3,4},{4,3},{5,2},{6,1},{7,0},{8,15},{9,14},{10,... | collective-permute-start | bytes 466952 | tf_op jit(solution)/shard_map/ppermute | solution.py:636
  688.4 18.1 %collective-permute-start.47 = (s16[304,256]{1,0:T(8,128)(2,1)}, s16[304,256]{1,0:T(8,128)(2,1)S(1)}, u32[]{:S(2)}, u32[]{:S(2)}) collective-permute-start(s16[304,256]{1,0:T(8,128)(2,1)} %get-tuple-element.279), channel_id=1, source_target_pairs={{0,3},{1,2},{2,1},{3,0},{4,7},{5,6},{6,5},{7,4},{8,11},{9,10},{10,... | collective-permute-start | bytes 466952 | tf_op jit(solution)/shard_map/ppermute | solution.py:636
  706.5 25.8 %collective-permute-start.51 = (s16[576,256]{1,0:T(8,128)(2,1)}, s16[576,256]{1,0:T(8,128)(2,1)S(1)}, u32[]{:S(2)}, u32[]{:S(2)}) collective-permute-start(s16[576,256]{1,0:T(8,128)(2,1)} %get-tuple-element.285), channel_id=1, source_target_pairs={{0,5},{1,4},{2,7},{3,6},{4,1},{5,0},{6,3},{7,2},{8,13},{9,12},{10,... | collective-permute-start | bytes 884744 | tf_op jit(solution)/shard_map/ppermute | solution.py:636
  706.5 33.0 %collective-permute-start.52 = (s16[576,256]{1,0:T(8,128)(2,1)}, s16[576,256]{1,0:T(8,128)(2,1)}, u32[]{:S(2)}, u32[]{:S(2)}) collective-permute-start(s16[576,256]{1,0:T(8,128)(2,1)} %get-tuple-element.286), channel_id=1, source_target_pairs={{0,6},{1,7},{2,4},{3,5},{4,2},{5,3},{6,0},{7,1},{8,14},{9,15},{10,... | collective-permute-start | bytes 884744 | tf_op jit(solution)/shard_map/ppermute | solution.py:636
  706.9 39.1 %collective-permute-start.53 = (s16[576,256]{1,0:T(8,128)(2,1)}, s16[576,256]{1,0:T(8,128)(2,1)}, u32[]{:S(2)}, u32[]{:S(2)}) collective-permute-start(s16[576,256]{1,0:T(8,128)(2,1)} %get-tuple-element.287), channel_id=1, source_target_pairs={{0,7},{1,6},{2,5},{3,4},{4,3},{5,2},{6,1},{7,0},{8,15},{9,14},{10,... | collective-permute-start | bytes 884744 | tf_op jit(solution)/shard_map/ppermute | solution.py:636
  708.4 37.7 %collective-permute-start.54 = (s16[576,256]{1,0:T(8,128)(2,1)}, s16[576,256]{1,0:T(8,128)(2,1)}, u32[]{:S(2)}, u32[]{:S(2)}) collective-permute-start(s16[576,256]{1,0:T(8,128)(2,1)} %get-tuple-element.288), channel_id=1, source_target_pairs={{0,3},{1,2},{2,1},{3,0},{4,7},{5,6},{6,5},{7,4},{8,11},{9,10},{10,... | collective-permute-start | bytes 884744 | tf_op jit(solution)/shard_map/ppermute | solution.py:636
  711.9 34.2 %collective-permute-start.55 = (s16[576,256]{1,0:T(8,128)(2,1)}, s16[576,256]{1,0:T(8,128)(2,1)}, u32[]{:S(2)}, u32[]{:S(2)}) collective-permute-start(s16[576,256]{1,0:T(8,128)(2,1)} %get-tuple-element.289), channel_id=1, source_target_pairs={{0,1},{1,0},{2,3},{3,2},{4,5},{5,4},{6,7},{7,6},{8,9},{9,8},{10,11... | collective-permute-start | bytes 884744 | tf_op jit(solution)/shard_map/ppermute | solution.py:636
  746.1 84.6 %all-to-all-start.6 = ((s16[8,400,256]{2,1,0:T(8,128)(2,1)}), s16[8,400,256]{2,1,0:T(8,128)(2,1)S(1)}, u32[]{:S(2)}, u32[]{:S(2)}) async-start(s16[8,400,256]{2,1,0:T(8,128)(2,1)} %advance_lines.10), calls=%async_computation.6 | async-start | bytes 3276800 | tf_op jit(solution)/shard_map/all_to_all | solution.py:632
  767.0 19.6 %collective-permute-start.56 = (s16[784,256]{1,0:T(8,128)(2,1)}, s16[784,256]{1,0:T(8,128)(2,1)S(1)}, u32[]{:S(2)}, u32[]{:S(2)}) collective-permute-start(s16[784,256]{1,0:T(8,128)(2,1)} %get-tuple-element.300), channel_id=1, source_target_pairs={{0,2},{1,3},{2,0},{3,1},{4,6},{5,7},{6,4},{7,5},{8,10},{9,11},{10,... | collective-permute-start | bytes 1204232 | tf_op jit(solution)/shard_map/ppermute | solution.py:636
  767.1 61.8 %collective-permute-start.57 = (s16[784,256]{1,0:T(8,128)(2,1)}, s16[784,256]{1,0:T(8,128)(2,1)S(1)}, u32[]{:S(2)}, u32[]{:S(2)}) collective-permute-start(s16[784,256]{1,0:T(8,128)(2,1)} %get-tuple-element.301), channel_id=1, source_target_pairs={{0,4},{1,5},{2,6},{3,7},{4,0},{5,1},{6,2},{7,3},{8,12},{9,13},{10,... | collective-permute-start | bytes 1204232 | tf_op jit(solution)/shard_map/ppermute | solution.py:636
  769.4 68.6 %collective-permute-start.58 = (s16[784,256]{1,0:T(8,128)(2,1)}, s16[784,256]{1,0:T(8,128)(2,1)S(1)}, u32[]{:S(2)}, u32[]{:S(2)}) collective-permute-start(s16[784,256]{1,0:T(8,128)(2,1)} %get-tuple-element.302), channel_id=1, source_target_pairs={{0,5},{1,4},{2,7},{3,6},{4,1},{5,0},{6,3},{7,2},{8,13},{9,12},{10,... | collective-permute-start | bytes 1204232 | tf_op jit(solution)/shard_map/ppermute | solution.py:636
  770.0 77.7 %collective-permute-start.59 = (s16[784,256]{1,0:T(8,128)(2,1)}, s16[784,256]{1,0:T(8,128)(2,1)S(1)}, u32[]{:S(2)}, u32[]{:S(2)}) collective-permute-start(s16[784,256]{1,0:T(8,128)(2,1)} %get-tuple-element.303), channel_id=1, source_target_pairs={{0,6},{1,7},{2,4},{3,5},{4,2},{5,3},{6,0},{7,1},{8,14},{9,15},{10,... | collective-permute-start | bytes 1204232 | tf_op jit(solution)/shard_map/ppermute | solution.py:636
  772.6 84.1 %collective-permute-start.60 = (s16[784,256]{1,0:T(8,128)(2,1)}, s16[784,256]{1,0:T(8,128)(2,1)}, u32[]{:S(2)}, u32[]{:S(2)}) collective-permute-start(s16[784,256]{1,0:T(8,128)(2,1)} %get-tuple-element.304), channel_id=1, source_target_pairs={{0,7},{1,6},{2,5},{3,4},{4,3},{5,2},{6,1},{7,0},{8,15},{9,14},{10,... | collective-permute-start | bytes 1204232 | tf_op jit(solution)/shard_map/ppermute | solution.py:636
  786.6 70.0 %collective-permute-start.61 = (s16[784,256]{1,0:T(8,128)(2,1)}, s16[784,256]{1,0:T(8,128)(2,1)}, u32[]{:S(2)}, u32[]{:S(2)}) collective-permute-start(s16[784,256]{1,0:T(8,128)(2,1)} %get-tuple-element.305), channel_id=1, source_target_pairs={{0,3},{1,2},{2,1},{3,0},{4,7},{5,6},{6,5},{7,4},{8,11},{9,10},{10,... | collective-permute-start | bytes 1204232 | tf_op jit(solution)/shard_map/ppermute | solution.py:636
  828.9 27.7 %collective-permute-start.62 = (s16[784,256]{1,0:T(8,128)(2,1)}, s16[784,256]{1,0:T(8,128)(2,1)}, u32[]{:S(2)}, u32[]{:S(2)}) collective-permute-start(s16[784,256]{1,0:T(8,128)(2,1)} %get-tuple-element.306), channel_id=1, source_target_pairs={{0,1},{1,0},{2,3},{3,2},{4,5},{5,4},{6,7},{7,6},{8,9},{9,8},{10,11... | collective-permute-start | bytes 1204232 | tf_op jit(solution)/shard_map/ppermute | solution.py:636
  (68 other events, 1473.0 us)
Sparse Core Ops, SparseCore 0:
  18.4 334.1 all-gather.2

commit v5 on v4

--- a/solution.py
+++ b/solution.py
@@ -108,21 +108,24 @@
 
 
 def pack_kernel(plan, tangent_ref, flow_ref, out_ref, codes):
-    row = pl.program_id(0)
-    for d in range(plan.parts):
-        along, across = plan.piece(d)
-        values = [tangent_ref[c, 0, along, across] for c in range(3)]
-        values.append(flow_ref[0, 0, along, across].astype(F32))
-        for first, group in ((0, values[:3]), (3, values[3:])):
-            code = scale_code(column_max(group))
-            factor = encode(code)
-            for k, value in enumerate(group):
-                start = pl.multiple_of(((first + k) * plan.rows + row) * plan.width, plan.width)
-                out_ref[d, pl.ds(start, plan.width), :] = to_short(value * factor)
-            base = 0 if first == 0 else plan.scale_rows
-            codes[d, pl.ds(base + row, 1), :] = code
-
-    @pl.when(row == plan.rows - 1)
+    step, size = pl.program_id(0), tangent_ref.shape[1]
+    for j in range(size):
+        row = step * size + j
+        for d in range(plan.parts):
+            along, across = plan.piece(d)
+            values = [tangent_ref[c, j, along, across] for c in range(3)]
+            values.append(flow_ref[0, j, along, across].astype(F32))
+            for first, group in ((0, values[:3]), (3, values[3:])):
+                code = scale_code(column_max(group))
+                factor = encode(code)
+                for k, value in enumerate(group):
+                    start = ((first + k) * plan.rows + row) * plan.width
+                    here = pl.ds(pl.multiple_of(start, plan.width), plan.width)
+                    out_ref[d, here, :] = to_short(value * factor)
+                base = 0 if first == 0 else plan.scale_rows
+                codes[d, pl.ds(base + row, 1), :] = code
+
+    @pl.when(step == pl.num_programs(0) - 1)
     def _():
         for d in range(plan.parts):
             out_ref[d, plan.rows_of(4) :, :] = codes[d].astype(jnp.int32).astype(jnp.int16)
@@ -130,12 +133,13 @@
 
 def pack_start(plan, tangent, flow):
     shape = (plan.parts, plan.rows_of(4) + 2 * plan.scale_rows, plan.depth)
+    size = 4 if plan.rows % 4 == 0 else 1
     return pl.pallas_call(
         functools.partial(pack_kernel, plan),
-        grid=(plan.rows,),
+        grid=(plan.rows // size,),
         in_specs=[
-            pl.BlockSpec((3, 1, plan.nx, plan.nz), lambda j: (0, j, 0, 0)),
-            pl.BlockSpec((1, 1, plan.nx, plan.nz), lambda j: (1, j, 0, 0)),
+            pl.BlockSpec((3, size, plan.nx, plan.nz), lambda j: (0, j, 0, 0)),
+            pl.BlockSpec((1, size, plan.nx, plan.nz), lambda j: (1, j, 0, 0)),
         ],
         out_specs=pl.BlockSpec(shape, lambda j: (0, 0, 0)),
         scratch_shapes=[pltpu.VMEM((plan.parts, 2 * plan.scale_rows, plan.depth), F32)],
@@ -587,7 +591,7 @@
 
 def result(plan, group, whole, me, shift, successor, blocks, tangents, before):
     height = plan.rows_of(len(group)) + 16
-    rows = next(r for r in (4, 3, 2, 1) if plan.rows % r == 0)
+    rows = next(r for r in (6, 4, 3, 2, 1) if plan.rows % r == 0)
     specs = block_specs(
         plan, whole, height, plan.depth, lambda c: 0, pipeline_mode=pl.Buffered(1)
     )

time: 875 us -> 870 us (level)
  transfers between devices with their start and end apart: 71 -> 71, of which waited for: 38 -> 39; matrix products, arithmetic and copies ran while one was open for 0% -> 0% of each run, Pallas kernels for 24% -> 24%
where the time goes in v5:
time: 870 us; the launch traced here: 869 us
  waiting for transfers between devices  495 us (57%)
  Pallas kernels  224 us (26%)
  starting transfers between devices  125 us (14%)
  between operations  14.6 us (2%)
  local copies, waits for them, and re-layouts  10.3 us (1%)
    ppermute x63, waiting for transfers between devices, exchange(): moved[d] = lax.ppermute(blocks[d], 'grid', route)  386 us
    all_to_all x7, waiting for transfers between devices, exchange(): lax.all_to_all(blocks[0], 'grid', split_axis=0, concat_axis=0, tiled=True)  109 us
    pallas_call x6, Pallas kernels, advance_lines(): pl.pallas_call(functools.partial(lines_kernel, plan, section, group, whol...  100 us
    ppermute x63, starting transfers between devices, exchange(): moved[d] = lax.ppermute(blocks[d], 'grid', route)  90.7 us
    pallas_call x6, Pallas kernels, explicit(): pl.pallas_call(functools.partial(explicit_kernel, plan, late, received),...  80.1 us
    all_to_all x7, starting transfers between devices, exchange(): lax.all_to_all(blocks[0], 'grid', split_axis=0, concat_axis=0, tiled=True)  34.3 us
    pallas_call x1, Pallas kernels, first_lines(): pl.pallas_call(functools.partial(first_lines_kernel, plan), grid=(3,), in...  21.5 us
  transfers between devices with their start and end apart: 71, of which 39 were waited for; matrix products, arithmetic and copies ran while one was open for 0% of the time, Pallas kernels for 24%

profile of v5, /device:TPU:9, one launch (start us, length us, event | category | flops | bytes accessed | tf_op | source)
XLA Modules:
  0.0 869.1 jit_solution(13465748115645595058)
XLA Ops:
  6.5 8.6 pack_start.1
  15.2 5.7 all-to-all-start.1
  20.8 8.7 explicit.6
  29.5 20.3 %explicit.7 = (s16[304,256]{1,0:T(8,128)(2,1)}, s16[304,256]{1,0:T(8,128)(2,1)}, s16[304,256]{1,0:T(8,128)(2,1)}, s16[304,256]{1,0:T(8,128)(2,1)}, s16[304,256]{...) custom-call(s32[1]{0:T(128)} %bitcast.me_ref, ...), custom_call_target="tpu_custom_call" | custom-call | flops 8999999488 | bytes 36000000 | tf_op jit(solution)/shard_map/explicit/pallas_call | solution.py:314
  49.8 109.2 %all-to-all-done.1.refs_0_.refs_1_.refs_2_.refs_3_ = s16[8,1568,256]{2,1,0:T(8,128)(2,1)} async-done(((s16[8,1568,256]{2,1,0:T(8,128)(2,1)}), s16[8,1568,256]{2,1,0:T(8,128)(2,1)}, u32[]{:S(2)}, u32[]{:S(2)}) %all-to-all-start.1) | async-done | bytes 6422560 | tf_op jit(solution)/shard_map/all_to_all | solution.py:636
  159.0 7.1 all-to-all-start
  166.2 21.5 %first_lines.1 = (f32[3,32,96,256]{3,2,1,0:T(8,128)}, f32[3,32,96,256]{3,2,1,0:T(8,128)}, f32[32,96,256]{2,1,0:T(8,128)}) custom-call(s16[8,1568,256]{2,1,0:T(8,128)(2,1)} %all-to-all-done.1.refs_0_.refs_1_.refs_2_.refs_3_, s16[8,1568,256]{2,1,0:T(8,128)(2,1)} %all-to-all-done.1.refs_0_.refs_1_.refs_2_.refs_3_, ...), custom_call_target="tpu_custom_call" | custom-call | flops 1000000000 | bytes 30000000 | tf_op jit(solution)/shard_map/first_lines/pallas_call | solution.py:412
  197.5 21.8 %collective-permute-done.1.refs_3_.refs_12_ = s16[304,256]{1,0:T(8,128)(2,1)S(1)} collective-permute-done((s16[304,256]{1,0:T(8,128)(2,1)S(1)}, s16[304,256]{1,0:T(8,128)(2,1)S(1)}, u32[]{:S(2)}, u32[]{:S(2)}) %collective-permute-start.1) | collective-permute-done | bytes 155680 | tf_op jit(solution)/shard_map/ppermute | solution.py:640
  222.7 3.2 collective-permute-start.5
  225.9 5.3 collective-permute-done.3.refs_5_.refs_14_
  232.4 15.2 %collective-permute-done.4.refs_6_.refs_15_ = s16[304,256]{1,0:T(8,128)(2,1)S(1)} collective-permute-done((s16[304,256]{1,0:T(8,128)(2,1)S(1)}, s16[304,256]{1,0:T(8,128)(2,1)S(1)}, u32[]{:S(2)}, u32[]{:S(2)}) %collective-permute-start.4) | collective-permute-done | bytes 155680 | tf_op jit(solution)/shard_map/ppermute | solution.py:640
  249.5 2.9 collective-permute-start.9
  253.5 14.3 %advance_lines.6 = (s16[8,400,256]{2,1,0:T(8,128)(2,1)}, f32[1,32,96,256]{3,2,1,0:T(8,128)}, f32[1,32,96,256]{3,2,1,0:T(8,128)}) custom-call(s32[1]{0:T(128)} %bitcast.me_ref, s16[8,304,256]{2,1,0:T(8,128)(2,1)} %copy-done.2, s16[304,256]{1,0:T(8,128)(2,1)} %get-tuple-element.194.refs_1_.refs_10_, s16[304,256]{1,0:T(8,128)(2,1)} %copy-done.20, ...), custom_call_target="tpu_custom_call" | custom-call | flops 700000000 | bytes 17000000 | tf_op jit(solution)/shard_map/advance_lines/pallas_call | solution.py:543
  267.9 4.1 collective-permute-done.7.refs_2_
  272.0 3.6 collective-permute-done.9.refs_4_
  275.6 6.2 all-to-all-start.2
  281.8 22.4 %advance_lines.7 = (s16[784,256]{1,0:T(8,128)(2,1)}, s16[784,256]{1,0:T(8,128)(2,1)}, s16[784,256]{1,0:T(8,128)(2,1)}, s16[784,256]{1,0:T(8,128)(2,1)}, s16[784,...) custom-call(s32[1]{0:T(128)} %bitcast.me_ref, ...), custom_call_target="tpu_custom_call" | custom-call | flops 1400000000 | bytes 34000000 | tf_op jit(solution)/shard_map/advance_lines/pallas_call | solution.py:543
  309.9 11.6 %collective-permute-done.14.refs_2_ = s16[784,256]{1,0:T(8,128)(2,1)S(1)} collective-permute-done((s16[784,256]{1,0:T(8,128)(2,1)}, s16[784,256]{1,0:T(8,128)(2,1)S(1)}, u32[]{:S(2)}, u32[]{:S(2)}) %collective-permute-start.14) | collective-permute-done | bytes 401440 | tf_op jit(solution)/shard_map/ppermute | solution.py:640
  324.0 36.6 %collective-permute-done.15.refs_3_ = s16[784,256]{1,0:T(8,128)(2,1)S(1)} collective-permute-done((s16[784,256]{1,0:T(8,128)(2,1)}, s16[784,256]{1,0:T(8,128)(2,1)S(1)}, u32[]{:S(2)}, u32[]{:S(2)}) %collective-permute-start.15) | collective-permute-done | bytes 401440 | tf_op jit(solution)/shard_map/ppermute | solution.py:640
  361.4 7.8 collective-permute-done.16.refs_4_
  369.2 10.2 %collective-permute-done.17.refs_5_ = s16[784,256]{1,0:T(8,128)(2,1)S(1)} collective-permute-done((s16[784,256]{1,0:T(8,128)(2,1)}, s16[784,256]{1,0:T(8,128)(2,1)S(1)}, u32[]{:S(2)}, u32[]{:S(2)}) %collective-permute-start.17) | collective-permute-done | bytes 401440 | tf_op jit(solution)/shard_map/ppermute | solution.py:640
  379.4 8.8 %collective-permute-done.18.refs_6_ = s16[784,256]{1,0:T(8,128)(2,1)S(1)} collective-permute-done((s16[784,256]{1,0:T(8,128)(2,1)}, s16[784,256]{1,0:T(8,128)(2,1)S(1)}, u32[]{:S(2)}, u32[]{:S(2)}) %collective-permute-start.18) | collective-permute-done | bytes 401440 | tf_op jit(solution)/shard_map/ppermute | solution.py:640
  390.8 8.1 explicit.8
  398.9 3.5 all-to-all-start.3
  402.5 17.5 %explicit.9 = (s16[304,256]{1,0:T(8,128)(2,1)}, s16[304,256]{1,0:T(8,128)(2,1)}, s16[304,256]{1,0:T(8,128)(2,1)}, s16[304,256]{1,0:T(8,128)(2,1)}, s16[304,256]{...) custom-call(s32[1]{0:T(128)} %bitcast.me_ref, ...), custom_call_target="tpu_custom_call" | custom-call | flops 8999999488 | bytes 36000000 | tf_op jit(solution)/shard_map/explicit/pallas_call | solution.py:314
  428.8 14.1 %collective-permute-done.22.refs_3_.refs_12_ = s16[304,256]{1,0:T(8,128)(2,1)S(1)} collective-permute-done((s16[304,256]{1,0:T(8,128)(2,1)}, s16[304,256]{1,0:T(8,128)(2,1)S(1)}, u32[]{:S(2)}, u32[]{:S(2)}) %collective-permute-start.22) | collective-permute-done | bytes 155680 | tf_op jit(solution)/shard_map/ppermute | solution.py:640
  445.1 7.6 collective-permute-done.23.refs_4_.refs_13_
  452.6 6.3 collective-permute-start.26
  462.2 8.5 collective-permute-done.25.refs_6_.refs_15_
  472.7 3.5 collective-permute-start.33
  477.7 14.3 %advance_lines.8 = (s16[8,400,256]{2,1,0:T(8,128)(2,1)}, f32[1,32,96,256]{3,2,1,0:T(8,128)}, f32[1,32,96,256]{3,2,1,0:T(8,128)}) custom-call(s32[1]{0:T(128)} %bitcast.me_ref, s16[8,304,256]{2,1,0:T(8,128)(2,1)} %copy-done, s16[304,256]{1,0:T(8,128)(2,1)} %get-tuple-element.235.refs_1_.refs_10_, s16[304,256]{1,0:T(8,128)(2,1)} %copy-done.6, ...), custom_call_target="tpu_custom_call" | custom-call | flops 700000000 | bytes 17000000 | tf_op jit(solution)/shard_map/advance_lines/pallas_call | solution.py:543
  491.9 4.7 collective-permute-done.30.refs_4_
  496.6 7.2 collective-permute-done.31.refs_5_
  503.8 6.5 collective-permute-done.32.refs_6_
  510.4 4.1 all-to-all-start.4
  514.5 22.7 %advance_lines.9 = (s16[784,256]{1,0:T(8,128)(2,1)}, s16[784,256]{1,0:T(8,128)(2,1)}, s16[784,256]{1,0:T(8,128)(2,1)}, s16[784,256]{1,0:T(8,128)(2,1)}, s16[784,...) custom-call(s32[1]{0:T(128)} %bitcast.me_ref, ...), custom_call_target="tpu_custom_call" | custom-call | flops 1400000000 | bytes 34000000 | tf_op jit(solution)/shard_map/advance_lines/pallas_call | solution.py:543
  540.2 2.6 collective-permute-start.38
  542.8 11.2 %collective-permute-done.35.refs_2_ = s16[784,256]{1,0:T(8,128)(2,1)S(1)} collective-permute-done((s16[784,256]{1,0:T(8,128)(2,1)}, s16[784,256]{1,0:T(8,128)(2,1)S(1)}, u32[]{:S(2)}, u32[]{:S(2)}) %collective-permute-start.35) | collective-permute-done | bytes 401440 | tf_op jit(solution)/shard_map/ppermute | solution.py:640
  554.0 2.6 collective-permute-start.40
  556.6 36.7 %collective-permute-done.36.refs_3_ = s16[784,256]{1,0:T(8,128)(2,1)S(1)} collective-permute-done((s16[784,256]{1,0:T(8,128)(2,1)}, s16[784,256]{1,0:T(8,128)(2,1)S(1)}, u32[]{:S(2)}, u32[]{:S(2)}) %collective-permute-start.36) | collective-permute-done | bytes 401440 | tf_op jit(solution)/shard_map/ppermute | solution.py:640
  593.7 8.1 collective-permute-done.37.refs_4_
  601.8 10.2 %collective-permute-done.38.refs_5_ = s16[784,256]{1,0:T(8,128)(2,1)S(1)} collective-permute-done((s16[784,256]{1,0:T(8,128)(2,1)}, s16[784,256]{1,0:T(8,128)(2,1)S(1)}, u32[]{:S(2)}, u32[]{:S(2)}) %collective-permute-start.38) | collective-permute-done | bytes 401440 | tf_op jit(solution)/shard_map/ppermute | solution.py:640
  612.0 8.8 %collective-permute-done.39.refs_6_ = s16[784,256]{1,0:T(8,128)(2,1)S(1)} collective-permute-done((s16[784,256]{1,0:T(8,128)(2,1)}, s16[784,256]{1,0:T(8,128)(2,1)S(1)}, u32[]{:S(2)}, u32[]{:S(2)}) %collective-permute-start.39) | collective-permute-done | bytes 401440 | tf_op jit(solution)/shard_map/ppermute | solution.py:640
  623.5 8.1 explicit.10
  631.6 3.5 all-to-all-start.5
  635.1 17.4 %explicit.11 = (s16[304,256]{1,0:T(8,128)(2,1)}, s16[304,256]{1,0:T(8,128)(2,1)}, s16[304,256]{1,0:T(8,128)(2,1)}, s16[304,256]{1,0:T(8,128)(2,1)}, s16[304,256]...) custom-call(s32[1]{0:T(128)} %bitcast.me_ref, ...), custom_call_target="tpu_custom_call" | custom-call | flops 8999999488 | bytes 36000000 | tf_op jit(solution)/shard_map/explicit/pallas_call | solution.py:314
  661.2 14.3 %collective-permute-done.43.refs_3_.refs_12_ = s16[304,256]{1,0:T(8,128)(2,1)S(1)} collective-permute-done((s16[304,256]{1,0:T(8,128)(2,1)}, s16[304,256]{1,0:T(8,128)(2,1)S(1)}, u32[]{:S(2)}, u32[]{:S(2)}) %collective-permute-start.43) | collective-permute-done | bytes 155680 | tf_op jit(solution)/shard_map/ppermute | solution.py:640
  677.7 7.6 collective-permute-done.44.refs_4_.refs_13_
  685.3 6.3 collective-permute-start.47
  694.8 8.5 collective-permute-done.46.refs_6_.refs_15_
  705.3 3.5 collective-permute-start.54
  710.2 9.9 %advance_lines.10 = s16[8,400,256]{2,1,0:T(8,128)(2,1)} custom-call(s32[1]{0:T(128)} %bitcast.me_ref, s16[8,304,256]{2,1,0:T(8,128)(2,1)} %copy-done.1, s16[304,256]{1,0:T(8,128)(2,1)} %get-tuple-element.273.refs_1_.refs_10_, s16[304,256]{1,0:T(8,128)(2,1)} %copy-done.10, s16[304,256]{1,0:T(8,128)(2,1)} %copy-done.11, s16[304,256]{1,0:T(8,128)(2,1)} %copy-done.12, ...), custom_call_target="tpu_custom_call" | custom-call | flops 700000000 | bytes 17000000 | tf_op jit(solution)/shard_map/advance_lines/pallas_call | solution.py:543
  720.1 9.1 %collective-permute-done.51.refs_4_ = s16[576,256]{1,0:T(8,128)(2,1)S(1)} collective-permute-done((s16[576,256]{1,0:T(8,128)(2,1)}, s16[576,256]{1,0:T(8,128)(2,1)S(1)}, u32[]{:S(2)}, u32[]{:S(2)}) %collective-permute-start.51) | collective-permute-done | bytes 294944 | tf_op jit(solution)/shard_map/ppermute | solution.py:640
  729.2 7.2 collective-permute-done.52.refs_5_
  736.4 6.5 collective-permute-done.53.refs_6_
  743.0 4.1 all-to-all-start.6
  747.1 16.7 %advance_lines.11 = (s16[784,256]{1,0:T(8,128)(2,1)}, s16[784,256]{1,0:T(8,128)(2,1)}, s16[784,256]{1,0:T(8,128)(2,1)}, s16[784,256]{1,0:T(8,128)(2,1)}, s16[784...) custom-call(s32[1]{0:T(128)} %bitcast.me_ref, ...), custom_call_target="tpu_custom_call" | custom-call | flops 1400000000 | bytes 34000000 | tf_op jit(solution)/shard_map/advance_lines/pallas_call | solution.py:543
  766.9 2.6 collective-permute-start.59
  769.4 14.0 %collective-permute-done.56.refs_1_ = s16[784,256]{1,0:T(8,128)(2,1)S(1)} collective-permute-done((s16[784,256]{1,0:T(8,128)(2,1)}, s16[784,256]{1,0:T(8,128)(2,1)S(1)}, u32[]{:S(2)}, u32[]{:S(2)}) %collective-permute-start.56) | collective-permute-done | bytes 401440 | tf_op jit(solution)/shard_map/ppermute | solution.py:640
  783.5 42.3 %collective-permute-done.57.refs_2_ = s16[784,256]{1,0:T(8,128)(2,1)S(1)} collective-permute-done((s16[784,256]{1,0:T(8,128)(2,1)}, s16[784,256]{1,0:T(8,128)(2,1)S(1)}, u32[]{:S(2)}, u32[]{:S(2)}) %collective-permute-start.57) | collective-permute-done | bytes 401440 | tf_op jit(solution)/shard_map/ppermute | solution.py:640
  828.7 4.7 result.2.refs_9_
  834.4 10.2 %collective-permute-done.59.refs_4_ = s16[784,256]{1,0:T(8,128)(2,1)S(1)} collective-permute-done((s16[784,256]{1,0:T(8,128)(2,1)}, s16[784,256]{1,0:T(8,128)(2,1)S(1)}, u32[]{:S(2)}, u32[]{:S(2)}) %collective-permute-start.59) | collective-permute-done | bytes 401440 | tf_op jit(solution)/shard_map/ppermute | solution.py:640
  844.6 8.9 %collective-permute-done.60.refs_5_ = s16[784,256]{1,0:T(8,128)(2,1)} collective-permute-done((s16[784,256]{1,0:T(8,128)(2,1)}, s16[784,256]{1,0:T(8,128)(2,1)}, u32[]{:S(2)}, u32[]{:S(2)}) %collective-permute-start.60) | collective-permute-done | bytes 401440 | tf_op jit(solution)/shard_map/ppermute | solution.py:640
  853.5 8.7 %result.3 = f32[3,12,256,256]{3,2,1,0:T(8,128)} custom-call(s32[1]{0:T(128)} %bitcast.me_ref, s32[1]{0:T(128)S(6)} %copy.12.shift_ref, s32[1]{0:T(128)} %dynamic_slice.3.successor_ref, s16[784,256]{1,0:T(8,128)(2,1)} %get-tuple-element.299.refs_0_, s16[784,256]{1,0:T(8,128)(2,1)} %copy-done.27, ...), custom_call_target="tpu_custom_call", output_to_operand_aliasing={{}: (12, {})} | custom-call | bytes 16000000 | tf_op jit(solution)/shard_map/result/pallas_call | solution.py:610
  (218 shorter events, 76.4 us)
Async XLA Ops:
  6.5 821.0 %all-gather.3.cloned.1.call-start = ((), (), s32[]{:S(2)}) async-start(), calls=%async_computation.7 | async-start | bytes 47185920 | tf_op jit(solution)/shard_map/all_gather | solution.py:657
  15.2 143.9 %all-to-all-start.1 = ((s16[8,1568,256]{2,1,0:T(8,128)(2,1)}), s16[8,1568,256]{2,1,0:T(8,128)(2,1)}, u32[]{:S(2)}, u32[]{:S(2)}) async-start(s16[8,1568,256]{2,1,0:T(8,128)(2,1)} %pack_start.1), calls=%async_computation.1 | async-start | bytes 12845056 | tf_op jit(solution)/shard_map/all_to_all | solution.py:636
  159.0 93.4 %all-to-all-start = ((s16[8,304,256]{2,1,0:T(8,128)(2,1)}), s16[8,304,256]{2,1,0:T(8,128)(2,1)S(1)}, u32[]{:S(2)}, u32[]{:S(2)}) async-start(s16[8,304,256]{2,1,0:T(8,128)(2,1)} %get-tuple-element.175), calls=%async_computation | async-start | bytes 2490368 | tf_op jit(solution)/shard_map/all_to_all | solution.py:636
  187.9 31.4 %collective-permute-start.1 = (s16[304,256]{1,0:T(8,128)(2,1)S(1)}, s16[304,256]{1,0:T(8,128)(2,1)S(1)}, u32[]{:S(2)}, u32[]{:S(2)}) collective-permute-start(s16[304,256]{1,0:T(8,128)(2,1)S(1)} %copy-done.58), channel_id=1, source_target_pairs={{0,4},{1,5},{2,6},{3,7},{4,0},{5,1},{6,2},{7,3},{8,12},{9,13},{10,... | collective-permute-start | bytes 466952 | tf_op jit(solution)/shard_map/ppermute | solution.py:640
  190.2 32.5 %collective-permute-start.2 = (s16[304,256]{1,0:T(8,128)(2,1)S(1)}, s16[304,256]{1,0:T(8,128)(2,1)S(1)}, u32[]{:S(2)}, u32[]{:S(2)}) collective-permute-start(s16[304,256]{1,0:T(8,128)(2,1)S(1)} %copy-done.57), channel_id=1, source_target_pairs={{0,5},{1,4},{2,7},{3,6},{4,1},{5,0},{6,3},{7,2},{8,13},{9,12},{10,... | collective-permute-start | bytes 466952 | tf_op jit(solution)/shard_map/ppermute | solution.py:640
  190.9 40.3 %collective-permute-start.3 = (s16[304,256]{1,0:T(8,128)(2,1)S(1)}, s16[304,256]{1,0:T(8,128)(2,1)S(1)}, u32[]{:S(2)}, u32[]{:S(2)}) collective-permute-start(s16[304,256]{1,0:T(8,128)(2,1)S(1)} %copy-done.56), channel_id=1, source_target_pairs={{0,6},{1,7},{2,4},{3,5},{4,2},{5,3},{6,0},{7,1},{8,14},{9,15},{10,... | collective-permute-start | bytes 466952 | tf_op jit(solution)/shard_map/ppermute | solution.py:640
  193.4 56.1 %collective-permute-start.10 = (s16[576,256]{1,0:T(8,128)(2,1)}, s16[576,256]{1,0:T(8,128)(2,1)S(1)}, u32[]{:S(2)}, u32[]{:S(2)}) collective-permute-start(s16[576,256]{1,0:T(8,128)(2,1)} %get-tuple-element.210), channel_id=1, source_target_pairs={{0,6},{1,7},{2,4},{3,5},{4,2},{5,3},{6,0},{7,1},{8,14},{9,15},{10,... | collective-permute-start | bytes 884744 | tf_op jit(solution)/shard_map/ppermute | solution.py:640
  195.2 54.3 %collective-permute-start.11 = (s16[576,256]{1,0:T(8,128)(2,1)S(1)}, s16[576,256]{1,0:T(8,128)(2,1)S(1)}, u32[]{:S(2)}, u32[]{:S(2)}) collective-permute-start(s16[576,256]{1,0:T(8,128)(2,1)S(1)} %copy-done.52), channel_id=1, source_target_pairs={{0,7},{1,6},{2,5},{3,4},{4,3},{5,2},{6,1},{7,0},{8,15},{9,14},{10,... | collective-permute-start | bytes 884744 | tf_op jit(solution)/shard_map/ppermute | solution.py:640
  219.3 28.3 %collective-permute-start.4 = (s16[304,256]{1,0:T(8,128)(2,1)S(1)}, s16[304,256]{1,0:T(8,128)(2,1)S(1)}, u32[]{:S(2)}, u32[]{:S(2)}) collective-permute-start(s16[304,256]{1,0:T(8,128)(2,1)S(1)} %copy-done.55), channel_id=1, source_target_pairs={{0,7},{1,6},{2,5},{3,4},{4,3},{5,2},{6,1},{7,0},{8,15},{9,14},{10,... | collective-permute-start | bytes 466952 | tf_op jit(solution)/shard_map/ppermute | solution.py:640
  222.7 24.9 %collective-permute-start.5 = (s16[304,256]{1,0:T(8,128)(2,1)S(1)}, s16[304,256]{1,0:T(8,128)(2,1)S(1)}, u32[]{:S(2)}, u32[]{:S(2)}) collective-permute-start(s16[304,256]{1,0:T(8,128)(2,1)S(1)} %copy-done.54), channel_id=1, source_target_pairs={{0,3},{1,2},{2,1},{3,0},{4,7},{5,6},{6,5},{7,4},{8,11},{9,10},{10,... | collective-permute-start | bytes 466952 | tf_op jit(solution)/shard_map/ppermute | solution.py:640
  247.6 20.2 %collective-permute-start.12 = (s16[576,256]{1,0:T(8,128)(2,1)}, s16[576,256]{1,0:T(8,128)(2,1)S(1)}, u32[]{:S(2)}, u32[]{:S(2)}) collective-permute-start(s16[576,256]{1,0:T(8,128)(2,1)} %get-tuple-element.212), channel_id=1, source_target_pairs={{0,3},{1,2},{2,1},{3,0},{4,7},{5,6},{6,5},{7,4},{8,11},{9,10},{10,... | collective-permute-start | bytes 884744 | tf_op jit(solution)/shard_map/ppermute | solution.py:640
  247.6 20.2 %collective-permute-start.13 = (s16[576,256]{1,0:T(8,128)(2,1)}, s16[576,256]{1,0:T(8,128)(2,1)}, u32[]{:S(2)}, u32[]{:S(2)}) collective-permute-start(s16[576,256]{1,0:T(8,128)(2,1)} %get-tuple-element.213), channel_id=1, source_target_pairs={{0,1},{1,0},{2,3},{3,2},{4,5},{5,4},{6,7},{7,6},{8,9},{9,8},{10,11... | collective-permute-start | bytes 884744 | tf_op jit(solution)/shard_map/ppermute | solution.py:640
  247.7 24.3 %collective-permute-start.7 = (s16[576,256]{1,0:T(8,128)(2,1)}, s16[576,256]{1,0:T(8,128)(2,1)}, u32[]{:S(2)}, u32[]{:S(2)}) collective-permute-start(s16[576,256]{1,0:T(8,128)(2,1)} %get-tuple-element.207), channel_id=1, source_target_pairs={{0,2},{1,3},{2,0},{3,1},{4,6},{5,7},{6,4},{7,5},{8,10},{9,11},{10,... | collective-permute-start | bytes 884744 | tf_op jit(solution)/shard_map/ppermute | solution.py:640
  249.5 22.5 %collective-permute-start.8 = (s16[576,256]{1,0:T(8,128)(2,1)}, s16[576,256]{1,0:T(8,128)(2,1)}, u32[]{:S(2)}, u32[]{:S(2)}) collective-permute-start(s16[576,256]{1,0:T(8,128)(2,1)} %get-tuple-element.208), channel_id=1, source_target_pairs={{0,4},{1,5},{2,6},{3,7},{4,0},{5,1},{6,2},{7,3},{8,12},{9,13},{10,... | collective-permute-start | bytes 884744 | tf_op jit(solution)/shard_map/ppermute | solution.py:640
  249.5 26.1 %collective-permute-start.9 = (s16[576,256]{1,0:T(8,128)(2,1)}, s16[576,256]{1,0:T(8,128)(2,1)}, u32[]{:S(2)}, u32[]{:S(2)}) collective-permute-start(s16[576,256]{1,0:T(8,128)(2,1)} %get-tuple-element.209), channel_id=1, source_target_pairs={{0,5},{1,4},{2,7},{3,6},{4,1},{5,0},{6,3},{7,2},{8,13},{9,12},{10,... | collective-permute-start | bytes 884744 | tf_op jit(solution)/shard_map/ppermute | solution.py:640
  275.6 114.0 %all-to-all-start.2 = ((s16[8,400,256]{2,1,0:T(8,128)(2,1)}), s16[8,400,256]{2,1,0:T(8,128)(2,1)S(1)}, u32[]{:S(2)}, u32[]{:S(2)}) async-start(s16[8,400,256]{2,1,0:T(8,128)(2,1)} %get-tuple-element.214), calls=%async_computation.2 | async-start | bytes 3276800 | tf_op jit(solution)/shard_map/all_to_all | solution.py:636
  304.2 17.2 %collective-permute-start.14 = (s16[784,256]{1,0:T(8,128)(2,1)}, s16[784,256]{1,0:T(8,128)(2,1)S(1)}, u32[]{:S(2)}, u32[]{:S(2)}) collective-permute-start(s16[784,256]{1,0:T(8,128)(2,1)} %get-tuple-element.224), channel_id=1, source_target_pairs={{0,2},{1,3},{2,0},{3,1},{4,6},{5,7},{6,4},{7,5},{8,10},{9,11},{10,... | collective-permute-start | bytes 1204232 | tf_op jit(solution)/shard_map/ppermute | solution.py:640
  304.9 55.7 %collective-permute-start.15 = (s16[784,256]{1,0:T(8,128)(2,1)}, s16[784,256]{1,0:T(8,128)(2,1)S(1)}, u32[]{:S(2)}, u32[]{:S(2)}) collective-permute-start(s16[784,256]{1,0:T(8,128)(2,1)} %get-tuple-element.225), channel_id=1, source_target_pairs={{0,4},{1,5},{2,6},{3,7},{4,0},{5,1},{6,2},{7,3},{8,12},{9,13},{10,... | collective-permute-start | bytes 1204232 | tf_op jit(solution)/shard_map/ppermute | solution.py:640
  306.7 62.5 %collective-permute-start.16 = (s16[784,256]{1,0:T(8,128)(2,1)}, s16[784,256]{1,0:T(8,128)(2,1)S(1)}, u32[]{:S(2)}, u32[]{:S(2)}) collective-permute-start(s16[784,256]{1,0:T(8,128)(2,1)} %get-tuple-element.226), channel_id=1, source_target_pairs={{0,5},{1,4},{2,7},{3,6},{4,1},{5,0},{6,3},{7,2},{8,13},{9,12},{10,... | collective-permute-start | bytes 1204232 | tf_op jit(solution)/shard_map/ppermute | solution.py:640
  307.6 71.8 %collective-permute-start.17 = (s16[784,256]{1,0:T(8,128)(2,1)}, s16[784,256]{1,0:T(8,128)(2,1)S(1)}, u32[]{:S(2)}, u32[]{:S(2)}) collective-permute-start(s16[784,256]{1,0:T(8,128)(2,1)} %get-tuple-element.227), channel_id=1, source_target_pairs={{0,6},{1,7},{2,4},{3,5},{4,2},{5,3},{6,0},{7,1},{8,14},{9,15},{10,... | collective-permute-start | bytes 1204232 | tf_op jit(solution)/shard_map/ppermute | solution.py:640
  309.9 78.3 %collective-permute-start.18 = (s16[784,256]{1,0:T(8,128)(2,1)}, s16[784,256]{1,0:T(8,128)(2,1)S(1)}, u32[]{:S(2)}, u32[]{:S(2)}) collective-permute-start(s16[784,256]{1,0:T(8,128)(2,1)} %get-tuple-element.228), channel_id=1, source_target_pairs={{0,7},{1,6},{2,5},{3,4},{4,3},{5,2},{6,1},{7,0},{8,15},{9,14},{10,... | collective-permute-start | bytes 1204232 | tf_op jit(solution)/shard_map/ppermute | solution.py:640
  321.5 66.7 %collective-permute-start.19 = (s16[784,256]{1,0:T(8,128)(2,1)}, s16[784,256]{1,0:T(8,128)(2,1)S(1)}, u32[]{:S(2)}, u32[]{:S(2)}) collective-permute-start(s16[784,256]{1,0:T(8,128)(2,1)} %get-tuple-element.229), channel_id=1, source_target_pairs={{0,3},{1,2},{2,1},{3,0},{4,7},{5,6},{6,5},{7,4},{8,11},{9,10},{10,... | collective-permute-start | bytes 1204232 | tf_op jit(solution)/shard_map/ppermute | solution.py:640
  360.6 29.1 %collective-permute-start.20 = (s16[784,256]{1,0:T(8,128)(2,1)}, s16[784,256]{1,0:T(8,128)(2,1)}, u32[]{:S(2)}, u32[]{:S(2)}) collective-permute-start(s16[784,256]{1,0:T(8,128)(2,1)} %get-tuple-element.230), channel_id=1, source_target_pairs={{0,1},{1,0},{2,3},{3,2},{4,5},{5,4},{6,7},{7,6},{8,9},{9,8},{10,11... | collective-permute-start | bytes 1204232 | tf_op jit(solution)/shard_map/ppermute | solution.py:640
  398.9 77.6 %all-to-all-start.3 = ((s16[8,304,256]{2,1,0:T(8,128)(2,1)}), s16[8,304,256]{2,1,0:T(8,128)(2,1)S(1)}, u32[]{:S(2)}, u32[]{:S(2)}) async-start(s16[8,304,256]{2,1,0:T(8,128)(2,1)} %explicit.8), calls=%async_computation.3 | async-start | bytes 2490368 | tf_op jit(solution)/shard_map/all_to_all | solution.py:636
  420.1 22.8 %collective-permute-start.22 = (s16[304,256]{1,0:T(8,128)(2,1)}, s16[304,256]{1,0:T(8,128)(2,1)S(1)}, u32[]{:S(2)}, u32[]{:S(2)}) collective-permute-start(s16[304,256]{1,0:T(8,128)(2,1)} %get-tuple-element.237), channel_id=1, source_target_pairs={{0,4},{1,5},{2,6},{3,7},{4,0},{5,1},{6,2},{7,3},{8,12},{9,13},{10,... | collective-permute-start | bytes 466952 | tf_op jit(solution)/shard_map/ppermute | solution.py:640
  422.2 30.4 %collective-permute-start.23 = (s16[304,256]{1,0:T(8,128)(2,1)}, s16[304,256]{1,0:T(8,128)(2,1)S(1)}, u32[]{:S(2)}, u32[]{:S(2)}) collective-permute-start(s16[304,256]{1,0:T(8,128)(2,1)} %get-tuple-element.238), channel_id=1, source_target_pairs={{0,5},{1,4},{2,7},{3,6},{4,1},{5,0},{6,3},{7,2},{8,13},{9,12},{10,... | collective-permute-start | bytes 466952 | tf_op jit(solution)/shard_map/ppermute | solution.py:640
  422.9 38.0 %collective-permute-start.24 = (s16[304,256]{1,0:T(8,128)(2,1)}, s16[304,256]{1,0:T(8,128)(2,1)S(1)}, u32[]{:S(2)}, u32[]{:S(2)}) collective-permute-start(s16[304,256]{1,0:T(8,128)(2,1)} %get-tuple-element.239), channel_id=1, source_target_pairs={{0,6},{1,7},{2,4},{3,5},{4,2},{5,3},{6,0},{7,1},{8,14},{9,15},{10,... | collective-permute-start | bytes 466952 | tf_op jit(solution)/shard_map/ppermute | solution.py:640
  425.4 47.3 %collective-permute-start.28 = (s16[576,256]{1,0:T(8,128)(2,1)}, s16[576,256]{1,0:T(8,128)(2,1)S(1)}, u32[]{:S(2)}, u32[]{:S(2)}) collective-permute-start(s16[576,256]{1,0:T(8,128)(2,1)} %get-tuple-element.247), channel_id=1, source_target_pairs={{0,2},{1,3},{2,0},{3,1},{4,6},{5,7},{6,4},{7,5},{8,10},{9,11},{10,... | collective-permute-start | bytes 884744 | tf_op jit(solution)/shard_map/ppermute | solution.py:640
  427.1 49.1 %collective-permute-start.29 = (s16[576,256]{1,0:T(8,128)(2,1)}, s16[576,256]{1,0:T(8,128)(2,1)S(1)}, u32[]{:S(2)}, u32[]{:S(2)}) collective-permute-start(s16[576,256]{1,0:T(8,128)(2,1)} %get-tuple-element.248), channel_id=1, source_target_pairs={{0,4},{1,5},{2,6},{3,7},{4,0},{5,1},{6,2},{7,3},{8,12},{9,13},{10,... | collective-permute-start | bytes 884744 | tf_op jit(solution)/shard_map/ppermute | solution.py:640
  442.9 27.8 %collective-permute-start.25 = (s16[304,256]{1,0:T(8,128)(2,1)}, s16[304,256]{1,0:T(8,128)(2,1)S(1)}, u32[]{:S(2)}, u32[]{:S(2)}) collective-permute-start(s16[304,256]{1,0:T(8,128)(2,1)} %get-tuple-element.240), channel_id=1, source_target_pairs={{0,7},{1,6},{2,5},{3,4},{4,3},{5,2},{6,1},{7,0},{8,15},{9,14},{10,... | collective-permute-start | bytes 466952 | tf_op jit(solution)/shard_map/ppermute | solution.py:640
  452.6 18.1 %collective-permute-start.26 = (s16[304,256]{1,0:T(8,128)(2,1)}, s16[304,256]{1,0:T(8,128)(2,1)S(1)}, u32[]{:S(2)}, u32[]{:S(2)}) collective-permute-start(s16[304,256]{1,0:T(8,128)(2,1)} %get-tuple-element.241), channel_id=1, source_target_pairs={{0,3},{1,2},{2,1},{3,0},{4,7},{5,6},{6,5},{7,4},{8,11},{9,10},{10,... | collective-permute-start | bytes 466952 | tf_op jit(solution)/shard_map/ppermute | solution.py:640
  470.7 25.8 %collective-permute-start.30 = (s16[576,256]{1,0:T(8,128)(2,1)}, s16[576,256]{1,0:T(8,128)(2,1)S(1)}, u32[]{:S(2)}, u32[]{:S(2)}) collective-permute-start(s16[576,256]{1,0:T(8,128)(2,1)} %get-tuple-element.249), channel_id=1, source_target_pairs={{0,5},{1,4},{2,7},{3,6},{4,1},{5,0},{6,3},{7,2},{8,13},{9,12},{10,... | collective-permute-start | bytes 884744 | tf_op jit(solution)/shard_map/ppermute | solution.py:640
  470.8 33.0 %collective-permute-start.31 = (s16[576,256]{1,0:T(8,128)(2,1)}, s16[576,256]{1,0:T(8,128)(2,1)}, u32[]{:S(2)}, u32[]{:S(2)}) collective-permute-start(s16[576,256]{1,0:T(8,128)(2,1)} %get-tuple-element.250), channel_id=1, source_target_pairs={{0,6},{1,7},{2,4},{3,5},{4,2},{5,3},{6,0},{7,1},{8,14},{9,15},{10,... | collective-permute-start | bytes 884744 | tf_op jit(solution)/shard_map/ppermute | solution.py:640
  471.2 39.1 %collective-permute-start.32 = (s16[576,256]{1,0:T(8,128)(2,1)}, s16[576,256]{1,0:T(8,128)(2,1)}, u32[]{:S(2)}, u32[]{:S(2)}) collective-permute-start(s16[576,256]{1,0:T(8,128)(2,1)} %get-tuple-element.251), channel_id=1, source_target_pairs={{0,7},{1,6},{2,5},{3,4},{4,3},{5,2},{6,1},{7,0},{8,15},{9,14},{10,... | collective-permute-start | bytes 884744 | tf_op jit(solution)/shard_map/ppermute | solution.py:640
  472.7 37.7 %collective-permute-start.33 = (s16[576,256]{1,0:T(8,128)(2,1)}, s16[576,256]{1,0:T(8,128)(2,1)}, u32[]{:S(2)}, u32[]{:S(2)}) collective-permute-start(s16[576,256]{1,0:T(8,128)(2,1)} %get-tuple-element.252), channel_id=1, source_target_pairs={{0,3},{1,2},{2,1},{3,0},{4,7},{5,6},{6,5},{7,4},{8,11},{9,10},{10,... | collective-permute-start | bytes 884744 | tf_op jit(solution)/shard_map/ppermute | solution.py:640
  476.2 34.2 %collective-permute-start.34 = (s16[576,256]{1,0:T(8,128)(2,1)}, s16[576,256]{1,0:T(8,128)(2,1)}, u32[]{:S(2)}, u32[]{:S(2)}) collective-permute-start(s16[576,256]{1,0:T(8,128)(2,1)} %get-tuple-element.253), channel_id=1, source_target_pairs={{0,1},{1,0},{2,3},{3,2},{4,5},{5,4},{6,7},{7,6},{8,9},{9,8},{10,11... | collective-permute-start | bytes 884744 | tf_op jit(solution)/shard_map/ppermute | solution.py:640
  510.4 112.0 %all-to-all-start.4 = ((s16[8,400,256]{2,1,0:T(8,128)(2,1)}), s16[8,400,256]{2,1,0:T(8,128)(2,1)S(1)}, u32[]{:S(2)}, u32[]{:S(2)}) async-start(s16[8,400,256]{2,1,0:T(8,128)(2,1)} %get-tuple-element.254), calls=%async_computation.4 | async-start | bytes 3276800 | tf_op jit(solution)/shard_map/all_to_all | solution.py:636
  537.3 55.9 %collective-permute-start.36 = (s16[784,256]{1,0:T(8,128)(2,1)}, s16[784,256]{1,0:T(8,128)(2,1)S(1)}, u32[]{:S(2)}, u32[]{:S(2)}) collective-permute-start(s16[784,256]{1,0:T(8,128)(2,1)} %get-tuple-element.267), channel_id=1, source_target_pairs={{0,4},{1,5},{2,6},{3,7},{4,0},{5,1},{6,2},{7,3},{8,12},{9,13},{10,... | collective-permute-start | bytes 1204232 | tf_op jit(solution)/shard_map/ppermute | solution.py:640
  539.6 62.2 %collective-permute-start.37 = (s16[784,256]{1,0:T(8,128)(2,1)}, s16[784,256]{1,0:T(8,128)(2,1)S(1)}, u32[]{:S(2)}, u32[]{:S(2)}) collective-permute-start(s16[784,256]{1,0:T(8,128)(2,1)} %get-tuple-element.268), channel_id=1, source_target_pairs={{0,5},{1,4},{2,7},{3,6},{4,1},{5,0},{6,3},{7,2},{8,13},{9,12},{10,... | collective-permute-start | bytes 1204232 | tf_op jit(solution)/shard_map/ppermute | solution.py:640
  540.2 71.8 %collective-permute-start.38 = (s16[784,256]{1,0:T(8,128)(2,1)}, s16[784,256]{1,0:T(8,128)(2,1)S(1)}, u32[]{:S(2)}, u32[]{:S(2)}) collective-permute-start(s16[784,256]{1,0:T(8,128)(2,1)} %get-tuple-element.269), channel_id=1, source_target_pairs={{0,6},{1,7},{2,4},{3,5},{4,2},{5,3},{6,0},{7,1},{8,14},{9,15},{10,... | collective-permute-start | bytes 1204232 | tf_op jit(solution)/shard_map/ppermute | solution.py:640
  542.8 78.0 %collective-permute-start.39 = (s16[784,256]{1,0:T(8,128)(2,1)}, s16[784,256]{1,0:T(8,128)(2,1)S(1)}, u32[]{:S(2)}, u32[]{:S(2)}) collective-permute-start(s16[784,256]{1,0:T(8,128)(2,1)} %get-tuple-element.270), channel_id=1, source_target_pairs={{0,7},{1,6},{2,5},{3,4},{4,3},{5,2},{6,1},{7,0},{8,15},{9,14},{10,... | collective-permute-start | bytes 1204232 | tf_op jit(solution)/shard_map/ppermute | solution.py:640
  554.0 66.9 %collective-permute-start.40 = (s16[784,256]{1,0:T(8,128)(2,1)}, s16[784,256]{1,0:T(8,128)(2,1)S(1)}, u32[]{:S(2)}, u32[]{:S(2)}) collective-permute-start(s16[784,256]{1,0:T(8,128)(2,1)} %get-tuple-element.271), channel_id=1, source_target_pairs={{0,3},{1,2},{2,1},{3,0},{4,7},{5,6},{6,5},{7,4},{8,11},{9,10},{10,... | collective-permute-start | bytes 1204232 | tf_op jit(solution)/shard_map/ppermute | solution.py:640
  593.2 29.1 %collective-permute-start.41 = (s16[784,256]{1,0:T(8,128)(2,1)}, s16[784,256]{1,0:T(8,128)(2,1)}, u32[]{:S(2)}, u32[]{:S(2)}) collective-permute-start(s16[784,256]{1,0:T(8,128)(2,1)} %get-tuple-element.272), channel_id=1, source_target_pairs={{0,1},{1,0},{2,3},{3,2},{4,5},{5,4},{6,7},{7,6},{8,9},{9,8},{10,11... | collective-permute-start | bytes 1204232 | tf_op jit(solution)/shard_map/ppermute | solution.py:640
  631.6 77.6 %all-to-all-start.5 = ((s16[8,304,256]{2,1,0:T(8,128)(2,1)}), s16[8,304,256]{2,1,0:T(8,128)(2,1)S(1)}, u32[]{:S(2)}, u32[]{:S(2)}) async-start(s16[8,304,256]{2,1,0:T(8,128)(2,1)} %explicit.10), calls=%async_computation.5 | async-start | bytes 2490368 | tf_op jit(solution)/shard_map/all_to_all | solution.py:636
  652.6 22.9 %collective-permute-start.43 = (s16[304,256]{1,0:T(8,128)(2,1)}, s16[304,256]{1,0:T(8,128)(2,1)S(1)}, u32[]{:S(2)}, u32[]{:S(2)}) collective-permute-start(s16[304,256]{1,0:T(8,128)(2,1)} %get-tuple-element.275), channel_id=1, source_target_pairs={{0,4},{1,5},{2,6},{3,7},{4,0},{5,1},{6,2},{7,3},{8,12},{9,13},{10,... | collective-permute-start | bytes 466952 | tf_op jit(solution)/shard_map/ppermute | solution.py:640
  654.7 30.5 %collective-permute-start.44 = (s16[304,256]{1,0:T(8,128)(2,1)}, s16[304,256]{1,0:T(8,128)(2,1)S(1)}, u32[]{:S(2)}, u32[]{:S(2)}) collective-permute-start(s16[304,256]{1,0:T(8,128)(2,1)} %get-tuple-element.276), channel_id=1, source_target_pairs={{0,5},{1,4},{2,7},{3,6},{4,1},{5,0},{6,3},{7,2},{8,13},{9,12},{10,... | collective-permute-start | bytes 466952 | tf_op jit(solution)/shard_map/ppermute | solution.py:640
  655.4 38.1 %collective-permute-start.45 = (s16[304,256]{1,0:T(8,128)(2,1)}, s16[304,256]{1,0:T(8,128)(2,1)S(1)}, u32[]{:S(2)}, u32[]{:S(2)}) collective-permute-start(s16[304,256]{1,0:T(8,128)(2,1)} %get-tuple-element.277), channel_id=1, source_target_pairs={{0,6},{1,7},{2,4},{3,5},{4,2},{5,3},{6,0},{7,1},{8,14},{9,15},{10,... | collective-permute-start | bytes 466952 | tf_op jit(solution)/shard_map/ppermute | solution.py:640
  657.9 47.4 %collective-permute-start.49 = (s16[576,256]{1,0:T(8,128)(2,1)}, s16[576,256]{1,0:T(8,128)(2,1)S(1)}, u32[]{:S(2)}, u32[]{:S(2)}) collective-permute-start(s16[576,256]{1,0:T(8,128)(2,1)} %get-tuple-element.283), channel_id=1, source_target_pairs={{0,2},{1,3},{2,0},{3,1},{4,6},{5,7},{6,4},{7,5},{8,10},{9,11},{10,... | collective-permute-start | bytes 884744 | tf_op jit(solution)/shard_map/ppermute | solution.py:640
  659.7 49.1 %collective-permute-start.50 = (s16[576,256]{1,0:T(8,128)(2,1)}, s16[576,256]{1,0:T(8,128)(2,1)S(1)}, u32[]{:S(2)}, u32[]{:S(2)}) collective-permute-start(s16[576,256]{1,0:T(8,128)(2,1)} %get-tuple-element.284), channel_id=1, source_target_pairs={{0,4},{1,5},{2,6},{3,7},{4,0},{5,1},{6,2},{7,3},{8,12},{9,13},{10,... | collective-permute-start | bytes 884744 | tf_op jit(solution)/shard_map/ppermute | solution.py:640
  675.5 27.8 %collective-permute-start.46 = (s16[304,256]{1,0:T(8,128)(2,1)}, s16[304,256]{1,0:T(8,128)(2,1)S(1)}, u32[]{:S(2)}, u32[]{:S(2)}) collective-permute-start(s16[304,256]{1,0:T(8,128)(2,1)} %get-tuple-element.278), channel_id=1, source_target_pairs={{0,7},{1,6},{2,5},{3,4},{4,3},{5,2},{6,1},{7,0},{8,15},{9,14},{10,... | collective-permute-start | bytes 466952 | tf_op jit(solution)/shard_map/ppermute | solution.py:640
  685.3 18.1 %collective-permute-start.47 = (s16[304,256]{1,0:T(8,128)(2,1)}, s16[304,256]{1,0:T(8,128)(2,1)S(1)}, u32[]{:S(2)}, u32[]{:S(2)}) collective-permute-start(s16[304,256]{1,0:T(8,128)(2,1)} %get-tuple-element.279), channel_id=1, source_target_pairs={{0,3},{1,2},{2,1},{3,0},{4,7},{5,6},{6,5},{7,4},{8,11},{9,10},{10,... | collective-permute-start | bytes 466952 | tf_op jit(solution)/shard_map/ppermute | solution.py:640
  703.4 25.8 %collective-permute-start.51 = (s16[576,256]{1,0:T(8,128)(2,1)}, s16[576,256]{1,0:T(8,128)(2,1)S(1)}, u32[]{:S(2)}, u32[]{:S(2)}) collective-permute-start(s16[576,256]{1,0:T(8,128)(2,1)} %get-tuple-element.285), channel_id=1, source_target_pairs={{0,5},{1,4},{2,7},{3,6},{4,1},{5,0},{6,3},{7,2},{8,13},{9,12},{10,... | collective-permute-start | bytes 884744 | tf_op jit(solution)/shard_map/ppermute | solution.py:640
  703.4 33.1 %collective-permute-start.52 = (s16[576,256]{1,0:T(8,128)(2,1)}, s16[576,256]{1,0:T(8,128)(2,1)}, u32[]{:S(2)}, u32[]{:S(2)}) collective-permute-start(s16[576,256]{1,0:T(8,128)(2,1)} %get-tuple-element.286), channel_id=1, source_target_pairs={{0,6},{1,7},{2,4},{3,5},{4,2},{5,3},{6,0},{7,1},{8,14},{9,15},{10,... | collective-permute-start | bytes 884744 | tf_op jit(solution)/shard_map/ppermute | solution.py:640
  703.8 39.1 %collective-permute-start.53 = (s16[576,256]{1,0:T(8,128)(2,1)}, s16[576,256]{1,0:T(8,128)(2,1)}, u32[]{:S(2)}, u32[]{:S(2)}) collective-permute-start(s16[576,256]{1,0:T(8,128)(2,1)} %get-tuple-element.287), channel_id=1, source_target_pairs={{0,7},{1,6},{2,5},{3,4},{4,3},{5,2},{6,1},{7,0},{8,15},{9,14},{10,... | collective-permute-start | bytes 884744 | tf_op jit(solution)/shard_map/ppermute | solution.py:640
  705.3 37.7 %collective-permute-start.54 = (s16[576,256]{1,0:T(8,128)(2,1)}, s16[576,256]{1,0:T(8,128)(2,1)}, u32[]{:S(2)}, u32[]{:S(2)}) collective-permute-start(s16[576,256]{1,0:T(8,128)(2,1)} %get-tuple-element.288), channel_id=1, source_target_pairs={{0,3},{1,2},{2,1},{3,0},{4,7},{5,6},{6,5},{7,4},{8,11},{9,10},{10,... | collective-permute-start | bytes 884744 | tf_op jit(solution)/shard_map/ppermute | solution.py:640
  708.8 34.2 %collective-permute-start.55 = (s16[576,256]{1,0:T(8,128)(2,1)}, s16[576,256]{1,0:T(8,128)(2,1)}, u32[]{:S(2)}, u32[]{:S(2)}) collective-permute-start(s16[576,256]{1,0:T(8,128)(2,1)} %get-tuple-element.289), channel_id=1, source_target_pairs={{0,1},{1,0},{2,3},{3,2},{4,5},{5,4},{6,7},{7,6},{8,9},{9,8},{10,11... | collective-permute-start | bytes 884744 | tf_op jit(solution)/shard_map/ppermute | solution.py:640
  743.0 84.6 %all-to-all-start.6 = ((s16[8,400,256]{2,1,0:T(8,128)(2,1)}), s16[8,400,256]{2,1,0:T(8,128)(2,1)S(1)}, u32[]{:S(2)}, u32[]{:S(2)}) async-start(s16[8,400,256]{2,1,0:T(8,128)(2,1)} %advance_lines.10), calls=%async_computation.6 | async-start | bytes 3276800 | tf_op jit(solution)/shard_map/all_to_all | solution.py:636
  763.8 19.6 %collective-permute-start.56 = (s16[784,256]{1,0:T(8,128)(2,1)}, s16[784,256]{1,0:T(8,128)(2,1)S(1)}, u32[]{:S(2)}, u32[]{:S(2)}) collective-permute-start(s16[784,256]{1,0:T(8,128)(2,1)} %get-tuple-element.300), channel_id=1, source_target_pairs={{0,2},{1,3},{2,0},{3,1},{4,6},{5,7},{6,4},{7,5},{8,10},{9,11},{10,... | collective-permute-start | bytes 1204232 | tf_op jit(solution)/shard_map/ppermute | solution.py:640
  764.0 61.8 %collective-permute-start.57 = (s16[784,256]{1,0:T(8,128)(2,1)}, s16[784,256]{1,0:T(8,128)(2,1)S(1)}, u32[]{:S(2)}, u32[]{:S(2)}) collective-permute-start(s16[784,256]{1,0:T(8,128)(2,1)} %get-tuple-element.301), channel_id=1, source_target_pairs={{0,4},{1,5},{2,6},{3,7},{4,0},{5,1},{6,2},{7,3},{8,12},{9,13},{10,... | collective-permute-start | bytes 1204232 | tf_op jit(solution)/shard_map/ppermute | solution.py:640
  766.3 68.1 %collective-permute-start.58 = (s16[784,256]{1,0:T(8,128)(2,1)}, s16[784,256]{1,0:T(8,128)(2,1)S(1)}, u32[]{:S(2)}, u32[]{:S(2)}) collective-permute-start(s16[784,256]{1,0:T(8,128)(2,1)} %get-tuple-element.302), channel_id=1, source_target_pairs={{0,5},{1,4},{2,7},{3,6},{4,1},{5,0},{6,3},{7,2},{8,13},{9,12},{10,... | collective-permute-start | bytes 1204232 | tf_op jit(solution)/shard_map/ppermute | solution.py:640
  766.9 77.7 %collective-permute-start.59 = (s16[784,256]{1,0:T(8,128)(2,1)}, s16[784,256]{1,0:T(8,128)(2,1)S(1)}, u32[]{:S(2)}, u32[]{:S(2)}) collective-permute-start(s16[784,256]{1,0:T(8,128)(2,1)} %get-tuple-element.303), channel_id=1, source_target_pairs={{0,6},{1,7},{2,4},{3,5},{4,2},{5,3},{6,0},{7,1},{8,14},{9,15},{10,... | collective-permute-start | bytes 1204232 | tf_op jit(solution)/shard_map/ppermute | solution.py:640
  769.4 84.1 %collective-permute-start.60 = (s16[784,256]{1,0:T(8,128)(2,1)}, s16[784,256]{1,0:T(8,128)(2,1)}, u32[]{:S(2)}, u32[]{:S(2)}) collective-permute-start(s16[784,256]{1,0:T(8,128)(2,1)} %get-tuple-element.304), channel_id=1, source_target_pairs={{0,7},{1,6},{2,5},{3,4},{4,3},{5,2},{6,1},{7,0},{8,15},{9,14},{10,... | collective-permute-start | bytes 1204232 | tf_op jit(solution)/shard_map/ppermute | solution.py:640
  783.4 70.0 %collective-permute-start.61 = (s16[784,256]{1,0:T(8,128)(2,1)}, s16[784,256]{1,0:T(8,128)(2,1)}, u32[]{:S(2)}, u32[]{:S(2)}) collective-permute-start(s16[784,256]{1,0:T(8,128)(2,1)} %get-tuple-element.305), channel_id=1, source_target_pairs={{0,3},{1,2},{2,1},{3,0},{4,7},{5,6},{6,5},{7,4},{8,11},{9,10},{10,... | collective-permute-start | bytes 1204232 | tf_op jit(solution)/shard_map/ppermute | solution.py:640
  825.8 27.7 %collective-permute-start.62 = (s16[784,256]{1,0:T(8,128)(2,1)}, s16[784,256]{1,0:T(8,128)(2,1)}, u32[]{:S(2)}, u32[]{:S(2)}) collective-permute-start(s16[784,256]{1,0:T(8,128)(2,1)} %get-tuple-element.306), channel_id=1, source_target_pairs={{0,1},{1,0},{2,3},{3,2},{4,5},{5,4},{6,7},{7,6},{8,9},{9,8},{10,11... | collective-permute-start | bytes 1204232 | tf_op jit(solution)/shard_map/ppermute | solution.py:640
  (68 other events, 1470.7 us)
Sparse Core Ops, SparseCore 0:
  15.3 334.1 all-gather.2
